TPU v7x, 32 devices: a whole 2x2x4 slice. The times are simulated.
32 devices in a mesh: groups: 2 (over y), seq: 16 (over z, x, core).
Axes of the slice: x: 2, y: 2, z: 4, core: 2. Of those that a mesh axis runs over, the one named last changes fastest.
Arguments:
- query_src: bfloat16 [4096, 2048], P(('groups', 'seq')), parts along dimension 0, may hold values from -6 to 6
- key_src: bfloat16 [4096, 2048], P(('groups', 'seq')), parts along dimension 0, may hold values from -6 to 6
- value_src: bfloat16 [4096, 2048], P(('groups', 'seq')), parts along dimension 0, may hold values from -6 to 6
- up_query: bfloat16 [4096, 2048], P(('groups', 'seq')), parts along dimension 0, may hold values from -6 to 6
- query_gain: float32 [2048], replicated, may hold values from 1.2 to 2.4
- key_gain: float32 [2048], replicated, may hold values from 1.2 to 2.4
- up_gain: float32 [2048], replicated, may hold values from 1.5 to 5
Outputs:
- upsampled: bfloat16 [4096, 2048], P(('groups', 'seq')), parts along dimension 0
There are 2 independent parts, one for each index of `groups`. A program takes and returns all parts, laid end to end along the dimension named above; an argument that names none is the same for every part. Nothing has to cross between parts.
All inputs are finite; a program needn't handle non-finite values.
Results may differ from a plain program's by a relative error of at most 0.002.
The roundings to bfloat16 on the way count: a program that leaves them out, or rounds other values in their place, can miss the bound.
Values may be sent and summed in bfloat16 or wider, within the bound.
No kernel may reach another device: no remote copies, remote signals or barrier semaphores. Data moves between devices by JAX's collectives and lax.ppermute only.
A program may use at most 128 MiB of HBM per device.

v0:
```python
import math

import jax
import jax.numpy as jnp
from jax import lax
from jax.sharding import PartitionSpec as P

HEADS = 16
HDIM = 128
SHORT = 4
SHIFT = 3


epsilon = 1e-06


def shifted(value, axis, steps):
    count = lax.axis_size(axis)
    leading, last = (max(0, -steps), min(count, count - steps))
    return lax.ppermute(value, axis, [(source, source + steps) for source in range(leading, last)])


def head_norm(values, gain_vector):
    row_count = values.shape[0]
    by_head = values.reshape(row_count, HEADS, HDIM)
    inverse_rms = lax.rsqrt(jnp.mean(by_head * by_head, axis=2, keepdims=True) + epsilon)
    return (by_head * inverse_rms * gain_vector.reshape(1, HEADS, HDIM)).reshape(
        row_count, HEADS * HDIM
    )


def row_norm(values):
    return values * lax.rsqrt(jnp.mean(values * values, axis=-1, keepdims=True) + epsilon)


def pooled_rows(source, edge_rows):
    widened = jnp.concatenate([edge_rows, source[: source.shape[0] - SHIFT]], axis=0).astype(
        jnp.float32
    )
    return jnp.mean(widened.reshape(-1, SHORT, widened.shape[1]), axis=1)


def blocked_attention(queries, query_limit, key_rows, value_rows, key_positions, block_size):
    head_count, query_count, head_size = queries.shape
    block_total = key_rows.shape[1] // block_size
    ceiling = jnp.max(query_limit)

    def visit_block(block_index, totals):
        offset = block_index * block_size
        block_pos = lax.dynamic_slice_in_dim(key_positions, offset, block_size, 0)

        def compute(state):
            numer_in, denom_in = state
            key_block = lax.dynamic_slice_in_dim(key_rows, offset, block_size, 1)
            value_block = lax.dynamic_slice_in_dim(value_rows, offset, block_size, 1)
            scores = jnp.einsum(
                "hqd,hkd->hqk", queries, key_block, preferred_element_type=jnp.float32
            ) / math.sqrt(HDIM)
            visible = block_pos[None, :] <= query_limit[:, None]
            exponent = jnp.where(visible[None], jnp.exp(scores), 0.0)
            denom_out = denom_in + jnp.sum(exponent, axis=2)
            numer_out = numer_in + jnp.einsum(
                "hqk,hkd->hqd",
                exponent.astype(jnp.bfloat16),
                value_block,
                preferred_element_type=jnp.float32,
            )
            return (numer_out, denom_out)

        return lax.cond(jnp.min(block_pos) <= ceiling, compute, lambda state: state, totals)

    initial = (
        jnp.zeros((head_count, query_count, head_size), jnp.float32),
        jnp.zeros((head_count, query_count), jnp.float32),
    )
    numerator, denominator = lax.fori_loop(0, block_total, visit_block, initial)
    return numerator / denominator[:, :, None]


def spread_heads(matrices, row_count, block_count, device_count):
    count = len(matrices)
    joined = jnp.stack(matrices).reshape(count, row_count, HEADS, HDIM)
    joined = jnp.transpose(joined, (2, 0, 1, 3)).reshape(HEADS, 1, count * row_count, HDIM)
    return jnp.broadcast_to(joined, (HEADS, block_count, count * row_count, HDIM)).reshape(
        device_count, count * row_count, HDIM
    )


def split_pieces(matrix, row_count, block_count, device_count):
    piece = row_count // block_count
    parted = matrix.reshape(block_count, piece, HEADS, HDIM)
    return jnp.transpose(parted, (2, 0, 1, 3)).reshape(device_count, piece, HDIM)


def local(query_src, key_src, value_src, up_query, query_gain, key_gain, up_gain):
    device_count = lax.axis_size("seq")
    device_index = lax.axis_index("seq")
    block_count = device_count // HEADS
    block_index = device_index % block_count
    token_count = query_src.shape[0]
    edges = jnp.stack(
        [
            query_src[token_count - SHIFT :],
            key_src[token_count - SHIFT :],
            value_src[token_count - SHIFT :],
        ]
    )
    edges = shifted(edges, "seq", 1)
    short_query = head_norm(pooled_rows(query_src, edges[0]), query_gain).astype(jnp.bfloat16)
    short_key = head_norm(pooled_rows(key_src, edges[1]), key_gain).astype(jnp.bfloat16)
    short_value = pooled_rows(value_src, edges[2]).astype(jnp.bfloat16)
    row_count = short_query.shape[0]
    up_heads = head_norm(up_query.astype(jnp.float32), up_gain).astype(jnp.bfloat16)
    row_total = row_count * device_count
    key_block = math.gcd(512, row_total)
    row_positions = jnp.arange(row_total, dtype=jnp.int32)
    device_rows = jnp.arange(device_count, dtype=jnp.int32)[:, None]
    qkv_out = spread_heads(
        [short_query, short_key, short_value], row_count, block_count, device_count
    )
    up_out = split_pieces(up_heads, token_count, block_count, device_count)
    arrived, own_up = (
        lax.all_to_all(qkv_out, "seq", split_axis=0, concat_axis=0, tiled=True),
        lax.all_to_all(up_out, "seq", split_axis=0, concat_axis=0, tiled=True),
    )
    all_query = arrived[:, :row_count].reshape(row_total, HDIM)
    all_key = arrived[:, row_count : 2 * row_count].reshape(row_total, HDIM)
    all_value = arrived[:, 2 * row_count :].reshape(row_total, HDIM)

    def fill_block(index_now, memory_now):
        offset = index_now * key_block
        block_query = lax.dynamic_slice_in_dim(all_query, offset, key_block, 0)[None]
        limits = offset + jnp.arange(key_block, dtype=jnp.int32)
        attended = blocked_attention(
            block_query, limits, all_key[None], all_value[None], row_positions, key_block
        )[0]
        return lax.dynamic_update_slice_in_dim(
            memory_now, row_norm(attended).astype(jnp.bfloat16), offset, 0
        )

    memory = lax.fori_loop(
        0, row_total // key_block, fill_block, jnp.zeros((row_total, HDIM), jnp.bfloat16)
    )
    token_piece = token_count // block_count
    own_tokens = (
        device_rows * token_count
        + block_index * token_piece
        + jnp.arange(token_piece, dtype=jnp.int32)[None, :]
    ).reshape(-1)
    own_up = own_up.reshape(1, device_count * token_piece, HDIM)
    result = blocked_attention(
        own_up, own_tokens // SHORT, memory[None], memory[None], row_positions, key_block
    )[0]
    result = result.astype(jnp.bfloat16).reshape(device_count, token_piece, HDIM)
    returned = lax.all_to_all(result, "seq", split_axis=0, concat_axis=0, tiled=True)
    output_heads = returned.reshape(HEADS, token_count, HDIM)
    return jnp.transpose(output_heads, (1, 0, 2)).reshape(token_count, HEADS * HDIM)


def solution(mesh):
    in_specs = (
        P(("groups", "seq"), None),
        P(("groups", "seq"), None),
        P(("groups", "seq"), None),
        P(("groups", "seq"), None),
        P(),
        P(),
        P(),
    )
    out_specs = P(("groups", "seq"), None)
    return jax.shard_map(local, mesh=mesh, in_specs=in_specs, out_specs=out_specs, check_vma=False)
```

profile of v0, /device:TPU:0, one launch (start us, length us, event | category | flops | bytes accessed | tf_op | source)
XLA Modules:
  0.0 73.0 jit_solution(4951900636859663489)
XLA Ops:
  0.0 0.8 %slice_bitcast_fusion.5 = bf16[1,3,2048]{2,1,0:T(4,128)(2,1)S(1)} fusion(bf16[128,2048]{1,0:T(8,128)(2,1)} %param.9), kind=kLoop, calls=%fused_computation.47 | loop fusion | bytes 24576 | tf_op jit(solution)/shard_map/stack | solution.py:101
  0.8 0.8 %slice_bitcast_fusion.3 = (bf16[1,3,2048]{2,1,0:T(4,128)(2,1)S(1)}, bf16[1,3,2048]{2,1,0:T(4,128)(2,1)S(1)}) fusion(bf16[128,2048]{1,0:T(8,128)(2,1)} %param.11, bf16[128,2048]{1,0:T(8,128)(2,1)} %param.10), kind=kLoop, calls=%fused_computation.45 | loop fusion | bytes 49152 | tf_op jit(solution)/shard_map/stack | solution.py:101
  1.6 2.4 %collective-permute-start = (bf16[3,3,2048]{2,1,0:T(4,128)(2,1)S(1)}, bf16[3,3,2048]{2,1,0:T(4,128)(2,1)S(1)}, u32[]{:S(2)}, u32[]{:S(2)}) collective-permute-start(bf16[3,3,2048]{2,1,0:T(4,128)(2,1)S(1)} %pad_maximum_fusion.1), channel_id=1, source_target_pairs={{0,1},{1,2},{2,3},{3,4},{4,5},{5,6},{6,7},{7,8},{8,9},{9,10},{10,1... | collective-permute-start | bytes 110600 | tf_op jit(solution)/shard_map/ppermute | solution.py:20
  4.0 0.9 %collective-permute-done = bf16[3,3,2048]{2,1,0:T(4,128)(2,1)S(1)} collective-permute-done((bf16[3,3,2048]{2,1,0:T(4,128)(2,1)S(1)}, bf16[3,3,2048]{2,1,0:T(4,128)(2,1)S(1)}, u32[]{:S(2)}, u32[]{:S(2)}) %collective-permute-start) | collective-permute-done | bytes 36896 | tf_op jit(solution)/shard_map/ppermute | solution.py:20
  4.9 1.2 %maximum_convert_fusion = f32[128,2048]{1,0:T(8,128)S(1)} fusion(bf16[125,2048]{1,0:T(8,128)(2,1)} %bitcast.90, bf16[3,2048]{1,0:T(4,128)(2,1)S(1)} %get-tuple-element.347), kind=kLoop, calls=%fused_computation.22 | loop fusion | flops 1048576 | bytes 1572864 | tf_op jit(solution)/shard_map/convert_element_type | solution.py:37
  6.1 0.3 reshape.261
  6.4 0.0 copy-start
  6.4 0.6 reduce_sum.89
  7.2 0.1 reduce_sum.91
  7.4 0.1 copy-done
  7.5 0.1 maximum_convert_fusion.2
  7.6 0.0 copy-start.1
  7.6 0.3 reshape.263
  7.9 0.6 reduce_sum.95
  8.6 0.0 copy-done.1
  8.6 0.1 maximum_convert_fusion.1
  8.8 0.3 reshape.262
  9.1 0.0 copy-start.4
  9.1 0.0 copy-start.5
  9.1 0.6 reduce_sum.92
  9.9 0.0 copy-start.2
  9.9 0.1 reduce_sum.94
  10.1 0.0 copy-done.4
  10.1 0.1 fusion.12
  10.2 0.0 copy-done.5
  10.2 0.0 copy-start.3
  10.3 0.1 fusion.10
  10.5 0.8 %copy.30 = bf16[16,96,128]{2,1,0:T(8,128)(2,1)} copy(bf16[16,96,128]{2,0,1:T(8,128)(2,1)S(1)} %bitcast.85) | data formatting | bytes 786432 | tf_op jit(solution)/shard_map/reshape;reshape | solution.py:84
  11.3 9.5 %all-to-all-start.1 = ((bf16[16,96,128]{2,1,0:T(8,128)(2,1)}), bf16[16,96,128]{2,1,0:T(8,128)(2,1)S(1)}, u32[]{:S(2)}, u32[]{:S(2)}) async-start(bf16[16,96,128]{2,1,0:T(8,128)(2,1)} %copy.30), calls=%async_computation.1 | async-start | bytes 786432 | tf_op jit(solution)/shard_map/all_to_all | solution.py:123
  20.8 0.7 fusion.16
  22.2 0.0 copy-done.2
  22.2 0.3 copy.29
  22.5 0.1 bitcast_reduce_fusion
  22.6 0.0 copy-done.3
  22.6 1.1 %fusion.7 = bf16[128,2048]{0,1:T(8,128)(2,1)} fusion(bf16[128,2048]{0,1:T(8,128)(2,1)S(1)} %copy.29, f32[2048]{0:T(1024)S(1)} %copy-done.3, f32[128,16]{0,1:T(8,128)S(1)} %add_rsqrt_fusion), kind=kLoop, calls=%fused_computation.18 | loop fusion | flops 1048576 | bytes 1064960 | tf_op jit(solution)/shard_map/convert_element_type | solution.py:113
  23.8 0.1 broadcast_in_dim.17
  23.8 9.1 %all-to-all-done.1 = bf16[16,96,128]{2,1,0:T(8,128)(2,1)S(1)} async-done(((bf16[16,96,128]{2,1,0:T(8,128)(2,1)}), bf16[16,96,128]{2,1,0:T(8,128)(2,1)S(1)}, u32[]{:S(2)}, u32[]{:S(2)}) %all-to-all-start.1) | async-done | bytes 393248 | tf_op jit(solution)/shard_map/all_to_all | solution.py:123
  33.0 3.6 %all-to-all-start = ((bf16[16,128,128]{1,2,0:T(8,128)(2,1)}), bf16[16,128,128]{1,2,0:T(8,128)(2,1)S(1)}, u32[]{:S(2)}, u32[]{:S(2)}) async-start(bf16[16,128,128]{1,2,0:T(8,128)(2,1)} %bitcast.5), calls=%async_computation | async-start | bytes 1048576 | tf_op jit(solution)/shard_map/all_to_all | solution.py:124
  36.6 0.3 fusion.21
  36.9 0.3 multiply_reduce_fusion
  37.3 13.5 %all-to-all-done = bf16[16,128,128]{1,2,0:T(8,128)(2,1)S(1)} async-done(((bf16[16,128,128]{1,2,0:T(8,128)(2,1)}), bf16[16,128,128]{1,2,0:T(8,128)(2,1)S(1)}, u32[]{:S(2)}, u32[]{:S(2)}) %all-to-all-start) | async-done | bytes 524320 | tf_op jit(solution)/shard_map/all_to_all | solution.py:124
  50.8 2.4 %conditional.1 = ((f32[1,2048,128]{2,1,0:T(8,128)S(1)}, f32[1,2048]{1,0:T(1,128)S(1)})) conditional(s32[]{:T(128)} %convert_element_type.96, (f32[1,2048,128]{2,1,0:T(8,128)S(1)}, f32[1,2048]{1,0:T(1,128)S(1)}) %tuple.32, (s32[512]{0:T(512)S(1)}, s32[2048]{0:T(1024)S(1)}, s32[2048]{0:T(1024)S(1)}, s32[]{:T(128)}, ...), branch_computations={%region_9.0_spmd, %region_10.12_spmd.clone} | conditional | flops 542406656 | bytes 8194076 | solution.py:70
  50.8 0.3 copy.31
  51.1 1.2 %fusion.19 = (f32[2048]{0:T(1024)S(1)}, bf16[2048,512]{0,1:T(8,128)(2,1)S(1)}) fusion(bf16[2048,128]{1,0:T(8,128)(2,1)S(1)} %bitcast.93, bf16[512,128]{0,1:T(8,128)(2,1)S(1)} %get-tuple-element.339, s32[2048]{0:T(1024)S(1)} %add_select_fusion, s32[512]{0:T(512)S(1)} %get-tuple-element.279), kind=kOutput, calls=%fused_computation.62 | convolution fusion | flops 273676288 | bytes 2770944 | tf_op jit(solution)/shard_map/while/body/eval_jaxpr/cond/branch_1_fun/hqd,hkd->hqk/dot_general | solution.py:56
  52.3 0.9 %fusion = f32[1,2048,128]{2,1,0:T(8,128)S(1)} fusion(f32[1,2048,128]{2,1,0:T(8,128)S(1)} %get-tuple-element.278, bf16[512,128]{0,1:T(8,128)(2,1)S(1)} %get-tuple-element.339, bf16[2048,512]{0,1:T(8,128)(2,1)S(1)} %get-tuple-element.343), kind=kOutput, calls=%fused_computation.2 | convolution fusion | flops 268697600 | bytes 4325376 | tf_op jit(solution)/shard_map/while/body/eval_jaxpr/cond/branch_1_fun/hqk,hkd->hqd/dot_general | solution.py:62
  53.2 0.3 divide_convert_fusion
  53.6 18.2 %all_to_all.15 = bf16[16,128,128]{2,1,0:T(8,128)(2,1)S(1)} all-to-all(bf16[16,128,128]{2,1,0:T(8,128)(2,1)S(1)} %bitcast.83), channel_id=1, replica_groups=mesh['groups'=2,'seq'=16] {'seq'}, dimensions={0} | all-to-all | bytes 1048576 | tf_op jit(solution)/shard_map/all_to_all | solution.py:155
  71.7 0.3 copy.33
  72.0 1.0 %copy.34 = bf16[128,2048]{1,0:T(8,128)(2,1)} copy(bf16[128,2048]{0,1:T(8,128)(2,1)S(1)} %bitcast.84) | data formatting | bytes 1048576 | tf_op jit(solution)/shard_map/reshape | solution.py:157
  (22 shorter events, 0.5 us)
Async XLA Ops:
  1.6 3.3 %collective-permute-start = (bf16[3,3,2048]{2,1,0:T(4,128)(2,1)S(1)}, bf16[3,3,2048]{2,1,0:T(4,128)(2,1)S(1)}, u32[]{:S(2)}, u32[]{:S(2)}) collective-permute-start(bf16[3,3,2048]{2,1,0:T(4,128)(2,1)S(1)} %pad_maximum_fusion.1), channel_id=1, source_target_pairs={{0,1},{1,2},{2,3},{3,4},{4,5},{5,6},{6,7},{7,8},{8,9},{9,10},{10,1... | collective-permute-start | bytes 110600 | tf_op jit(solution)/shard_map/ppermute | solution.py:20
  6.4 1.0 %copy-start = (bf16[128,2048]{1,0:T(8,128)(2,1)S(1)}, bf16[128,2048]{1,0:T(8,128)(2,1)}, u32[]{:S(2)}) copy-start(bf16[128,2048]{1,0:T(8,128)(2,1)} %param.11) | copy-start | bytes 1572868
  7.6 1.0 %copy-start.1 = (bf16[128,2048]{1,0:T(8,128)(2,1)S(1)}, bf16[128,2048]{1,0:T(8,128)(2,1)}, u32[]{:S(2)}) copy-start(bf16[128,2048]{1,0:T(8,128)(2,1)} %param.10) | copy-start | bytes 1572868
  9.1 1.0 %copy-start.4 = (f32[2048]{0:T(1024)S(1)}, f32[2048]{0:T(1024)}, u32[]{:S(2)}) copy-start(f32[2048]{0:T(1024)} %param.13) | copy-start | bytes 24580
  9.1 1.1 %copy-start.5 = (f32[2048]{0:T(1024)S(1)}, f32[2048]{0:T(1024)}, u32[]{:S(2)}) copy-start(f32[2048]{0:T(1024)} %param.14) | copy-start | bytes 24580
  9.9 12.3 %copy-start.2 = (bf16[128,2048]{1,0:T(8,128)(2,1)S(1)}, bf16[128,2048]{1,0:T(8,128)(2,1)}, u32[]{:S(2)}) copy-start(bf16[128,2048]{1,0:T(8,128)(2,1)} %param.12) | copy-start | bytes 1572868
  10.2 12.4 %copy-start.3 = (f32[2048]{0:T(1024)S(1)}, f32[2048]{0:T(1024)}, u32[]{:S(2)}) copy-start(f32[2048]{0:T(1024)} %param.15) | copy-start | bytes 24580
  11.3 21.7 %all-to-all-start.1 = ((bf16[16,96,128]{2,1,0:T(8,128)(2,1)}), bf16[16,96,128]{2,1,0:T(8,128)(2,1)S(1)}, u32[]{:S(2)}, u32[]{:S(2)}) async-start(bf16[16,96,128]{2,1,0:T(8,128)(2,1)} %copy.30), calls=%async_computation.1 | async-start | bytes 786432 | tf_op jit(solution)/shard_map/all_to_all | solution.py:123
  33.0 17.8 %all-to-all-start = ((bf16[16,128,128]{1,2,0:T(8,128)(2,1)}), bf16[16,128,128]{1,2,0:T(8,128)(2,1)S(1)}, u32[]{:S(2)}, u32[]{:S(2)}) async-start(bf16[16,128,128]{1,2,0:T(8,128)(2,1)} %bitcast.5), calls=%async_computation | async-start | bytes 1048576 | tf_op jit(solution)/shard_map/all_to_all | solution.py:124
where the time goes:
time: 73.7 us; the launch traced here: 73 us
  waiting for transfers between devices  23.6 us (32%)
  blocking collectives  18.2 us (25%)
  starting transfers between devices  15.5 us (21%)
  other arithmetic  6.43 us (9%)
  local copies, waits for them, and re-layouts  5.64 us (8%)
  matrix products  2.67 us (4%)
  between operations  1.04 us (1%)
    all_to_all x1, blocking collectives, local(): lax.all_to_all(result, 'seq', split_axis=0, concat_axis=0, tiled=True)  18.2 us
    all_to_all x1, waiting for transfers between devices, local(): lax.all_to_all(up_out, 'seq', split_axis=0, concat_axis=0, tiled=True)  13.5 us
    all_to_all x1, starting transfers between devices, local(): lax.all_to_all(qkv_out, 'seq', split_axis=0, concat_axis=0, tiled=True)  9.53 us
    all_to_all x1, waiting for transfers between devices, local(): lax.all_to_all(qkv_out, 'seq', split_axis=0, concat_axis=0, tiled=True)  9.14 us
    all_to_all x1, starting transfers between devices, local(): lax.all_to_all(up_out, 'seq', split_axis=0, concat_axis=0, tiled=True)  3.57 us
    ppermute x1, starting transfers between devices, shifted(): lax.ppermute(value, axis, [(source, source + steps) for source in range(l...  2.4 us
    reduce_sum x3, other arithmetic, pooled_rows(): return jnp.mean(widened.reshape(-1, SHORT, widened.shape[1]), axis=1)  1.9 us
    another operation x2, local copies, waits for them, and re-layouts, local(): jnp.stack([query_src[token_count - SHIFT:], key_src[token_count - SHIFT:]...  1.57 us
  transfers between devices with their start and end apart: 3, of which 3 were waited for; matrix products, arithmetic and copies ran while one was open for 4% of the time, Pallas kernels for 0%

commit v1 on v0

--- a/solution.py
+++ b/solution.py
@@ -1,8 +1,11 @@
+import functools
 import math
 
 import jax
 import jax.numpy as jnp
 from jax import lax
+from jax.experimental import pallas as pl
+from jax.experimental.pallas import tpu as pltpu
 from jax.sharding import PartitionSpec as P
 
 HEADS = 16
@@ -92,7 +95,7 @@
     return jnp.transpose(parted, (2, 0, 1, 3)).reshape(device_count, piece, HDIM)
 
 
-def local(query_src, key_src, value_src, up_query, query_gain, key_gain, up_gain):
+def head_exchange(query_src, key_src, value_src, up_query, query_gain, key_gain, up_gain):
     device_count = lax.axis_size("seq")
     device_index = lax.axis_index("seq")
     block_count = device_count // HEADS
@@ -157,6 +160,169 @@
     return jnp.transpose(output_heads, (1, 0, 2)).reshape(token_count, HEADS * HDIM)
 
 
+EDGE_ROWS = 16
+
+
+def rms_rows(values):
+    return values * lax.rsqrt(jnp.mean(values * values, axis=-1, keepdims=True) + epsilon)
+
+
+def select_matrix(tokens, rows, slot):
+    row = lax.broadcasted_iota(jnp.int32, (rows + EDGE_ROWS, tokens), 0)
+    col = lax.broadcasted_iota(jnp.int32, (rows + EDGE_ROWS, tokens), 1)
+    pooled = (row < rows) & (col <= SHORT * row) & (col >= SHORT * row - SHIFT)
+    weight = jnp.where(row == 0, 1.0, 1.0 / SHORT)
+    edge = (row >= rows + slot * SHIFT) & (row < rows + (slot + 1) * SHIFT)
+    edge = edge & (col == tokens - SHIFT + row - rows - slot * SHIFT)
+    return jnp.where(pooled, weight, jnp.where(edge, 1.0, 0.0)).astype(jnp.bfloat16)
+
+
+def pool_kernel(query_ref, key_ref, value_ref, query_gain_ref, key_gain_ref, out_ref):
+    tokens, width = query_ref.shape
+    rows = tokens // SHORT
+    picked = [
+        jnp.dot(select_matrix(tokens, rows, slot), ref[...], preferred_element_type=jnp.float32)
+        for slot, ref in enumerate((query_ref, key_ref, value_ref))
+    ]
+    first = lax.broadcasted_iota(jnp.int32, (rows, HDIM), 0) == 0
+    gains = (query_gain_ref, key_gain_ref)
+    for head in range(width // HDIM):
+        columns = slice(head * HDIM, (head + 1) * HDIM)
+        for slot in range(3):
+            part = picked[slot][:rows, columns]
+            if slot < 2:
+                part = jnp.where(first, part, rms_rows(part) * gains[slot][:, columns])
+            out_ref[head, slot * rows : (slot + 1) * rows, :] = part.astype(jnp.bfloat16)
+        edge = sum(values[rows:, columns] for values in picked)
+        out_ref[head, 3 * rows :, :] = edge.astype(jnp.bfloat16)
+
+
+def pool_inputs(query_src, key_src, value_src, query_gain, key_gain, heads_at_once):
+    tokens, columns = query_src.shape
+    width = heads_at_once * HDIM
+    depth = 3 * (tokens // SHORT) + EDGE_ROWS
+    source = pl.BlockSpec((tokens, width), lambda step: (0, step))
+    gain = pl.BlockSpec((1, width), lambda step: (0, step))
+    return pl.pallas_call(
+        pool_kernel,
+        grid=(columns // width,),
+        in_specs=[source, source, source, gain, gain],
+        out_specs=pl.BlockSpec((heads_at_once, depth, HDIM), lambda step: (step, 0, 0)),
+        out_shape=jax.ShapeDtypeStruct((columns // HDIM, depth, HDIM), jnp.bfloat16),
+    )(query_src, key_src, value_src, query_gain.reshape(1, -1), key_gain.reshape(1, -1))
+
+
+def masked_exp(scores, visible):
+    exponent = jnp.exp(scores * (1.0 / math.sqrt(HDIM)))
+    return exponent if visible is None else jnp.where(visible, exponent, 0.0)
+
+
+def across(left, right):
+    return lax.dot_general(
+        left, right, (((1,), (1,)), ((), ())), preferred_element_type=jnp.float32
+    )
+
+
+def short_kernel(block, arrived_ref, query_gain_ref, key_gain_ref, memory_ref):
+    count, depth, _ = arrived_ref.shape
+    rows = (depth - EDGE_ROWS) // 3
+    head = lax.axis_index("seq")
+    edges = arrived_ref[:, 3 * rows :, :].astype(jnp.float32)
+    edge_row = lax.broadcasted_iota(jnp.int32, edges.shape, 1)
+    first = lax.broadcasted_iota(jnp.int32, (count, rows, HDIM), 1) == 0
+    tensors = []
+    for slot, gain_ref in enumerate((query_gain_ref, key_gain_ref, None)):
+        part = arrived_ref[:, slot * rows : (slot + 1) * rows, :].astype(jnp.float32)
+        own = (edge_row >= slot * SHIFT) & (edge_row < (slot + 1) * SHIFT)
+        tail = jnp.sum(jnp.where(own, edges, 0.0), axis=1, keepdims=True)
+        before = jnp.concatenate([jnp.zeros_like(tail[:1]), tail[:-1]], axis=0)
+        mean = (before + part[:, :1, :]) * (1.0 / SHORT)
+        if gain_ref is not None:
+            mean = rms_rows(mean) * gain_ref[pl.ds(head, 1), :][None]
+        part = jnp.where(first, mean, part).astype(jnp.bfloat16)
+        tensors.append(part.reshape(count * rows, HDIM))
+    query, key, value = tensors
+    diagonal = lax.broadcasted_iota(jnp.int32, (block, block), 1) <= lax.broadcasted_iota(
+        jnp.int32, (block, block), 0
+    )
+    for start in range(0, count * rows, block):
+        part = query[start : start + block]
+        exponent = masked_exp(across(part, key[start : start + block]), diagonal)
+        denominator = jnp.sum(exponent, axis=1, keepdims=True)
+        numerator = jnp.dot(
+            exponent.astype(jnp.bfloat16),
+            value[start : start + block],
+            preferred_element_type=jnp.float32,
+        )
+        if start:
+            exponent = masked_exp(across(part, key[:start]), None)
+            denominator += jnp.sum(exponent, axis=1, keepdims=True)
+            numerator += jnp.dot(
+                exponent.astype(jnp.bfloat16), value[:start], preferred_element_type=jnp.float32
+            )
+        memory_ref[start : start + block, :] = rms_rows(numerator / denominator).astype(
+            jnp.bfloat16
+        )
+
+
+def short_attention(arrived, query_gain, key_gain):
+    count, depth, _ = arrived.shape
+    row_total = count * (depth - EDGE_ROWS) // 3
+    return pl.pallas_call(
+        functools.partial(short_kernel, math.gcd(128, row_total)),
+        out_shape=jax.ShapeDtypeStruct((row_total, HDIM), jnp.bfloat16),
+    )(arrived, query_gain.reshape(-1, HDIM), key_gain.reshape(-1, HDIM))
+
+
+def up_kernel(offsets, up_ref, gain_ref, *refs):
+    unit_refs, out_ref = refs[:-1], refs[-1]
+    tokens = up_ref.shape[0]
+    row_total = unit_refs[0].shape[0]
+    device = lax.axis_index("seq")
+    limit = device * tokens + lax.broadcasted_iota(jnp.int32, (tokens, row_total), 0)
+    visible = SHORT * lax.broadcasted_iota(jnp.int32, (tokens, row_total), 1) <= limit
+    for offset, unit_ref in zip(offsets, unit_refs):
+        head = device ^ offset
+        columns = pl.ds(pl.multiple_of(head * HDIM, HDIM), HDIM)
+        query = rms_rows(up_ref[:, columns].astype(jnp.float32)) * gain_ref[pl.ds(head, 1), :]
+        memory = unit_ref[...]
+        exponent = masked_exp(across(query.astype(jnp.bfloat16), memory), visible)
+        denominator = jnp.sum(exponent, axis=1, keepdims=True)
+        numerator = jnp.dot(
+            exponent.astype(jnp.bfloat16), memory, preferred_element_type=jnp.float32
+        )
+        out_ref[:, columns] = (numerator / denominator).astype(jnp.bfloat16)
+
+
+def up_attention(up_query, up_gain, units):
+    offsets = tuple(sorted(units))
+    return pl.pallas_call(
+        functools.partial(up_kernel, offsets),
+        out_shape=jax.ShapeDtypeStruct(up_query.shape, jnp.bfloat16),
+    )(up_query, up_gain.reshape(-1, HDIM), *[units[offset] for offset in offsets])
+
+
+def swapped(value, offset):
+    count = lax.axis_size("seq")
+    return lax.ppermute(value, "seq", [(source, source ^ offset) for source in range(count)])
+
+
+def memory_gather(query_src, key_src, value_src, up_query, query_gain, key_gain, up_gain):
+    outgoing = pool_inputs(query_src, key_src, value_src, query_gain, key_gain, HEADS // 4)
+    arrived = lax.all_to_all(outgoing, "seq", split_axis=0, concat_axis=0, tiled=True)
+    units = {0: short_attention(arrived, query_gain, key_gain)}
+    offset = HEADS // 2
+    while offset:
+        units.update({held ^ offset: swapped(units[held], offset) for held in list(units)})
+        offset //= 2
+    return up_attention(up_query, up_gain, units)
+
+
+def local(*arrays):
+    whole = lax.axis_size("seq") == HEADS and HEADS & (HEADS - 1) == 0
+    return memory_gather(*arrays) if whole else head_exchange(*arrays)
+
+
 def solution(mesh):
     in_specs = (
         P(("groups", "seq"), None),

time: 73.7 us -> 55.6 us (0.75)
  Pallas kernels: 0 us -> 12.5 us
  waiting for transfers between devices: 23.6 us -> 12.8 us
  starting transfers between devices: 15.5 us -> 8.45 us
  other arithmetic: 6.43 us -> 0 us
  local copies, waits for them, and re-layouts: 5.64 us -> 0.58 us
  matrix products: 2.67 us -> 0 us
  blocking collectives: 18.2 us -> 20.7 us
  between operations: 1.04 us -> 0.22 us
    all_to_all x2 -> x0, waiting for transfers between devices: 22.7 us -> none  [the longest x1 13.5 us: local(): lax.all_to_all(up_out, 'seq', split_axis=0, concat_axis=0, tiled=True)]
    all_to_all x2 -> x0, starting transfers between devices: 13.1 us -> none  [the longest x1 9.53 us: local(): lax.all_to_all(qkv_out, 'seq', split_axis=0, concat_axis=0, tiled=True)]
    pallas_call x0 -> x3, Pallas kernels: none -> 12.5 us  [the longest x1 5.87 us: up_attention(): pl.pallas_call(functools.partial(up_kernel, offsets), out_shape=jax.Shape...]
    ppermute x1 -> x15, waiting for transfers between devices: 0.86 us -> 12.8 us  [swapped(): lax.ppermute(value, 'seq', [(source, source ^ offset) for source in range...]
    ppermute x1 -> x15, starting transfers between devices: 2.4 us -> 8.45 us  [swapped(): lax.ppermute(value, 'seq', [(source, source ^ offset) for source in range...]
    convert_element_type x8 -> x0, other arithmetic: 3.21 us -> none  [the longest x3 1.45 us: pooled_rows(): jnp.concatenate([edge_rows, source[:source.shape[0] - SHIFT]], axis=0)]
    another operation x4 -> x0, local copies, waits for them, and re-layouts: 2.69 us -> none  [the longest x2 1.57 us: local(): jnp.stack([query_src[token_count - SHIFT:], key_src[token_count - SHIFT:]...]
    dot_general x4 -> x0, matrix products: 2.67 us -> none  [the longest x2 1.49 us: compute(): jnp.einsum('hqd,hkd->hqk', queries, key_block, preferred_element_type=jnp...]
  transfers between devices with their start and end apart: 3 -> 15, of which waited for: 3 -> 5; matrix products, arithmetic and copies ran while one was open for 4% -> 0% of each run, Pallas kernels for 0% -> 0%
where the time goes in v1:
time: 55.6 us; the launch traced here: 55.3 us
  blocking collectives  20.7 us (37%)
  waiting for transfers between devices  12.8 us (23%)
  Pallas kernels  12.5 us (22%)
  starting transfers between devices  8.45 us (15%)
  local copies, waits for them, and re-layouts  0.58 us (1%)
    all_to_all x1, blocking collectives, memory_gather(): lax.all_to_all(outgoing, 'seq', split_axis=0, concat_axis=0, tiled=True)  20.7 us
    ppermute x15, waiting for transfers between devices, swapped(): lax.ppermute(value, 'seq', [(source, source ^ offset) for source in range...  12.8 us
    ppermute x15, starting transfers between devices, swapped(): lax.ppermute(value, 'seq', [(source, source ^ offset) for source in range...  8.45 us
    pallas_call x1, Pallas kernels, up_attention(): pl.pallas_call(functools.partial(up_kernel, offsets), out_shape=jax.Shape...  5.87 us
    pallas_call x1, Pallas kernels, pool_inputs(): pl.pallas_call(pool_kernel, grid=(columns // width,), in_specs=[source, s...  3.96 us
    pallas_call x1, Pallas kernels, short_attention(): pl.pallas_call(functools.partial(short_kernel, math.gcd(128, row_total)),...  2.7 us
  transfers between devices with their start and end apart: 15, of which 5 were waited for; matrix products, arithmetic and copies ran while one was open for 0% of the time, Pallas kernels for 0%

profile of v1, /device:TPU:0, one launch (start us, length us, event | category | flops | bytes accessed | tf_op | source)
XLA Modules:
  0.0 55.3 jit_solution(9437177844861912590)
XLA Ops:
  0.0 4.0 %shard_map.73 = bf16[16,112,128]{2,1,0:T(8,128)(2,1)} custom-call(bf16[128,2048]{1,0:T(8,128)(2,1)} %query_ref.1, bf16[128,2048]{1,0:T(8,128)(2,1)} %key_ref.1, bf16[128,2048]{1,0:T(8,128)(2,1)} %value_ref.1, f32[1,2048]{1,0:T(1,128)} %bitcast.5, f32[1,2048]{1,0:T(1,128)} %bitcast.7), custom_call_target="tpu_custom_call" | custom-call | tf_op jit(solution)/shard_map/pallas_call | solution.py:206
  4.0 20.7 %all_to_all.5.arrived_ref = bf16[16,112,128]{2,1,0:T(8,128)(2,1)} all-to-all(bf16[16,112,128]{2,1,0:T(8,128)(2,1)} %shard_map.73), channel_id=1, replica_groups=mesh['groups'=2,'seq'=16] {'seq'}, dimensions={0} | all-to-all | bytes 917504 | tf_op jit(solution)/shard_map/all_to_all | solution.py:312
  24.7 2.7 %shard_map.74.refs_0_ = bf16[512,128]{1,0:T(8,128)(2,1)} custom-call(bf16[16,112,128]{2,1,0:T(8,128)(2,1)} %all_to_all.5.arrived_ref, f32[16,128]{1,0:T(8,128)} %bitcast.6, f32[16,128]{1,0:T(8,128)} %bitcast.8), custom_call_target="tpu_custom_call" | custom-call | tf_op jit(solution)/shard_map/pallas_call | solution.py:271
  27.4 2.1 %collective-permute-start.7 = (bf16[512,128]{1,0:T(8,128)(2,1)}, bf16[512,128]{1,0:T(8,128)(2,1)S(1)}, u32[]{:S(2)}, u32[]{:S(2)}) collective-permute-start(bf16[512,128]{1,0:T(8,128)(2,1)} %shard_map.74.refs_0_), channel_id=1, source_target_pairs={{0,8},{1,9},{2,10},{3,11},{4,12},{5,13},{6,14},{7,15},{8,0},{9,1},... | collective-permute-start | bytes 393224 | tf_op jit(solution)/shard_map/ppermute | solution.py:307
  29.4 0.0 collective-permute-start.3
  29.4 1.5 %collective-permute-start.1 = (bf16[512,128]{1,0:T(8,128)(2,1)}, bf16[512,128]{1,0:T(8,128)(2,1)S(1)}, u32[]{:S(2)}, u32[]{:S(2)}) collective-permute-start(bf16[512,128]{1,0:T(8,128)(2,1)} %shard_map.74.refs_0_), channel_id=1, source_target_pairs={{0,2},{1,3},{2,0},{3,1},{4,6},{5,7},{6,4},{7,5},{8,10},{9,11},{10,... | collective-permute-start | bytes 393224 | tf_op jit(solution)/shard_map/ppermute | solution.py:307
  30.9 0.0 collective-permute-start
  30.9 5.9 %collective-permute-done.7.refs_8_ = bf16[512,128]{1,0:T(8,128)(2,1)S(1)} collective-permute-done((bf16[512,128]{1,0:T(8,128)(2,1)}, bf16[512,128]{1,0:T(8,128)(2,1)S(1)}, u32[]{:S(2)}, u32[]{:S(2)}) %collective-permute-start.7) | collective-permute-done | bytes 131104 | tf_op jit(solution)/shard_map/ppermute | solution.py:307
  36.8 0.0 copy-start
  36.8 0.0 collective-permute-start.11
  36.8 1.1 %collective-permute-start.9 = (bf16[512,128]{1,0:T(8,128)(2,1)S(1)}, bf16[512,128]{1,0:T(8,128)(2,1)S(1)}, u32[]{:S(2)}, u32[]{:S(2)}) collective-permute-start(bf16[512,128]{1,0:T(8,128)(2,1)S(1)} %collective-permute-done.7.refs_8_), channel_id=1, source_target_pairs={{0,2},{1,3},{2,0},{3,1},{4,6},{5,7},{6,4},{7,5},{8,10},{9,11},{10,... | collective-permute-start | bytes 393224 | tf_op jit(solution)/shard_map/ppermute | solution.py:307
  37.9 0.0 collective-permute-done.3.refs_4_
  37.9 0.0 copy-start.1
  37.9 0.0 collective-permute-start.8
  37.9 0.0 collective-permute-done.1.refs_2_
  38.0 0.0 copy-start.2
  38.0 1.0 %collective-permute-start.5 = (bf16[512,128]{1,0:T(8,128)(2,1)S(1)}, bf16[512,128]{1,0:T(8,128)(2,1)S(1)}, u32[]{:S(2)}, u32[]{:S(2)}) collective-permute-start(bf16[512,128]{1,0:T(8,128)(2,1)S(1)} %collective-permute-done.3.refs_4_), channel_id=1, source_target_pairs={{0,2},{1,3},{2,0},{3,1},{4,6},{5,7},{6,4},{7,5},{8,10},{9,11},{10,... | collective-permute-start | bytes 393224 | tf_op jit(solution)/shard_map/ppermute | solution.py:307
  38.9 0.0 collective-permute-done.refs_1_
  38.9 0.0 copy-start.3
  38.9 0.1 collective-permute-start.4
  39.1 2.7 %collective-permute-done.11.refs_12_ = bf16[512,128]{1,0:T(8,128)(2,1)S(1)} collective-permute-done((bf16[512,128]{1,0:T(8,128)(2,1)S(1)}, bf16[512,128]{1,0:T(8,128)(2,1)S(1)}, u32[]{:S(2)}, u32[]{:S(2)}) %collective-permute-start.11) | collective-permute-done | bytes 131104 | tf_op jit(solution)/shard_map/ppermute | solution.py:307
  41.8 0.0 copy-start.4
  41.8 1.7 %collective-permute-start.13 = (bf16[512,128]{1,0:T(8,128)(2,1)S(1)}, bf16[512,128]{1,0:T(8,128)(2,1)S(1)}, u32[]{:S(2)}, u32[]{:S(2)}) collective-permute-start(bf16[512,128]{1,0:T(8,128)(2,1)S(1)} %collective-permute-done.11.refs_12_), channel_id=1, source_target_pairs={{0,2},{1,3},{2,0},{3,1},{4,6},{5,7},{6,4},{7,5},{8,10},{9,11},{10,... | collective-permute-start | bytes 393224 | tf_op jit(solution)/shard_map/ppermute | solution.py:307
  43.4 0.0 collective-permute-done.9.refs_10_
  43.5 0.0 copy-start.5
  43.5 0.0 collective-permute-start.2
  43.5 0.0 collective-permute-done.8.refs_9_
  43.5 0.0 copy-start.6
  43.5 0.5 collective-permute-start.12
  44.0 1.4 %collective-permute-done.5.refs_6_ = bf16[512,128]{1,0:T(8,128)(2,1)S(1)} collective-permute-done((bf16[512,128]{1,0:T(8,128)(2,1)S(1)}, bf16[512,128]{1,0:T(8,128)(2,1)S(1)}, u32[]{:S(2)}, u32[]{:S(2)}) %collective-permute-start.5) | collective-permute-done | bytes 131104 | tf_op jit(solution)/shard_map/ppermute | solution.py:307
  45.3 0.0 copy-start.7
  45.3 0.0 collective-permute-start.10
  45.3 0.0 collective-permute-done.4.refs_5_
  45.3 0.0 copy-start.8
  45.3 0.5 collective-permute-start.6
  45.8 1.6 %collective-permute-done.13.refs_14_ = bf16[512,128]{1,0:T(8,128)(2,1)S(1)} collective-permute-done((bf16[512,128]{1,0:T(8,128)(2,1)S(1)}, bf16[512,128]{1,0:T(8,128)(2,1)S(1)}, u32[]{:S(2)}, u32[]{:S(2)}) %collective-permute-start.13) | collective-permute-done | bytes 131104 | tf_op jit(solution)/shard_map/ppermute | solution.py:307
  47.4 0.0 copy-start.9
  47.4 0.0 collective-permute-start.14
  47.4 0.0 collective-permute-done.2.refs_3_
  47.4 0.0 copy-start.10
  47.4 0.0 collective-permute-done.12.refs_13_
  47.4 0.0 copy-start.11
  47.4 0.0 collective-permute-done.10.refs_11_
  47.5 0.0 copy-start.12
  47.5 0.0 collective-permute-done.6.refs_7_
  47.5 0.0 copy-start.13
  47.5 1.3 %collective-permute-done.14.refs_15_ = bf16[512,128]{1,0:T(8,128)(2,1)S(1)} collective-permute-done((bf16[512,128]{1,0:T(8,128)(2,1)S(1)}, bf16[512,128]{1,0:T(8,128)(2,1)S(1)}, u32[]{:S(2)}, u32[]{:S(2)}) %collective-permute-start.14) | collective-permute-done | bytes 131104 | tf_op jit(solution)/shard_map/ppermute | solution.py:307
  48.8 0.0 copy-start.14
  48.8 0.0 copy-done
  48.8 0.0 copy-done.1
  48.8 0.0 copy-done.2
  48.8 0.0 copy-done.3
  48.8 0.0 copy-done.4
  48.8 0.0 copy-done.5
  48.8 0.0 copy-done.6
  48.8 0.0 copy-done.7
  48.8 0.0 copy-done.8
  48.8 0.0 copy-done.9
  48.8 0.0 copy-done.10
  48.8 0.0 copy-done.11
  48.9 0.0 copy-done.12
  48.9 0.0 copy-done.13
  48.9 0.5 copy-done.14
  49.4 5.9 %shard_map.75 = bf16[128,2048]{1,0:T(8,128)(2,1)} custom-call(bf16[128,2048]{1,0:T(8,128)(2,1)} %up_ref.1, f32[16,128]{1,0:T(8,128)} %bitcast.9, bf16[512,128]{1,0:T(8,128)(2,1)} %shard_map.74.refs_0_, bf16[512,128]{1,0:T(8,128)(2,1)} %copy-done.3, bf16[512,128]{1,0:T(8,128)(2,1)} %copy-done.2, bf16[512,128]{1,0:T(8,128)(2,1)} %copy-done.10, ...), custom_call_target="tpu_custom_call" | custom-call | tf_op jit(solution)/shard_map/pallas_call | solution.py:299
Async XLA Ops:
  27.4 9.4 %collective-permute-start.7 = (bf16[512,128]{1,0:T(8,128)(2,1)}, bf16[512,128]{1,0:T(8,128)(2,1)S(1)}, u32[]{:S(2)}, u32[]{:S(2)}) collective-permute-start(bf16[512,128]{1,0:T(8,128)(2,1)} %shard_map.74.refs_0_), channel_id=1, source_target_pairs={{0,8},{1,9},{2,10},{3,11},{4,12},{5,13},{6,14},{7,15},{8,0},{9,1},... | collective-permute-start | bytes 393224 | tf_op jit(solution)/shard_map/ppermute | solution.py:307
  29.4 8.5 %collective-permute-start.3 = (bf16[512,128]{1,0:T(8,128)(2,1)}, bf16[512,128]{1,0:T(8,128)(2,1)S(1)}, u32[]{:S(2)}, u32[]{:S(2)}) collective-permute-start(bf16[512,128]{1,0:T(8,128)(2,1)} %shard_map.74.refs_0_), channel_id=1, source_target_pairs={{0,4},{1,5},{2,6},{3,7},{4,0},{5,1},{6,2},{7,3},{8,12},{9,13},{10,... | collective-permute-start | bytes 393224 | tf_op jit(solution)/shard_map/ppermute | solution.py:307
  29.4 8.5 %collective-permute-start.1 = (bf16[512,128]{1,0:T(8,128)(2,1)}, bf16[512,128]{1,0:T(8,128)(2,1)S(1)}, u32[]{:S(2)}, u32[]{:S(2)}) collective-permute-start(bf16[512,128]{1,0:T(8,128)(2,1)} %shard_map.74.refs_0_), channel_id=1, source_target_pairs={{0,2},{1,3},{2,0},{3,1},{4,6},{5,7},{6,4},{7,5},{8,10},{9,11},{10,... | collective-permute-start | bytes 393224 | tf_op jit(solution)/shard_map/ppermute | solution.py:307
  30.9 8.0 %collective-permute-start = (bf16[512,128]{1,0:T(8,128)(2,1)}, bf16[512,128]{1,0:T(8,128)(2,1)S(1)}, u32[]{:S(2)}, u32[]{:S(2)}) collective-permute-start(bf16[512,128]{1,0:T(8,128)(2,1)} %shard_map.74.refs_0_), channel_id=1, source_target_pairs={{0,1},{1,0},{2,3},{3,2},{4,5},{5,4},{6,7},{7,6},{8,9},{9,8},{10,11... | collective-permute-start | bytes 393224 | tf_op jit(solution)/shard_map/ppermute | solution.py:307
  36.8 11.9 %copy-start = (bf16[512,128]{1,0:T(8,128)(2,1)}, bf16[512,128]{1,0:T(8,128)(2,1)S(1)}, u32[]{:S(2)}) copy-start(bf16[512,128]{1,0:T(8,128)(2,1)S(1)} %collective-permute-done.7.refs_8_) | copy-start | bytes 393220
  36.8 5.0 %collective-permute-start.11 = (bf16[512,128]{1,0:T(8,128)(2,1)S(1)}, bf16[512,128]{1,0:T(8,128)(2,1)S(1)}, u32[]{:S(2)}, u32[]{:S(2)}) collective-permute-start(bf16[512,128]{1,0:T(8,128)(2,1)S(1)} %collective-permute-done.7.refs_8_), channel_id=1, source_target_pairs={{0,4},{1,5},{2,6},{3,7},{4,0},{5,1},{6,2},{7,3},{8,12},{9,13},{10,... | collective-permute-start | bytes 393224 | tf_op jit(solution)/shard_map/ppermute | solution.py:307
  36.8 6.6 %collective-permute-start.9 = (bf16[512,128]{1,0:T(8,128)(2,1)S(1)}, bf16[512,128]{1,0:T(8,128)(2,1)S(1)}, u32[]{:S(2)}, u32[]{:S(2)}) collective-permute-start(bf16[512,128]{1,0:T(8,128)(2,1)S(1)} %collective-permute-done.7.refs_8_), channel_id=1, source_target_pairs={{0,2},{1,3},{2,0},{3,1},{4,6},{5,7},{6,4},{7,5},{8,10},{9,11},{10,... | collective-permute-start | bytes 393224 | tf_op jit(solution)/shard_map/ppermute | solution.py:307
  37.9 10.8 %copy-start.1 = (bf16[512,128]{1,0:T(8,128)(2,1)}, bf16[512,128]{1,0:T(8,128)(2,1)S(1)}, u32[]{:S(2)}) copy-start(bf16[512,128]{1,0:T(8,128)(2,1)S(1)} %collective-permute-done.3.refs_4_) | copy-start | bytes 393220
  37.9 5.5 %collective-permute-start.8 = (bf16[512,128]{1,0:T(8,128)(2,1)S(1)}, bf16[512,128]{1,0:T(8,128)(2,1)S(1)}, u32[]{:S(2)}, u32[]{:S(2)}) collective-permute-start(bf16[512,128]{1,0:T(8,128)(2,1)S(1)} %collective-permute-done.7.refs_8_), channel_id=1, source_target_pairs={{0,1},{1,0},{2,3},{3,2},{4,5},{5,4},{6,7},{7,6},{8,9},{9,8},{10,11... | collective-permute-start | bytes 393224 | tf_op jit(solution)/shard_map/ppermute | solution.py:307
  38.0 10.8 %copy-start.2 = (bf16[512,128]{1,0:T(8,128)(2,1)}, bf16[512,128]{1,0:T(8,128)(2,1)S(1)}, u32[]{:S(2)}) copy-start(bf16[512,128]{1,0:T(8,128)(2,1)S(1)} %collective-permute-done.1.refs_2_) | copy-start | bytes 393220
  38.0 7.4 %collective-permute-start.5 = (bf16[512,128]{1,0:T(8,128)(2,1)S(1)}, bf16[512,128]{1,0:T(8,128)(2,1)S(1)}, u32[]{:S(2)}, u32[]{:S(2)}) collective-permute-start(bf16[512,128]{1,0:T(8,128)(2,1)S(1)} %collective-permute-done.3.refs_4_), channel_id=1, source_target_pairs={{0,2},{1,3},{2,0},{3,1},{4,6},{5,7},{6,4},{7,5},{8,10},{9,11},{10,... | collective-permute-start | bytes 393224 | tf_op jit(solution)/shard_map/ppermute | solution.py:307
  38.9 9.8 %copy-start.3 = (bf16[512,128]{1,0:T(8,128)(2,1)}, bf16[512,128]{1,0:T(8,128)(2,1)S(1)}, u32[]{:S(2)}) copy-start(bf16[512,128]{1,0:T(8,128)(2,1)S(1)} %collective-permute-done.refs_1_) | copy-start | bytes 393220
  38.9 6.4 %collective-permute-start.4 = (bf16[512,128]{1,0:T(8,128)(2,1)S(1)}, bf16[512,128]{1,0:T(8,128)(2,1)S(1)}, u32[]{:S(2)}, u32[]{:S(2)}) collective-permute-start(bf16[512,128]{1,0:T(8,128)(2,1)S(1)} %collective-permute-done.3.refs_4_), channel_id=1, source_target_pairs={{0,1},{1,0},{2,3},{3,2},{4,5},{5,4},{6,7},{7,6},{8,9},{9,8},{10,11... | collective-permute-start | bytes 393224 | tf_op jit(solution)/shard_map/ppermute | solution.py:307
  41.8 7.0 %copy-start.4 = (bf16[512,128]{1,0:T(8,128)(2,1)}, bf16[512,128]{1,0:T(8,128)(2,1)S(1)}, u32[]{:S(2)}) copy-start(bf16[512,128]{1,0:T(8,128)(2,1)S(1)} %collective-permute-done.11.refs_12_) | copy-start | bytes 393220
  41.8 5.6 %collective-permute-start.13 = (bf16[512,128]{1,0:T(8,128)(2,1)S(1)}, bf16[512,128]{1,0:T(8,128)(2,1)S(1)}, u32[]{:S(2)}, u32[]{:S(2)}) collective-permute-start(bf16[512,128]{1,0:T(8,128)(2,1)S(1)} %collective-permute-done.11.refs_12_), channel_id=1, source_target_pairs={{0,2},{1,3},{2,0},{3,1},{4,6},{5,7},{6,4},{7,5},{8,10},{9,11},{10,... | collective-permute-start | bytes 393224 | tf_op jit(solution)/shard_map/ppermute | solution.py:307
  43.5 5.3 %copy-start.5 = (bf16[512,128]{1,0:T(8,128)(2,1)}, bf16[512,128]{1,0:T(8,128)(2,1)S(1)}, u32[]{:S(2)}) copy-start(bf16[512,128]{1,0:T(8,128)(2,1)S(1)} %collective-permute-done.9.refs_10_) | copy-start | bytes 393220
  43.5 4.0 %collective-permute-start.2 = (bf16[512,128]{1,0:T(8,128)(2,1)S(1)}, bf16[512,128]{1,0:T(8,128)(2,1)S(1)}, u32[]{:S(2)}, u32[]{:S(2)}) collective-permute-start(bf16[512,128]{1,0:T(8,128)(2,1)S(1)} %collective-permute-done.1.refs_2_), channel_id=1, source_target_pairs={{0,1},{1,0},{2,3},{3,2},{4,5},{5,4},{6,7},{7,6},{8,9},{9,8},{10,11... | collective-permute-start | bytes 393224 | tf_op jit(solution)/shard_map/ppermute | solution.py:307
  43.5 5.3 %copy-start.6 = (bf16[512,128]{1,0:T(8,128)(2,1)}, bf16[512,128]{1,0:T(8,128)(2,1)S(1)}, u32[]{:S(2)}) copy-start(bf16[512,128]{1,0:T(8,128)(2,1)S(1)} %collective-permute-done.8.refs_9_) | copy-start | bytes 393220
  43.5 3.9 %collective-permute-start.12 = (bf16[512,128]{1,0:T(8,128)(2,1)S(1)}, bf16[512,128]{1,0:T(8,128)(2,1)S(1)}, u32[]{:S(2)}, u32[]{:S(2)}) collective-permute-start(bf16[512,128]{1,0:T(8,128)(2,1)S(1)} %collective-permute-done.11.refs_12_), channel_id=1, source_target_pairs={{0,1},{1,0},{2,3},{3,2},{4,5},{5,4},{6,7},{7,6},{8,9},{9,8},{10,11... | collective-permute-start | bytes 393224 | tf_op jit(solution)/shard_map/ppermute | solution.py:307
  45.3 3.5 %copy-start.7 = (bf16[512,128]{1,0:T(8,128)(2,1)}, bf16[512,128]{1,0:T(8,128)(2,1)S(1)}, u32[]{:S(2)}) copy-start(bf16[512,128]{1,0:T(8,128)(2,1)S(1)} %collective-permute-done.5.refs_6_) | copy-start | bytes 393220
  45.3 2.1 %collective-permute-start.10 = (bf16[512,128]{1,0:T(8,128)(2,1)S(1)}, bf16[512,128]{1,0:T(8,128)(2,1)S(1)}, u32[]{:S(2)}, u32[]{:S(2)}) collective-permute-start(bf16[512,128]{1,0:T(8,128)(2,1)S(1)} %collective-permute-done.9.refs_10_), channel_id=1, source_target_pairs={{0,1},{1,0},{2,3},{3,2},{4,5},{5,4},{6,7},{7,6},{8,9},{9,8},{10,11... | collective-permute-start | bytes 393224 | tf_op jit(solution)/shard_map/ppermute | solution.py:307
  45.3 3.5 %copy-start.8 = (bf16[512,128]{1,0:T(8,128)(2,1)}, bf16[512,128]{1,0:T(8,128)(2,1)S(1)}, u32[]{:S(2)}) copy-start(bf16[512,128]{1,0:T(8,128)(2,1)S(1)} %collective-permute-done.4.refs_5_) | copy-start | bytes 393220
  45.3 2.1 %collective-permute-start.6 = (bf16[512,128]{1,0:T(8,128)(2,1)S(1)}, bf16[512,128]{1,0:T(8,128)(2,1)S(1)}, u32[]{:S(2)}, u32[]{:S(2)}) collective-permute-start(bf16[512,128]{1,0:T(8,128)(2,1)S(1)} %collective-permute-done.5.refs_6_), channel_id=1, source_target_pairs={{0,1},{1,0},{2,3},{3,2},{4,5},{5,4},{6,7},{7,6},{8,9},{9,8},{10,11... | collective-permute-start | bytes 393224 | tf_op jit(solution)/shard_map/ppermute | solution.py:307
  47.4 1.4 %copy-start.9 = (bf16[512,128]{1,0:T(8,128)(2,1)}, bf16[512,128]{1,0:T(8,128)(2,1)S(1)}, u32[]{:S(2)}) copy-start(bf16[512,128]{1,0:T(8,128)(2,1)S(1)} %collective-permute-done.13.refs_14_) | copy-start | bytes 393220
  47.4 1.3 %collective-permute-start.14 = (bf16[512,128]{1,0:T(8,128)(2,1)S(1)}, bf16[512,128]{1,0:T(8,128)(2,1)S(1)}, u32[]{:S(2)}, u32[]{:S(2)}) collective-permute-start(bf16[512,128]{1,0:T(8,128)(2,1)S(1)} %collective-permute-done.13.refs_14_), channel_id=1, source_target_pairs={{0,1},{1,0},{2,3},{3,2},{4,5},{5,4},{6,7},{7,6},{8,9},{9,8},{10,11... | collective-permute-start | bytes 393224 | tf_op jit(solution)/shard_map/ppermute | solution.py:307
  47.4 1.4 %copy-start.10 = (bf16[512,128]{1,0:T(8,128)(2,1)}, bf16[512,128]{1,0:T(8,128)(2,1)S(1)}, u32[]{:S(2)}) copy-start(bf16[512,128]{1,0:T(8,128)(2,1)S(1)} %collective-permute-done.2.refs_3_) | copy-start | bytes 393220
  47.4 1.4 %copy-start.11 = (bf16[512,128]{1,0:T(8,128)(2,1)}, bf16[512,128]{1,0:T(8,128)(2,1)S(1)}, u32[]{:S(2)}) copy-start(bf16[512,128]{1,0:T(8,128)(2,1)S(1)} %collective-permute-done.12.refs_13_) | copy-start | bytes 393220
  47.5 1.4 %copy-start.12 = (bf16[512,128]{1,0:T(8,128)(2,1)}, bf16[512,128]{1,0:T(8,128)(2,1)S(1)}, u32[]{:S(2)}) copy-start(bf16[512,128]{1,0:T(8,128)(2,1)S(1)} %collective-permute-done.10.refs_11_) | copy-start | bytes 393220
  47.5 1.4 %copy-start.13 = (bf16[512,128]{1,0:T(8,128)(2,1)}, bf16[512,128]{1,0:T(8,128)(2,1)S(1)}, u32[]{:S(2)}) copy-start(bf16[512,128]{1,0:T(8,128)(2,1)S(1)} %collective-permute-done.6.refs_7_) | copy-start | bytes 393220
  48.8 0.6 %copy-start.14 = (bf16[512,128]{1,0:T(8,128)(2,1)}, bf16[512,128]{1,0:T(8,128)(2,1)S(1)}, u32[]{:S(2)}) copy-start(bf16[512,128]{1,0:T(8,128)(2,1)S(1)} %collective-permute-done.14.refs_15_) | copy-start | bytes 393220

commit v2 on v1

--- a/solution.py
+++ b/solution.py
@@ -7,6 +7,7 @@
 from jax.experimental import pallas as pl
 from jax.experimental.pallas import tpu as pltpu
 from jax.sharding import PartitionSpec as P
+
 
 HEADS = 16
 HDIM = 128
@@ -161,10 +162,16 @@
 
 
 EDGE_ROWS = 16
+PEER = 1
+CHUNKS = 4
 
 
 def rms_rows(values):
     return values * lax.rsqrt(jnp.mean(values * values, axis=-1, keepdims=True) + epsilon)
+
+
+def on_chip(value):
+    return pltpu.with_memory_space_constraint(value, pltpu.VMEM)
 
 
 def select_matrix(tokens, rows, slot):
@@ -177,39 +184,66 @@
     return jnp.where(pooled, weight, jnp.where(edge, 1.0, 0.0)).astype(jnp.bfloat16)
 
 
-def pool_kernel(query_ref, key_ref, value_ref, query_gain_ref, key_gain_ref, out_ref):
-    tokens, width = query_ref.shape
+def pool_kernel(*refs):
+    sources, gain_sources, out_ref = refs[:3], refs[3:5], refs[5]
+    buffers, gains, source_sems, gain_sems = refs[6:9], refs[9:11], refs[11], refs[12]
+    tokens, columns = sources[0].shape
     rows = tokens // SHORT
-    picked = [
-        jnp.dot(select_matrix(tokens, rows, slot), ref[...], preferred_element_type=jnp.float32)
-        for slot, ref in enumerate((query_ref, key_ref, value_ref))
-    ]
+    width = columns // CHUNKS
+    copies = {}
+    for chunk in range(CHUNKS):
+        part = pl.ds(chunk * width, width)
+        for slot in range(3):
+            copies[chunk, slot] = pltpu.make_async_copy(
+                sources[slot].at[:, part], buffers[slot].at[:, part], source_sems.at[chunk, slot]
+            )
+            copies[chunk, slot].start()
+        if chunk == 0:
+            for slot in range(2):
+                copies[slot] = pltpu.make_async_copy(
+                    gain_sources[slot], gains[slot], gain_sems.at[slot]
+                )
+                copies[slot].start()
+    picks = [select_matrix(tokens, rows, slot) for slot in range(3)]
     first = lax.broadcasted_iota(jnp.int32, (rows, HDIM), 0) == 0
-    gains = (query_gain_ref, key_gain_ref)
-    for head in range(width // HDIM):
-        columns = slice(head * HDIM, (head + 1) * HDIM)
+    for chunk in range(CHUNKS):
+        picked = []
         for slot in range(3):
-            part = picked[slot][:rows, columns]
-            if slot < 2:
-                part = jnp.where(first, part, rms_rows(part) * gains[slot][:, columns])
-            out_ref[head, slot * rows : (slot + 1) * rows, :] = part.astype(jnp.bfloat16)
-        edge = sum(values[rows:, columns] for values in picked)
-        out_ref[head, 3 * rows :, :] = edge.astype(jnp.bfloat16)
-
-
-def pool_inputs(query_src, key_src, value_src, query_gain, key_gain, heads_at_once):
+            copies[chunk, slot].wait()
+            picked.append(
+                jnp.dot(
+                    picks[slot],
+                    buffers[slot][:, chunk * width : (chunk + 1) * width],
+                    preferred_element_type=jnp.float32,
+                )
+            )
+        if chunk == 0:
+            copies[0].wait()
+            copies[1].wait()
+        for index in range(width // HDIM):
+            head = chunk * (width // HDIM) + index
+            inside = slice(index * HDIM, (index + 1) * HDIM)
+            for slot in range(3):
+                part = picked[slot][:rows, inside]
+                if slot < 2:
+                    part = jnp.where(first, part, rms_rows(part) * gains[slot][head : head + 1, :])
+                out_ref[head, slot * rows : (slot + 1) * rows, :] = part.astype(jnp.bfloat16)
+            edge = sum(values[rows:, inside] for values in picked)
+            out_ref[head, 3 * rows :, :] = edge.astype(jnp.bfloat16)
+
+
+def pool_inputs(query_src, key_src, value_src, query_gain, key_gain):
     tokens, columns = query_src.shape
-    width = heads_at_once * HDIM
+    heads = columns // HDIM
     depth = 3 * (tokens // SHORT) + EDGE_ROWS
-    source = pl.BlockSpec((tokens, width), lambda step: (0, step))
-    gain = pl.BlockSpec((1, width), lambda step: (0, step))
     return pl.pallas_call(
         pool_kernel,
-        grid=(columns // width,),
-        in_specs=[source, source, source, gain, gain],
-        out_specs=pl.BlockSpec((heads_at_once, depth, HDIM), lambda step: (step, 0, 0)),
-        out_shape=jax.ShapeDtypeStruct((columns // HDIM, depth, HDIM), jnp.bfloat16),
-    )(query_src, key_src, value_src, query_gain.reshape(1, -1), key_gain.reshape(1, -1))
+        in_specs=[pl.BlockSpec(memory_space=pl.ANY)] * 5,
+        out_shape=pltpu.VMEM((heads, depth, HDIM), jnp.bfloat16),
+        scratch_shapes=[pltpu.VMEM((tokens, columns), jnp.bfloat16)] * 3
+        + [pltpu.VMEM((heads, HDIM), jnp.float32)] * 2
+        + [pltpu.SemaphoreType.DMA((CHUNKS, 3)), pltpu.SemaphoreType.DMA((2,))],
+    )(query_src, key_src, value_src, query_gain.reshape(heads, HDIM), key_gain.reshape(heads, HDIM))
 
 
 def masked_exp(scores, visible):
@@ -270,36 +304,80 @@
     row_total = count * (depth - EDGE_ROWS) // 3
     return pl.pallas_call(
         functools.partial(short_kernel, math.gcd(128, row_total)),
-        out_shape=jax.ShapeDtypeStruct((row_total, HDIM), jnp.bfloat16),
-    )(arrived, query_gain.reshape(-1, HDIM), key_gain.reshape(-1, HDIM))
-
-
-def up_kernel(offsets, up_ref, gain_ref, *refs):
-    unit_refs, out_ref = refs[:-1], refs[-1]
-    tokens = up_ref.shape[0]
+        out_shape=pltpu.VMEM((row_total, HDIM), jnp.bfloat16),
+    )(on_chip(arrived), query_gain.reshape(-1, HDIM), key_gain.reshape(-1, HDIM))
+
+
+def norm_kernel(up_ref, gain_ref, own_ref, send_ref):
+    parity = lax.axis_index("seq") & PEER
+    for slot in range(HEADS // 2):
+        inside = slice(slot * HDIM, (slot + 1) * HDIM)
+        for flip, out_ref in ((0, own_ref), (PEER, send_ref)):
+            head = 2 * slot + (parity ^ flip)
+            columns = pl.ds(pl.multiple_of(head * HDIM, HDIM), HDIM)
+            query = rms_rows(up_ref[:, columns].astype(jnp.float32)) * gain_ref[pl.ds(head, 1), :]
+            out_ref[:, inside] = query.astype(jnp.bfloat16)
+
+
+def norm_up(up_query, up_gain):
+    tokens, columns = up_query.shape
+    return pl.pallas_call(
+        norm_kernel,
+        out_shape=[pltpu.VMEM((tokens, columns // 2), jnp.bfloat16)] * 2,
+    )(up_query, up_gain.reshape(-1, HDIM))
+
+
+def up_kernel(offsets, own_ref, peer_ref, *refs):
+    unit_refs, own_out_ref, send_out_ref = refs[:-2], refs[-2], refs[-1]
+    tokens = own_ref.shape[0]
     row_total = unit_refs[0].shape[0]
     device = lax.axis_index("seq")
-    limit = device * tokens + lax.broadcasted_iota(jnp.int32, (tokens, row_total), 0)
-    visible = SHORT * lax.broadcasted_iota(jnp.int32, (tokens, row_total), 1) <= limit
-    for offset, unit_ref in zip(offsets, unit_refs):
-        head = device ^ offset
-        columns = pl.ds(pl.multiple_of(head * HDIM, HDIM), HDIM)
-        query = rms_rows(up_ref[:, columns].astype(jnp.float32)) * gain_ref[pl.ds(head, 1), :]
+    token = lax.broadcasted_iota(jnp.int32, (2 * tokens, row_total), 0)
+    first = jnp.where(token < tokens, device * tokens, ((device ^ PEER) - 1) * tokens)
+    visible = SHORT * lax.broadcasted_iota(jnp.int32, (2 * tokens, row_total), 1) <= first + token
+    for index, (offset, unit_ref) in enumerate(zip(offsets, unit_refs)):
+        slot = lax.shift_right_logical(device ^ offset, 1)
+        columns = pl.ds(pl.multiple_of(slot * HDIM, HDIM), HDIM)
+        query = jnp.concatenate([own_ref[:, columns], peer_ref[:, columns]], axis=0)
         memory = unit_ref[...]
-        exponent = masked_exp(across(query.astype(jnp.bfloat16), memory), visible)
+        exponent = masked_exp(across(query, memory), visible)
         denominator = jnp.sum(exponent, axis=1, keepdims=True)
         numerator = jnp.dot(
             exponent.astype(jnp.bfloat16), memory, preferred_element_type=jnp.float32
         )
-        out_ref[:, columns] = (numerator / denominator).astype(jnp.bfloat16)
-
-
-def up_attention(up_query, up_gain, units):
-    offsets = tuple(sorted(units))
+        result = (numerator / denominator).astype(jnp.bfloat16)
+        inside = slice(index * HDIM, (index + 1) * HDIM)
+        own_out_ref[:, inside] = result[:tokens]
+        send_out_ref[:, inside] = result[tokens:]
+
+
+def up_attention(own_up, peer_up, units, offsets):
+    tokens = own_up.shape[0]
+    operands = [own_up, peer_up, *[units[offset] for offset in offsets]]
     return pl.pallas_call(
         functools.partial(up_kernel, offsets),
-        out_shape=jax.ShapeDtypeStruct(up_query.shape, jnp.bfloat16),
-    )(up_query, up_gain.reshape(-1, HDIM), *[units[offset] for offset in offsets])
+        out_shape=[pltpu.VMEM((tokens, len(offsets) * HDIM), jnp.bfloat16)] * 2,
+    )(*[on_chip(value) for value in operands])
+
+
+def place_kernel(groups, *refs):
+    piece_refs, out_ref = refs[:-1], refs[-1]
+    device = lax.axis_index("seq")
+    for number, offsets in enumerate(groups):
+        for flip in (0, PEER):
+            piece_ref = piece_refs[2 * number + flip]
+            for index, offset in enumerate(offsets):
+                head = device ^ (offset + flip)
+                columns = pl.ds(pl.multiple_of(head * HDIM, HDIM), HDIM)
+                out_ref[:, columns] = piece_ref[:, index * HDIM : (index + 1) * HDIM]
+
+
+def place(pieces, groups):
+    tokens = pieces[0].shape[0]
+    return pl.pallas_call(
+        functools.partial(place_kernel, groups),
+        out_shape=jax.ShapeDtypeStruct((tokens, HEADS * HDIM), jnp.bfloat16),
+    )(*[on_chip(piece) for piece in pieces])
 
 
 def swapped(value, offset):
@@ -308,14 +386,23 @@
 
 
 def memory_gather(query_src, key_src, value_src, up_query, query_gain, key_gain, up_gain):
-    outgoing = pool_inputs(query_src, key_src, value_src, query_gain, key_gain, HEADS // 4)
+    outgoing = pool_inputs(query_src, key_src, value_src, query_gain, key_gain)
     arrived = lax.all_to_all(outgoing, "seq", split_axis=0, concat_axis=0, tiled=True)
+    own_up, send_up = norm_up(up_query, up_gain)
+    peer_up = swapped(send_up, PEER)
     units = {0: short_attention(arrived, query_gain, key_gain)}
-    offset = HEADS // 2
-    while offset:
-        units.update({held ^ offset: swapped(units[held], offset) for held in list(units)})
-        offset //= 2
-    return up_attention(up_query, up_gain, units)
+    far = HEADS // 2
+    near = tuple(range(2, far, 2))
+    units[far] = swapped(units[0], far)
+    units.update({offset: swapped(units[0], offset) for offset in near})
+    for offset in near:
+        units[far + offset] = swapped(units[far], offset)
+    groups = ((0,), (*near, far), tuple(far + offset for offset in near))
+    pieces = []
+    for offsets in groups:
+        own, send = up_attention(own_up, peer_up, units, offsets)
+        pieces += [own, swapped(send, PEER)]
+    return place(pieces, groups)
 
 
 def local(*arrays):

time: 55.6 us -> 48.6 us (0.87)
  blocking collectives: 20.7 us -> 0 us
  starting transfers between devices: 8.45 us -> 17.7 us
  waiting for transfers between devices: 12.8 us -> 20.4 us
  Pallas kernels: 12.5 us -> 10.2 us
  local copies, waits for them, and re-layouts: 0.58 us -> 0 us
    all_to_all x1 -> x0, blocking collectives: 20.7 us -> none  [memory_gather(): lax.all_to_all(outgoing, 'seq', split_axis=0, concat_axis=0, tiled=True)]
    all_to_all x0 -> x1, waiting for transfers between devices: none -> 11.3 us  [memory_gather(): lax.all_to_all(outgoing, 'seq', split_axis=0, concat_axis=0, tiled=True)]
    all_to_all x0 -> x1, starting transfers between devices: none -> 7.4 us  [memory_gather(): lax.all_to_all(outgoing, 'seq', split_axis=0, concat_axis=0, tiled=True)]
    ppermute x15 -> x11, waiting for transfers between devices: 12.8 us -> 9.08 us  [swapped(): lax.ppermute(value, 'seq', [(source, source ^ offset) for source in range...]
    ppermute x15 -> x11, starting transfers between devices: 8.45 us -> 10.3 us  [swapped(): lax.ppermute(value, 'seq', [(source, source ^ offset) for source in range...]
    pallas_call x2 -> x6, Pallas kernels: 9.83 us -> 8.43 us  [the longest x1 3.6 us: pool_inputs(): pl.pallas_call(pool_kernel, in_specs=[pl.BlockSpec(memory_space=pl.ANY)]...]
    pallas_call x1, Pallas kernels: 2.7 us -> 1.73 us  [short_attention(): pl.pallas_call(functools.partial(short_kernel, math.gcd(128, row_total)),...]
    unnamed x30 -> x0, local copies, waits for them, and re-layouts: 0.58 us -> none
  transfers between devices with their start and end apart: 15 -> 12, of which waited for: 5 -> 6; matrix products, arithmetic and copies ran while one was open for 0% -> 0% of each run, Pallas kernels for 0% -> 12%
where the time goes in v2:
time: 48.6 us; the launch traced here: 48.3 us
  waiting for transfers between devices  20.4 us (42%)
  starting transfers between devices  17.7 us (36%)
  Pallas kernels  10.2 us (21%)
    all_to_all x1, waiting for transfers between devices, memory_gather(): lax.all_to_all(outgoing, 'seq', split_axis=0, concat_axis=0, tiled=True)  11.3 us
    ppermute x11, starting transfers between devices, swapped(): lax.ppermute(value, 'seq', [(source, source ^ offset) for source in range...  10.3 us
    ppermute x11, waiting for transfers between devices, swapped(): lax.ppermute(value, 'seq', [(source, source ^ offset) for source in range...  9.08 us
    all_to_all x1, starting transfers between devices, memory_gather(): lax.all_to_all(outgoing, 'seq', split_axis=0, concat_axis=0, tiled=True)  7.4 us
    pallas_call x1, Pallas kernels, pool_inputs(): pl.pallas_call(pool_kernel, in_specs=[pl.BlockSpec(memory_space=pl.ANY)]...  3.6 us
    pallas_call x3, Pallas kernels, up_attention(): pl.pallas_call(functools.partial(up_kernel, offsets), out_shape=[pltpu.VM...  2.49 us
    pallas_call x1, Pallas kernels, short_attention(): pl.pallas_call(functools.partial(short_kernel, math.gcd(128, row_total)),...  1.73 us
    pallas_call x1, Pallas kernels, norm_up(): pl.pallas_call(norm_kernel, out_shape=[pltpu.VMEM((tokens, columns // 2),...  1.4 us
  transfers between devices with their start and end apart: 12, of which 6 were waited for; matrix products, arithmetic and copies ran while one was open for 0% of the time, Pallas kernels for 12%

profile of v2, /device:TPU:0, one launch (start us, length us, event | category | flops | bytes accessed | tf_op | source)
XLA Modules:
  0.0 48.3 jit_solution(10077543760229575960)
XLA Ops:
  0.0 3.6 %shard_map.74 = bf16[16,112,128]{2,1,0:T(8,128)(2,1)} custom-call(bf16[128,2048]{1,0:T(8,128)(2,1)} %refs_0_.1, bf16[128,2048]{1,0:T(8,128)(2,1)} %refs_1_.1, bf16[128,2048]{1,0:T(8,128)(2,1)} %refs_2_.1, f32[16,128]{1,0:T(8,128)} %bitcast.3, f32[16,128]{1,0:T(8,128)} %bitcast.5), custom_call_target="tpu_custom_call" | custom-call | tf_op jit(solution)/shard_map/pallas_call | solution.py:239
  3.6 7.4 %all-to-all-start = ((bf16[16,112,128]{2,1,0:T(8,128)(2,1)}), bf16[16,112,128]{2,1,0:T(8,128)(2,1)S(1)}, u32[]{:S(2)}, u32[]{:S(2)}) async-start(bf16[16,112,128]{2,1,0:T(8,128)(2,1)} %shard_map.74), calls=%async_computation | async-start | bytes 917504 | tf_op jit(solution)/shard_map/all_to_all | solution.py:390
  11.0 1.4 %shard_map.73 = (bf16[128,1024]{1,0:T(8,128)(2,1)S(1)}, bf16[128,1024]{1,0:T(8,128)(2,1)S(1)}) custom-call(bf16[128,2048]{1,0:T(8,128)(2,1)} %up_ref.1, f32[16,128]{1,0:T(8,128)} %bitcast.7), custom_call_target="tpu_custom_call" | custom-call | tf_op jit(solution)/shard_map/pallas_call | solution.py:324
  12.4 0.5 collective-permute-start
  12.9 11.3 %all-to-all-done.arrived_ref = bf16[16,112,128]{2,1,0:T(8,128)(2,1)S(1)} async-done(((bf16[16,112,128]{2,1,0:T(8,128)(2,1)}), bf16[16,112,128]{2,1,0:T(8,128)(2,1)S(1)}, u32[]{:S(2)}, u32[]{:S(2)}) %all-to-all-start) | async-done | bytes 458784 | tf_op jit(solution)/shard_map/all_to_all | solution.py:390
  24.2 1.7 %shard_map.75.refs_0_ = bf16[512,128]{1,0:T(8,128)(2,1)S(1)} custom-call(bf16[16,112,128]{2,1,0:T(8,128)(2,1)S(1)} %all-to-all-done.arrived_ref, f32[16,128]{1,0:T(8,128)} %bitcast.4, f32[16,128]{1,0:T(8,128)} %bitcast.6), custom_call_target="tpu_custom_call" | custom-call | tf_op jit(solution)/shard_map/pallas_call | solution.py:305
  26.0 2.1 %collective-permute-start.5 = (bf16[512,128]{1,0:T(8,128)(2,1)S(1)}, bf16[512,128]{1,0:T(8,128)(2,1)S(1)}, u32[]{:S(2)}, u32[]{:S(2)}) collective-permute-start(bf16[512,128]{1,0:T(8,128)(2,1)S(1)} %shard_map.75.refs_0_), channel_id=1, source_target_pairs={{0,8},{1,9},{2,10},{3,11},{4,12},{5,13},{6,14},{7,15},{8,0},{9,1},... | collective-permute-start | bytes 393224 | tf_op jit(solution)/shard_map/ppermute | solution.py:385
  28.1 0.0 collective-permute-start.2
  28.1 1.5 %collective-permute-start.3 = (bf16[512,128]{1,0:T(8,128)(2,1)S(1)}, bf16[512,128]{1,0:T(8,128)(2,1)S(1)}, u32[]{:S(2)}, u32[]{:S(2)}) collective-permute-start(bf16[512,128]{1,0:T(8,128)(2,1)S(1)} %shard_map.75.refs_0_), channel_id=1, source_target_pairs={{0,4},{1,5},{2,6},{3,7},{4,0},{5,1},{6,2},{7,3},{8,12},{9,13},{10,... | collective-permute-start | bytes 393224 | tf_op jit(solution)/shard_map/ppermute | solution.py:385
  29.6 2.0 %collective-permute-start.4 = (bf16[512,128]{1,0:T(8,128)(2,1)S(1)}, bf16[512,128]{1,0:T(8,128)(2,1)S(1)}, u32[]{:S(2)}, u32[]{:S(2)}) collective-permute-start(bf16[512,128]{1,0:T(8,128)(2,1)S(1)} %shard_map.75.refs_0_), channel_id=1, source_target_pairs={{0,6},{1,7},{2,4},{3,5},{4,2},{5,3},{6,0},{7,1},{8,14},{9,15},{10,... | collective-permute-start | bytes 393224 | tf_op jit(solution)/shard_map/ppermute | solution.py:385
  31.6 3.8 %collective-permute-done.5.refs_3_ = bf16[512,128]{1,0:T(8,128)(2,1)S(1)} collective-permute-done((bf16[512,128]{1,0:T(8,128)(2,1)S(1)}, bf16[512,128]{1,0:T(8,128)(2,1)S(1)}, u32[]{:S(2)}, u32[]{:S(2)}) %collective-permute-start.5) | collective-permute-done | bytes 131104 | tf_op jit(solution)/shard_map/ppermute | solution.py:385
  35.4 1.1 %collective-permute-start.7 = (bf16[512,128]{1,0:T(8,128)(2,1)S(1)}, bf16[512,128]{1,0:T(8,128)(2,1)S(1)}, u32[]{:S(2)}, u32[]{:S(2)}) collective-permute-start(bf16[512,128]{1,0:T(8,128)(2,1)S(1)} %collective-permute-done.5.refs_3_), channel_id=1, source_target_pairs={{0,2},{1,3},{2,0},{3,1},{4,6},{5,7},{6,4},{7,5},{8,10},{9,11},{10,... | collective-permute-start | bytes 393224 | tf_op jit(solution)/shard_map/ppermute | solution.py:385
  36.5 0.0 collective-permute-done.peer_ref
  36.5 0.0 collective-permute-start.8
  36.5 0.0 collective-permute-done.2.refs_0_
  36.5 2.4 %collective-permute-start.9 = (bf16[512,128]{1,0:T(8,128)(2,1)S(1)}, bf16[512,128]{1,0:T(8,128)(2,1)S(1)}, u32[]{:S(2)}, u32[]{:S(2)}) collective-permute-start(bf16[512,128]{1,0:T(8,128)(2,1)S(1)} %collective-permute-done.5.refs_3_), channel_id=1, source_target_pairs={{0,6},{1,7},{2,4},{3,5},{4,2},{5,3},{6,0},{7,1},{8,14},{9,15},{10,... | collective-permute-start | bytes 393224 | tf_op jit(solution)/shard_map/ppermute | solution.py:385
  38.9 0.0 collective-permute-done.3.refs_1_
  38.9 0.4 collective-permute-done.4.refs_2_
  39.3 1.2 %shard_map.77 = (bf16[128,512]{1,0:T(8,128)(2,1)S(1)}, bf16[128,512]{1,0:T(8,128)(2,1)S(1)}) custom-call(bf16[128,1024]{1,0:T(8,128)(2,1)S(1)} %get-tuple-element.13.own_ref, bf16[128,1024]{1,0:T(8,128)(2,1)S(1)} %collective-permute-done.peer_ref, bf16[512,128]{1,0:T(8,128)(2,1)S(1)} %collective-permute-done.2.refs_0_, ...), custom_call_target="tpu_custom_call" | custom-call | tf_op jit(solution)/shard_map/pallas_call | solution.py:357
  40.5 0.1 collective-permute-start.6
  40.6 2.3 %collective-permute-done.7.refs_0_ = bf16[512,128]{1,0:T(8,128)(2,1)S(1)} collective-permute-done((bf16[512,128]{1,0:T(8,128)(2,1)S(1)}, bf16[512,128]{1,0:T(8,128)(2,1)S(1)}, u32[]{:S(2)}, u32[]{:S(2)}) %collective-permute-start.7) | collective-permute-done | bytes 131104 | tf_op jit(solution)/shard_map/ppermute | solution.py:385
  42.9 0.0 collective-permute-done.8.refs_1_
  42.9 1.7 %collective-permute-done.9.refs_2_ = bf16[512,128]{1,0:T(8,128)(2,1)S(1)} collective-permute-done((bf16[512,128]{1,0:T(8,128)(2,1)S(1)}, bf16[512,128]{1,0:T(8,128)(2,1)S(1)}, u32[]{:S(2)}, u32[]{:S(2)}) %collective-permute-start.9) | collective-permute-done | bytes 131104 | tf_op jit(solution)/shard_map/ppermute | solution.py:385
  44.6 0.9 %shard_map.78 = (bf16[128,384]{1,0:T(8,128)(2,1)S(1)}, bf16[128,384]{1,0:T(8,128)(2,1)S(1)}) custom-call(bf16[128,1024]{1,0:T(8,128)(2,1)S(1)} %get-tuple-element.13.own_ref, bf16[128,1024]{1,0:T(8,128)(2,1)S(1)} %collective-permute-done.peer_ref, bf16[512,128]{1,0:T(8,128)(2,1)S(1)} %collective-permute-done.7.refs_0_, ...), custom_call_target="tpu_custom_call" | custom-call | tf_op jit(solution)/shard_map/pallas_call | solution.py:357
  45.5 0.1 collective-permute-start.10
  45.6 0.4 shard_map.76
  46.0 0.6 %collective-permute-start.1 = (bf16[128,128]{1,0:T(8,128)(2,1)S(1)}, bf16[128,128]{1,0:T(8,128)(2,1)S(1)}, u32[]{:S(2)}, u32[]{:S(2)}) collective-permute-start(bf16[128,128]{1,0:T(8,128)(2,1)S(1)} %get-tuple-element.16), channel_id=1, source_target_pairs={{0,1},{1,0},{2,3},{3,2},{4,5},{5,4},{6,7},{7,6},{8,9},{9,8},{10,11... | collective-permute-start | bytes 98312 | tf_op jit(solution)/shard_map/ppermute | solution.py:385
  46.5 0.9 %collective-permute-done.1.refs_1_ = bf16[128,128]{1,0:T(8,128)(2,1)S(1)} collective-permute-done((bf16[128,128]{1,0:T(8,128)(2,1)S(1)}, bf16[128,128]{1,0:T(8,128)(2,1)S(1)}, u32[]{:S(2)}, u32[]{:S(2)}) %collective-permute-start.1) | collective-permute-done | bytes 32800 | tf_op jit(solution)/shard_map/ppermute | solution.py:385
  47.4 0.0 collective-permute-done.6.refs_3_
  47.4 0.0 collective-permute-done.10.refs_5_
  47.4 0.9 %shard_map.79 = bf16[128,2048]{1,0:T(8,128)(2,1)} custom-call(bf16[128,128]{1,0:T(8,128)(2,1)S(1)} %get-tuple-element.15.refs_0_, bf16[128,128]{1,0:T(8,128)(2,1)S(1)} %collective-permute-done.1.refs_1_, bf16[128,512]{1,0:T(8,128)(2,1)S(1)} %get-tuple-element.17.refs_2_, bf16[128,512]{1,0:T(8,128)(2,1)S(1)} %collective-permute-done.6.refs_3_, ...), custom_call_target="tpu_custom_call" | custom-call | tf_op jit(solution)/shard_map/pallas_call | solution.py:377
Async XLA Ops:
  3.6 20.6 %all-to-all-start = ((bf16[16,112,128]{2,1,0:T(8,128)(2,1)}), bf16[16,112,128]{2,1,0:T(8,128)(2,1)S(1)}, u32[]{:S(2)}, u32[]{:S(2)}) async-start(bf16[16,112,128]{2,1,0:T(8,128)(2,1)} %shard_map.74), calls=%async_computation | async-start | bytes 917504 | tf_op jit(solution)/shard_map/all_to_all | solution.py:390
  12.4 24.1 %collective-permute-start = (bf16[128,1024]{1,0:T(8,128)(2,1)S(1)}, bf16[128,1024]{1,0:T(8,128)(2,1)S(1)}, u32[]{:S(2)}, u32[]{:S(2)}) collective-permute-start(bf16[128,1024]{1,0:T(8,128)(2,1)S(1)} %get-tuple-element.14), channel_id=1, source_target_pairs={{0,1},{1,0},{2,3},{3,2},{4,5},{5,4},{6,7},{7,6},{8,9},{9,8},{10,11... | collective-permute-start | bytes 786440 | tf_op jit(solution)/shard_map/ppermute | solution.py:385
  26.0 9.4 %collective-permute-start.5 = (bf16[512,128]{1,0:T(8,128)(2,1)S(1)}, bf16[512,128]{1,0:T(8,128)(2,1)S(1)}, u32[]{:S(2)}, u32[]{:S(2)}) collective-permute-start(bf16[512,128]{1,0:T(8,128)(2,1)S(1)} %shard_map.75.refs_0_), channel_id=1, source_target_pairs={{0,8},{1,9},{2,10},{3,11},{4,12},{5,13},{6,14},{7,15},{8,0},{9,1},... | collective-permute-start | bytes 393224 | tf_op jit(solution)/shard_map/ppermute | solution.py:385
  28.1 8.4 %collective-permute-start.2 = (bf16[512,128]{1,0:T(8,128)(2,1)S(1)}, bf16[512,128]{1,0:T(8,128)(2,1)S(1)}, u32[]{:S(2)}, u32[]{:S(2)}) collective-permute-start(bf16[512,128]{1,0:T(8,128)(2,1)S(1)} %shard_map.75.refs_0_), channel_id=1, source_target_pairs={{0,2},{1,3},{2,0},{3,1},{4,6},{5,7},{6,4},{7,5},{8,10},{9,11},{10,... | collective-permute-start | bytes 393224 | tf_op jit(solution)/shard_map/ppermute | solution.py:385
  28.1 10.8 %collective-permute-start.3 = (bf16[512,128]{1,0:T(8,128)(2,1)S(1)}, bf16[512,128]{1,0:T(8,128)(2,1)S(1)}, u32[]{:S(2)}, u32[]{:S(2)}) collective-permute-start(bf16[512,128]{1,0:T(8,128)(2,1)S(1)} %shard_map.75.refs_0_), channel_id=1, source_target_pairs={{0,4},{1,5},{2,6},{3,7},{4,0},{5,1},{6,2},{7,3},{8,12},{9,13},{10,... | collective-permute-start | bytes 393224 | tf_op jit(solution)/shard_map/ppermute | solution.py:385
  29.6 9.7 %collective-permute-start.4 = (bf16[512,128]{1,0:T(8,128)(2,1)S(1)}, bf16[512,128]{1,0:T(8,128)(2,1)S(1)}, u32[]{:S(2)}, u32[]{:S(2)}) collective-permute-start(bf16[512,128]{1,0:T(8,128)(2,1)S(1)} %shard_map.75.refs_0_), channel_id=1, source_target_pairs={{0,6},{1,7},{2,4},{3,5},{4,2},{5,3},{6,0},{7,1},{8,14},{9,15},{10,... | collective-permute-start | bytes 393224 | tf_op jit(solution)/shard_map/ppermute | solution.py:385
  35.4 7.5 %collective-permute-start.7 = (bf16[512,128]{1,0:T(8,128)(2,1)S(1)}, bf16[512,128]{1,0:T(8,128)(2,1)S(1)}, u32[]{:S(2)}, u32[]{:S(2)}) collective-permute-start(bf16[512,128]{1,0:T(8,128)(2,1)S(1)} %collective-permute-done.5.refs_3_), channel_id=1, source_target_pairs={{0,2},{1,3},{2,0},{3,1},{4,6},{5,7},{6,4},{7,5},{8,10},{9,11},{10,... | collective-permute-start | bytes 393224 | tf_op jit(solution)/shard_map/ppermute | solution.py:385
  36.5 6.4 %collective-permute-start.8 = (bf16[512,128]{1,0:T(8,128)(2,1)S(1)}, bf16[512,128]{1,0:T(8,128)(2,1)S(1)}, u32[]{:S(2)}, u32[]{:S(2)}) collective-permute-start(bf16[512,128]{1,0:T(8,128)(2,1)S(1)} %collective-permute-done.5.refs_3_), channel_id=1, source_target_pairs={{0,4},{1,5},{2,6},{3,7},{4,0},{5,1},{6,2},{7,3},{8,12},{9,13},{10,... | collective-permute-start | bytes 393224 | tf_op jit(solution)/shard_map/ppermute | solution.py:385
  36.5 8.1 %collective-permute-start.9 = (bf16[512,128]{1,0:T(8,128)(2,1)S(1)}, bf16[512,128]{1,0:T(8,128)(2,1)S(1)}, u32[]{:S(2)}, u32[]{:S(2)}) collective-permute-start(bf16[512,128]{1,0:T(8,128)(2,1)S(1)} %collective-permute-done.5.refs_3_), channel_id=1, source_target_pairs={{0,6},{1,7},{2,4},{3,5},{4,2},{5,3},{6,0},{7,1},{8,14},{9,15},{10,... | collective-permute-start | bytes 393224 | tf_op jit(solution)/shard_map/ppermute | solution.py:385
  40.5 6.9 %collective-permute-start.6 = (bf16[128,512]{1,0:T(8,128)(2,1)S(1)}, bf16[128,512]{1,0:T(8,128)(2,1)S(1)}, u32[]{:S(2)}, u32[]{:S(2)}) collective-permute-start(bf16[128,512]{1,0:T(8,128)(2,1)S(1)} %get-tuple-element.18), channel_id=1, source_target_pairs={{0,1},{1,0},{2,3},{3,2},{4,5},{5,4},{6,7},{7,6},{8,9},{9,8},{10,11... | collective-permute-start | bytes 393224 | tf_op jit(solution)/shard_map/ppermute | solution.py:385
  45.5 1.9 %collective-permute-start.10 = (bf16[128,384]{1,0:T(8,128)(2,1)S(1)}, bf16[128,384]{1,0:T(8,128)(2,1)S(1)}, u32[]{:S(2)}, u32[]{:S(2)}) collective-permute-start(bf16[128,384]{1,0:T(8,128)(2,1)S(1)} %get-tuple-element.20), channel_id=1, source_target_pairs={{0,1},{1,0},{2,3},{3,2},{4,5},{5,4},{6,7},{7,6},{8,9},{9,8},{10,11... | collective-permute-start | bytes 294920 | tf_op jit(solution)/shard_map/ppermute | solution.py:385
  46.0 1.4 %collective-permute-start.1 = (bf16[128,128]{1,0:T(8,128)(2,1)S(1)}, bf16[128,128]{1,0:T(8,128)(2,1)S(1)}, u32[]{:S(2)}, u32[]{:S(2)}) collective-permute-start(bf16[128,128]{1,0:T(8,128)(2,1)S(1)} %get-tuple-element.16), channel_id=1, source_target_pairs={{0,1},{1,0},{2,3},{3,2},{4,5},{5,4},{6,7},{7,6},{8,9},{9,8},{10,11... | collective-permute-start | bytes 98312 | tf_op jit(solution)/shard_map/ppermute | solution.py:385

commit v3 on v2

--- a/solution.py
+++ b/solution.py
@@ -327,57 +327,89 @@
     )(up_query, up_gain.reshape(-1, HDIM))
 
 
-def up_kernel(offsets, own_ref, peer_ref, *refs):
-    unit_refs, own_out_ref, send_out_ref = refs[:-2], refs[-2], refs[-1]
+def pick_kernel(far, nears, own_ref, peer_ref, *out_refs):
     tokens = own_ref.shape[0]
-    row_total = unit_refs[0].shape[0]
     device = lax.axis_index("seq")
-    token = lax.broadcasted_iota(jnp.int32, (2 * tokens, row_total), 0)
-    first = jnp.where(token < tokens, device * tokens, ((device ^ PEER) - 1) * tokens)
-    visible = SHORT * lax.broadcasted_iota(jnp.int32, (2 * tokens, row_total), 1) <= first + token
-    for index, (offset, unit_ref) in enumerate(zip(offsets, unit_refs)):
-        slot = lax.shift_right_logical(device ^ offset, 1)
-        columns = pl.ds(pl.multiple_of(slot * HDIM, HDIM), HDIM)
-        query = jnp.concatenate([own_ref[:, columns], peer_ref[:, columns]], axis=0)
-        memory = unit_ref[...]
-        exponent = masked_exp(across(query, memory), visible)
+    for near, out_ref in zip(nears, out_refs):
+        for kind in range(2):
+            slot = lax.shift_right_logical(device ^ (near + kind * far), 1)
+            columns = pl.ds(pl.multiple_of(slot * HDIM, HDIM), HDIM)
+            out_ref[kind, :tokens, :] = own_ref[:, columns]
+            out_ref[kind, tokens:, :] = peer_ref[:, columns]
+
+
+def pick_up(own_up, peer_up, far, nears):
+    tokens = own_up.shape[0]
+    return pl.pallas_call(
+        functools.partial(pick_kernel, far, nears),
+        out_shape=[pltpu.VMEM((2, 2 * tokens, HDIM), jnp.bfloat16)] * len(nears),
+    )(on_chip(own_up), on_chip(peer_up))
+
+
+def attend_kernel(kind, nears, memory_ref, *refs):
+    query_refs, out_refs = refs[: len(nears)], refs[len(nears) :]
+    double = query_refs[0].shape[1]
+    tokens = double // 2
+    row_total = memory_ref.shape[0]
+    device = lax.axis_index("seq")
+    memory = memory_ref[...]
+    token = lax.broadcasted_iota(jnp.int32, (double, row_total), 0)
+    column = SHORT * lax.broadcasted_iota(jnp.int32, (double, row_total), 1)
+    for near, query_ref, out_ref in zip(nears, query_refs, out_refs):
+        source = device ^ near
+        first = jnp.where(token < tokens, source * tokens, ((source ^ PEER) - 1) * tokens)
+        exponent = masked_exp(across(query_ref[kind], memory), column <= first + token)
         denominator = jnp.sum(exponent, axis=1, keepdims=True)
         numerator = jnp.dot(
             exponent.astype(jnp.bfloat16), memory, preferred_element_type=jnp.float32
         )
-        result = (numerator / denominator).astype(jnp.bfloat16)
-        inside = slice(index * HDIM, (index + 1) * HDIM)
-        own_out_ref[:, inside] = result[:tokens]
-        send_out_ref[:, inside] = result[tokens:]
-
-
-def up_attention(own_up, peer_up, units, offsets):
-    tokens = own_up.shape[0]
-    operands = [own_up, peer_up, *[units[offset] for offset in offsets]]
-    return pl.pallas_call(
-        functools.partial(up_kernel, offsets),
-        out_shape=[pltpu.VMEM((tokens, len(offsets) * HDIM), jnp.bfloat16)] * 2,
+        out_ref[...] = (numerator / denominator).astype(jnp.bfloat16)
+
+
+def attend(kind, nears, memory, queries):
+    double = queries[nears[0]].shape[1]
+    operands = [memory, *[queries[near] for near in nears]]
+    results = pl.pallas_call(
+        functools.partial(attend_kernel, kind, nears),
+        out_shape=[pltpu.VMEM((double, HDIM), jnp.bfloat16)] * len(nears),
     )(*[on_chip(value) for value in operands])
-
-
-def place_kernel(groups, *refs):
+    return dict(zip(nears, results))
+
+
+def pack_kernel(*refs):
     piece_refs, out_ref = refs[:-1], refs[-1]
+    tokens = out_ref.shape[0]
+    for index, piece_ref in enumerate(piece_refs):
+        out_ref[:, index * HDIM : (index + 1) * HDIM] = piece_ref[tokens:, :]
+
+
+def pack(pieces):
+    tokens = pieces[0].shape[0] // 2
+    return pl.pallas_call(
+        pack_kernel,
+        out_shape=pltpu.VMEM((tokens, len(pieces) * HDIM), jnp.bfloat16),
+    )(*[on_chip(piece) for piece in pieces])
+
+
+def place_kernel(offsets, *refs):
+    piece_refs, peer_ref, out_ref = refs[:-2], refs[-2], refs[-1]
+    tokens = out_ref.shape[0]
     device = lax.axis_index("seq")
-    for number, offsets in enumerate(groups):
+    for index, (offset, piece_ref) in enumerate(zip(offsets, piece_refs)):
         for flip in (0, PEER):
-            piece_ref = piece_refs[2 * number + flip]
-            for index, offset in enumerate(offsets):
-                head = device ^ (offset + flip)
-                columns = pl.ds(pl.multiple_of(head * HDIM, HDIM), HDIM)
-                out_ref[:, columns] = piece_ref[:, index * HDIM : (index + 1) * HDIM]
-
-
-def place(pieces, groups):
-    tokens = pieces[0].shape[0]
-    return pl.pallas_call(
-        functools.partial(place_kernel, groups),
-        out_shape=jax.ShapeDtypeStruct((tokens, HEADS * HDIM), jnp.bfloat16),
-    )(*[on_chip(piece) for piece in pieces])
+            head = device ^ (offset + flip)
+            columns = pl.ds(pl.multiple_of(head * HDIM, HDIM), HDIM)
+            if flip:
+                out_ref[:, columns] = peer_ref[:, index * HDIM : (index + 1) * HDIM]
+            else:
+                out_ref[:, columns] = piece_ref[:tokens, :]
+
+
+def place(offsets, pieces, peer):
+    return pl.pallas_call(
+        functools.partial(place_kernel, offsets),
+        out_shape=jax.ShapeDtypeStruct((peer.shape[0], HEADS * HDIM), jnp.bfloat16),
+    )(*[on_chip(piece) for piece in pieces], on_chip(peer))
 
 
 def swapped(value, offset):
@@ -385,29 +417,32 @@
     return lax.ppermute(value, "seq", [(source, source ^ offset) for source in range(count)])
 
 
-def memory_gather(query_src, key_src, value_src, up_query, query_gain, key_gain, up_gain):
+def half_exchange(query_src, key_src, value_src, up_query, query_gain, key_gain, up_gain):
+    far = HEADS // 2
+    nears = tuple(range(0, far, 2))
     outgoing = pool_inputs(query_src, key_src, value_src, query_gain, key_gain)
     arrived = lax.all_to_all(outgoing, "seq", split_axis=0, concat_axis=0, tiled=True)
     own_up, send_up = norm_up(up_query, up_gain)
     peer_up = swapped(send_up, PEER)
-    units = {0: short_attention(arrived, query_gain, key_gain)}
-    far = HEADS // 2
-    near = tuple(range(2, far, 2))
-    units[far] = swapped(units[0], far)
-    units.update({offset: swapped(units[0], offset) for offset in near})
-    for offset in near:
-        units[far + offset] = swapped(units[far], offset)
-    groups = ((0,), (*near, far), tuple(far + offset for offset in near))
-    pieces = []
-    for offsets in groups:
-        own, send = up_attention(own_up, peer_up, units, offsets)
-        pieces += [own, swapped(send, PEER)]
-    return place(pieces, groups)
+    queries = dict(zip(nears, pick_up(own_up, peer_up, far, nears)))
+    for near in nears[1:]:
+        queries[near] = swapped(queries[near], near)
+    memory = short_attention(arrived, query_gain, key_gain)
+    far_memory = swapped(memory, far)
+    offsets, pieces = [], []
+    for kind, held in enumerate((memory, far_memory)):
+        results = attend(kind, nears, held, queries)
+        for near in nears:
+            pieces.append(swapped(results[near], near) if near else results[near])
+            offsets.append(near + kind * far)
+    packed = pack(pieces)
+    peer = swapped(packed, PEER)
+    return place(tuple(offsets), pieces, peer)
 
 
 def local(*arrays):
     whole = lax.axis_size("seq") == HEADS and HEADS & (HEADS - 1) == 0
-    return memory_gather(*arrays) if whole else head_exchange(*arrays)
+    return half_exchange(*arrays) if whole else head_exchange(*arrays)
 
 
 def solution(mesh):

time: 48.6 us -> 46 us (0.947)
  waiting for transfers between devices: 20.4 us -> 15.3 us
  starting transfers between devices: 17.7 us -> 20.2 us
    all_to_all x1, waiting for transfers between devices: 11.3 us -> 7.05 us  [half_exchange(): lax.all_to_all(outgoing, 'seq', split_axis=0, concat_axis=0, tiled=True)]
    ppermute x11 -> x12, starting transfers between devices: 10.3 us -> 12.8 us  [swapped(): lax.ppermute(value, 'seq', [(source, source ^ offset) for source in range...]
    ppermute x11 -> x12, waiting for transfers between devices: 9.08 us -> 8.25 us  [swapped(): lax.ppermute(value, 'seq', [(source, source ^ offset) for source in range...]
    pallas_call x4 -> x5, Pallas kernels: 3.42 us -> 3.4 us  [the longest x2 2.27 us: attend(): pl.pallas_call(functools.partial(attend_kernel, kind, nears), out_shape=[...]
  transfers between devices with their start and end apart: 12 -> 13, of which waited for: 6 -> 7; matrix products, arithmetic and copies ran while one was open for 0% -> 0% of each run, Pallas kernels for 12% -> 12%
where the time goes in v3:
time: 46 us; the launch traced here: 45.7 us
  starting transfers between devices  20.2 us (44%)
  waiting for transfers between devices  15.3 us (33%)
  Pallas kernels  10.1 us (22%)
    ppermute x12, starting transfers between devices, swapped(): lax.ppermute(value, 'seq', [(source, source ^ offset) for source in range...  12.8 us
    ppermute x12, waiting for transfers between devices, swapped(): lax.ppermute(value, 'seq', [(source, source ^ offset) for source in range...  8.25 us
    all_to_all x1, starting transfers between devices, half_exchange(): lax.all_to_all(outgoing, 'seq', split_axis=0, concat_axis=0, tiled=True)  7.4 us
    all_to_all x1, waiting for transfers between devices, half_exchange(): lax.all_to_all(outgoing, 'seq', split_axis=0, concat_axis=0, tiled=True)  7.05 us
    pallas_call x1, Pallas kernels, pool_inputs(): pl.pallas_call(pool_kernel, in_specs=[pl.BlockSpec(memory_space=pl.ANY)]...  3.6 us
    pallas_call x2, Pallas kernels, attend(): pl.pallas_call(functools.partial(attend_kernel, kind, nears), out_shape=[...  2.27 us
    pallas_call x1, Pallas kernels, short_attention(): pl.pallas_call(functools.partial(short_kernel, math.gcd(128, row_total)),...  1.73 us
    pallas_call x1, Pallas kernels, norm_up(): pl.pallas_call(norm_kernel, out_shape=[pltpu.VMEM((tokens, columns // 2),...  1.4 us
  transfers between devices with their start and end apart: 13, of which 7 were waited for; matrix products, arithmetic and copies ran while one was open for 0% of the time, Pallas kernels for 12%

profile of v3, /device:TPU:0, one launch (start us, length us, event | category | flops | bytes accessed | tf_op | source)
XLA Modules:
  0.0 45.7 jit_solution(13115779434907966448)
XLA Ops:
  0.0 3.6 %shard_map.73 = bf16[16,112,128]{2,1,0:T(8,128)(2,1)} custom-call(bf16[128,2048]{1,0:T(8,128)(2,1)} %refs_0_.1, bf16[128,2048]{1,0:T(8,128)(2,1)} %refs_1_.1, bf16[128,2048]{1,0:T(8,128)(2,1)} %refs_2_.1, f32[16,128]{1,0:T(8,128)} %bitcast.3, f32[16,128]{1,0:T(8,128)} %bitcast.5), custom_call_target="tpu_custom_call" | custom-call | tf_op jit(solution)/shard_map/pallas_call | solution.py:239
  3.6 7.4 %all-to-all-start = ((bf16[16,112,128]{2,1,0:T(8,128)(2,1)}), bf16[16,112,128]{2,1,0:T(8,128)(2,1)S(1)}, u32[]{:S(2)}, u32[]{:S(2)}) async-start(bf16[16,112,128]{2,1,0:T(8,128)(2,1)} %shard_map.73), calls=%async_computation | async-start | bytes 917504 | tf_op jit(solution)/shard_map/all_to_all | solution.py:424
  11.0 1.4 %shard_map.75 = (bf16[128,1024]{1,0:T(8,128)(2,1)S(1)}, bf16[128,1024]{1,0:T(8,128)(2,1)S(1)}) custom-call(bf16[128,2048]{1,0:T(8,128)(2,1)} %up_ref.1, f32[16,128]{1,0:T(8,128)} %bitcast.7), custom_call_target="tpu_custom_call" | custom-call | tf_op jit(solution)/shard_map/pallas_call | solution.py:324
  12.4 0.5 %collective-permute-start = (bf16[128,1024]{1,0:T(8,128)(2,1)S(1)}, bf16[128,1024]{1,0:T(8,128)(2,1)S(1)}, u32[]{:S(2)}, u32[]{:S(2)}) collective-permute-start(bf16[128,1024]{1,0:T(8,128)(2,1)S(1)} %get-tuple-element.20), channel_id=1, source_target_pairs={{0,1},{1,0},{2,3},{3,2},{4,5},{5,4},{6,7},{7,6},{8,9},{9,8},{10,11... | collective-permute-start | bytes 786440 | tf_op jit(solution)/shard_map/ppermute | solution.py:417
  12.9 1.2 %collective-permute-done.peer_ref = bf16[128,1024]{1,0:T(8,128)(2,1)S(1)} collective-permute-done((bf16[128,1024]{1,0:T(8,128)(2,1)S(1)}, bf16[128,1024]{1,0:T(8,128)(2,1)S(1)}, u32[]{:S(2)}, u32[]{:S(2)}) %collective-permute-start) | collective-permute-done | bytes 262176 | tf_op jit(solution)/shard_map/ppermute | solution.py:417
  14.1 0.1 shard_map.76
  14.2 2.0 %collective-permute-start.1 = (bf16[2,256,128]{2,1,0:T(8,128)(2,1)S(1)}, bf16[2,256,128]{2,1,0:T(8,128)(2,1)S(1)}, u32[]{:S(2)}, u32[]{:S(2)}) collective-permute-start(bf16[2,256,128]{2,1,0:T(8,128)(2,1)S(1)} %get-tuple-element.22), channel_id=1, source_target_pairs={{0,2},{1,3},{2,0},{3,1},{4,6},{5,7},{6,4},{7,5},{8,10},{9,11},{10,... | collective-permute-start | bytes 393224 | tf_op jit(solution)/shard_map/ppermute | solution.py:417
  16.2 1.5 %collective-permute-start.2 = (bf16[2,256,128]{2,1,0:T(8,128)(2,1)S(1)}, bf16[2,256,128]{2,1,0:T(8,128)(2,1)S(1)}, u32[]{:S(2)}, u32[]{:S(2)}) collective-permute-start(bf16[2,256,128]{2,1,0:T(8,128)(2,1)S(1)} %get-tuple-element.23), channel_id=1, source_target_pairs={{0,4},{1,5},{2,6},{3,7},{4,0},{5,1},{6,2},{7,3},{8,12},{9,13},{10,... | collective-permute-start | bytes 393224 | tf_op jit(solution)/shard_map/ppermute | solution.py:417
  17.6 0.1 collective-permute-start.3
  17.8 7.1 %all-to-all-done.arrived_ref = bf16[16,112,128]{2,1,0:T(8,128)(2,1)S(1)} async-done(((bf16[16,112,128]{2,1,0:T(8,128)(2,1)}), bf16[16,112,128]{2,1,0:T(8,128)(2,1)S(1)}, u32[]{:S(2)}, u32[]{:S(2)}) %all-to-all-start) | async-done | bytes 458784 | tf_op jit(solution)/shard_map/all_to_all | solution.py:424
  24.8 1.7 %shard_map.74.memory_ref = bf16[512,128]{1,0:T(8,128)(2,1)S(1)} custom-call(bf16[16,112,128]{2,1,0:T(8,128)(2,1)S(1)} %all-to-all-done.arrived_ref, f32[16,128]{1,0:T(8,128)} %bitcast.4, f32[16,128]{1,0:T(8,128)} %bitcast.6), custom_call_target="tpu_custom_call" | custom-call | tf_op jit(solution)/shard_map/pallas_call | solution.py:305
  26.5 1.6 %collective-permute-start.7 = (bf16[512,128]{1,0:T(8,128)(2,1)S(1)}, bf16[512,128]{1,0:T(8,128)(2,1)S(1)}, u32[]{:S(2)}, u32[]{:S(2)}) collective-permute-start(bf16[512,128]{1,0:T(8,128)(2,1)S(1)} %shard_map.74.memory_ref), channel_id=1, source_target_pairs={{0,8},{1,9},{2,10},{3,11},{4,12},{5,13},{6,14},{7,15},{8,0},{9,1},... | collective-permute-start | bytes 393224 | tf_op jit(solution)/shard_map/ppermute | solution.py:417
  28.1 0.0 collective-permute-done.1.refs_1_
  28.1 0.0 collective-permute-done.2.refs_2_
  28.1 0.0 collective-permute-done.3.refs_3_
  28.1 1.1 %shard_map.77 = (bf16[256,128]{1,0:T(8,128)(2,1)S(1)}, bf16[256,128]{1,0:T(8,128)(2,1)S(1)}, bf16[256,128]{1,0:T(8,128)(2,1)S(1)}, bf16[256,128]{1,0:T(8,128)(2,1)S(1)}) custom-call(bf16[512,128]{1,0:T(8,128)(2,1)S(1)} %shard_map.74.memory_ref, bf16[2,256,128]{2,1,0:T(8,128)(2,1)S(1)} %get-tuple-element.21.refs_0_, ...), custom_call_target="tpu_custom_call" | custom-call | tf_op jit(solution)/shard_map/pallas_call | solution.py:372
  29.3 0.5 %collective-permute-start.4 = (bf16[256,128]{1,0:T(8,128)(2,1)S(1)}, bf16[256,128]{1,0:T(8,128)(2,1)S(1)}, u32[]{:S(2)}, u32[]{:S(2)}) collective-permute-start(bf16[256,128]{1,0:T(8,128)(2,1)S(1)} %get-tuple-element.26), channel_id=1, source_target_pairs={{0,2},{1,3},{2,0},{3,1},{4,6},{5,7},{6,4},{7,5},{8,10},{9,11},{10,... | collective-permute-start | bytes 196616 | tf_op jit(solution)/shard_map/ppermute | solution.py:417
  29.8 1.0 %collective-permute-start.5 = (bf16[256,128]{1,0:T(8,128)(2,1)S(1)}, bf16[256,128]{1,0:T(8,128)(2,1)S(1)}, u32[]{:S(2)}, u32[]{:S(2)}) collective-permute-start(bf16[256,128]{1,0:T(8,128)(2,1)S(1)} %get-tuple-element.27), channel_id=1, source_target_pairs={{0,4},{1,5},{2,6},{3,7},{4,0},{5,1},{6,2},{7,3},{8,12},{9,13},{10,... | collective-permute-start | bytes 196616 | tf_op jit(solution)/shard_map/ppermute | solution.py:417
  30.8 2.0 %collective-permute-start.6 = (bf16[256,128]{1,0:T(8,128)(2,1)S(1)}, bf16[256,128]{1,0:T(8,128)(2,1)S(1)}, u32[]{:S(2)}, u32[]{:S(2)}) collective-permute-start(bf16[256,128]{1,0:T(8,128)(2,1)S(1)} %get-tuple-element.28), channel_id=1, source_target_pairs={{0,6},{1,7},{2,4},{3,5},{4,2},{5,3},{6,0},{7,1},{8,14},{9,15},{10,... | collective-permute-start | bytes 196616 | tf_op jit(solution)/shard_map/ppermute | solution.py:417
  32.8 2.2 %collective-permute-done.7.memory_ref = bf16[512,128]{1,0:T(8,128)(2,1)S(1)} collective-permute-done((bf16[512,128]{1,0:T(8,128)(2,1)S(1)}, bf16[512,128]{1,0:T(8,128)(2,1)S(1)}, u32[]{:S(2)}, u32[]{:S(2)}) %collective-permute-start.7) | collective-permute-done | bytes 131104 | tf_op jit(solution)/shard_map/ppermute | solution.py:417
  35.0 1.1 %shard_map.78 = (bf16[256,128]{1,0:T(8,128)(2,1)S(1)}, bf16[256,128]{1,0:T(8,128)(2,1)S(1)}, bf16[256,128]{1,0:T(8,128)(2,1)S(1)}, bf16[256,128]{1,0:T(8,128)(2,1)S(1)}) custom-call(bf16[512,128]{1,0:T(8,128)(2,1)S(1)} %collective-permute-done.7.memory_ref, bf16[2,256,128]{2,1,0:T(8,128)(2,1)S(1)} %get-tuple-element.21.refs_0_, ...), custom_call_target="tpu_custom_call" | custom-call | tf_op jit(solution)/shard_map/pallas_call | solution.py:372
  36.1 1.5 %collective-permute-start.8 = (bf16[256,128]{1,0:T(8,128)(2,1)S(1)}, bf16[256,128]{1,0:T(8,128)(2,1)S(1)}, u32[]{:S(2)}, u32[]{:S(2)}) collective-permute-start(bf16[256,128]{1,0:T(8,128)(2,1)S(1)} %get-tuple-element.30), channel_id=1, source_target_pairs={{0,2},{1,3},{2,0},{3,1},{4,6},{5,7},{6,4},{7,5},{8,10},{9,11},{10,... | collective-permute-start | bytes 196616 | tf_op jit(solution)/shard_map/ppermute | solution.py:417
  37.7 0.0 collective-permute-start.9
  37.7 0.0 collective-permute-done.4.refs_1_
  37.7 2.0 %collective-permute-start.10 = (bf16[256,128]{1,0:T(8,128)(2,1)S(1)}, bf16[256,128]{1,0:T(8,128)(2,1)S(1)}, u32[]{:S(2)}, u32[]{:S(2)}) collective-permute-start(bf16[256,128]{1,0:T(8,128)(2,1)S(1)} %get-tuple-element.32), channel_id=1, source_target_pairs={{0,6},{1,7},{2,4},{3,5},{4,2},{5,3},{6,0},{7,1},{8,14},{9,15},{10,... | collective-permute-start | bytes 196616 | tf_op jit(solution)/shard_map/ppermute | solution.py:417
  39.7 0.0 collective-permute-done.5.refs_2_
  39.7 0.0 collective-permute-done.6.refs_3_
  39.7 0.8 %collective-permute-done.8.refs_5_ = bf16[256,128]{1,0:T(8,128)(2,1)S(1)} collective-permute-done((bf16[256,128]{1,0:T(8,128)(2,1)S(1)}, bf16[256,128]{1,0:T(8,128)(2,1)S(1)}, u32[]{:S(2)}, u32[]{:S(2)}) %collective-permute-start.8) | collective-permute-done | bytes 65568 | tf_op jit(solution)/shard_map/ppermute | solution.py:417
  40.5 1.7 %collective-permute-done.9.refs_6_ = bf16[256,128]{1,0:T(8,128)(2,1)S(1)} collective-permute-done((bf16[256,128]{1,0:T(8,128)(2,1)S(1)}, bf16[256,128]{1,0:T(8,128)(2,1)S(1)}, u32[]{:S(2)}, u32[]{:S(2)}) %collective-permute-start.9) | collective-permute-done | bytes 65568 | tf_op jit(solution)/shard_map/ppermute | solution.py:417
  42.2 0.9 %collective-permute-done.10.refs_7_ = bf16[256,128]{1,0:T(8,128)(2,1)S(1)} collective-permute-done((bf16[256,128]{1,0:T(8,128)(2,1)S(1)}, bf16[256,128]{1,0:T(8,128)(2,1)S(1)}, u32[]{:S(2)}, u32[]{:S(2)}) %collective-permute-start.10) | collective-permute-done | bytes 65568 | tf_op jit(solution)/shard_map/ppermute | solution.py:417
  43.1 0.1 shard_map.79
  43.1 0.1 collective-permute-start.11
  43.2 1.5 %collective-permute-done.11.refs_8_ = bf16[128,1024]{1,0:T(8,128)(2,1)S(1)} collective-permute-done((bf16[128,1024]{1,0:T(8,128)(2,1)S(1)}, bf16[128,1024]{1,0:T(8,128)(2,1)S(1)}, u32[]{:S(2)}, u32[]{:S(2)}) %collective-permute-start.11) | collective-permute-done | bytes 262176 | tf_op jit(solution)/shard_map/ppermute | solution.py:417
  44.7 0.9 %shard_map.80 = bf16[128,2048]{1,0:T(8,128)(2,1)} custom-call(bf16[256,128]{1,0:T(8,128)(2,1)S(1)} %get-tuple-element.25.refs_0_, bf16[256,128]{1,0:T(8,128)(2,1)S(1)} %collective-permute-done.4.refs_1_, bf16[256,128]{1,0:T(8,128)(2,1)S(1)} %collective-permute-done.5.refs_2_, bf16[256,128]{1,0:T(8,128)(2,1)S(1)} %collective-permute-done.6.refs_3_, ...), custom_call_target="tpu_custom_call" | custom-call | tf_op jit(solution)/shard_map/pallas_call | solution.py:409
Async XLA Ops:
  3.6 21.2 %all-to-all-start = ((bf16[16,112,128]{2,1,0:T(8,128)(2,1)}), bf16[16,112,128]{2,1,0:T(8,128)(2,1)S(1)}, u32[]{:S(2)}, u32[]{:S(2)}) async-start(bf16[16,112,128]{2,1,0:T(8,128)(2,1)} %shard_map.73), calls=%async_computation | async-start | bytes 917504 | tf_op jit(solution)/shard_map/all_to_all | solution.py:424
  12.4 1.6 %collective-permute-start = (bf16[128,1024]{1,0:T(8,128)(2,1)S(1)}, bf16[128,1024]{1,0:T(8,128)(2,1)S(1)}, u32[]{:S(2)}, u32[]{:S(2)}) collective-permute-start(bf16[128,1024]{1,0:T(8,128)(2,1)S(1)} %get-tuple-element.20), channel_id=1, source_target_pairs={{0,1},{1,0},{2,3},{3,2},{4,5},{5,4},{6,7},{7,6},{8,9},{9,8},{10,11... | collective-permute-start | bytes 786440 | tf_op jit(solution)/shard_map/ppermute | solution.py:417
  14.2 13.9 %collective-permute-start.1 = (bf16[2,256,128]{2,1,0:T(8,128)(2,1)S(1)}, bf16[2,256,128]{2,1,0:T(8,128)(2,1)S(1)}, u32[]{:S(2)}, u32[]{:S(2)}) collective-permute-start(bf16[2,256,128]{2,1,0:T(8,128)(2,1)S(1)} %get-tuple-element.22), channel_id=1, source_target_pairs={{0,2},{1,3},{2,0},{3,1},{4,6},{5,7},{6,4},{7,5},{8,10},{9,11},{10,... | collective-permute-start | bytes 393224 | tf_op jit(solution)/shard_map/ppermute | solution.py:417
  16.2 12.0 %collective-permute-start.2 = (bf16[2,256,128]{2,1,0:T(8,128)(2,1)S(1)}, bf16[2,256,128]{2,1,0:T(8,128)(2,1)S(1)}, u32[]{:S(2)}, u32[]{:S(2)}) collective-permute-start(bf16[2,256,128]{2,1,0:T(8,128)(2,1)S(1)} %get-tuple-element.23), channel_id=1, source_target_pairs={{0,4},{1,5},{2,6},{3,7},{4,0},{5,1},{6,2},{7,3},{8,12},{9,13},{10,... | collective-permute-start | bytes 393224 | tf_op jit(solution)/shard_map/ppermute | solution.py:417
  17.6 10.5 %collective-permute-start.3 = (bf16[2,256,128]{2,1,0:T(8,128)(2,1)S(1)}, bf16[2,256,128]{2,1,0:T(8,128)(2,1)S(1)}, u32[]{:S(2)}, u32[]{:S(2)}) collective-permute-start(bf16[2,256,128]{2,1,0:T(8,128)(2,1)S(1)} %get-tuple-element.24), channel_id=1, source_target_pairs={{0,6},{1,7},{2,4},{3,5},{4,2},{5,3},{6,0},{7,1},{8,14},{9,15},{10,... | collective-permute-start | bytes 393224 | tf_op jit(solution)/shard_map/ppermute | solution.py:417
  26.5 8.5 %collective-permute-start.7 = (bf16[512,128]{1,0:T(8,128)(2,1)S(1)}, bf16[512,128]{1,0:T(8,128)(2,1)S(1)}, u32[]{:S(2)}, u32[]{:S(2)}) collective-permute-start(bf16[512,128]{1,0:T(8,128)(2,1)S(1)} %shard_map.74.memory_ref), channel_id=1, source_target_pairs={{0,8},{1,9},{2,10},{3,11},{4,12},{5,13},{6,14},{7,15},{8,0},{9,1},... | collective-permute-start | bytes 393224 | tf_op jit(solution)/shard_map/ppermute | solution.py:417
  29.3 8.4 %collective-permute-start.4 = (bf16[256,128]{1,0:T(8,128)(2,1)S(1)}, bf16[256,128]{1,0:T(8,128)(2,1)S(1)}, u32[]{:S(2)}, u32[]{:S(2)}) collective-permute-start(bf16[256,128]{1,0:T(8,128)(2,1)S(1)} %get-tuple-element.26), channel_id=1, source_target_pairs={{0,2},{1,3},{2,0},{3,1},{4,6},{5,7},{6,4},{7,5},{8,10},{9,11},{10,... | collective-permute-start | bytes 196616 | tf_op jit(solution)/shard_map/ppermute | solution.py:417
  29.8 9.9 %collective-permute-start.5 = (bf16[256,128]{1,0:T(8,128)(2,1)S(1)}, bf16[256,128]{1,0:T(8,128)(2,1)S(1)}, u32[]{:S(2)}, u32[]{:S(2)}) collective-permute-start(bf16[256,128]{1,0:T(8,128)(2,1)S(1)} %get-tuple-element.27), channel_id=1, source_target_pairs={{0,4},{1,5},{2,6},{3,7},{4,0},{5,1},{6,2},{7,3},{8,12},{9,13},{10,... | collective-permute-start | bytes 196616 | tf_op jit(solution)/shard_map/ppermute | solution.py:417
  30.8 8.9 %collective-permute-start.6 = (bf16[256,128]{1,0:T(8,128)(2,1)S(1)}, bf16[256,128]{1,0:T(8,128)(2,1)S(1)}, u32[]{:S(2)}, u32[]{:S(2)}) collective-permute-start(bf16[256,128]{1,0:T(8,128)(2,1)S(1)} %get-tuple-element.28), channel_id=1, source_target_pairs={{0,6},{1,7},{2,4},{3,5},{4,2},{5,3},{6,0},{7,1},{8,14},{9,15},{10,... | collective-permute-start | bytes 196616 | tf_op jit(solution)/shard_map/ppermute | solution.py:417
  36.1 4.3 %collective-permute-start.8 = (bf16[256,128]{1,0:T(8,128)(2,1)S(1)}, bf16[256,128]{1,0:T(8,128)(2,1)S(1)}, u32[]{:S(2)}, u32[]{:S(2)}) collective-permute-start(bf16[256,128]{1,0:T(8,128)(2,1)S(1)} %get-tuple-element.30), channel_id=1, source_target_pairs={{0,2},{1,3},{2,0},{3,1},{4,6},{5,7},{6,4},{7,5},{8,10},{9,11},{10,... | collective-permute-start | bytes 196616 | tf_op jit(solution)/shard_map/ppermute | solution.py:417
  37.7 4.5 %collective-permute-start.9 = (bf16[256,128]{1,0:T(8,128)(2,1)S(1)}, bf16[256,128]{1,0:T(8,128)(2,1)S(1)}, u32[]{:S(2)}, u32[]{:S(2)}) collective-permute-start(bf16[256,128]{1,0:T(8,128)(2,1)S(1)} %get-tuple-element.31), channel_id=1, source_target_pairs={{0,4},{1,5},{2,6},{3,7},{4,0},{5,1},{6,2},{7,3},{8,12},{9,13},{10,... | collective-permute-start | bytes 196616 | tf_op jit(solution)/shard_map/ppermute | solution.py:417
  37.7 5.4 %collective-permute-start.10 = (bf16[256,128]{1,0:T(8,128)(2,1)S(1)}, bf16[256,128]{1,0:T(8,128)(2,1)S(1)}, u32[]{:S(2)}, u32[]{:S(2)}) collective-permute-start(bf16[256,128]{1,0:T(8,128)(2,1)S(1)} %get-tuple-element.32), channel_id=1, source_target_pairs={{0,6},{1,7},{2,4},{3,5},{4,2},{5,3},{6,0},{7,1},{8,14},{9,15},{10,... | collective-permute-start | bytes 196616 | tf_op jit(solution)/shard_map/ppermute | solution.py:417
  43.1 1.6 %collective-permute-start.11 = (bf16[128,1024]{1,0:T(8,128)(2,1)S(1)}, bf16[128,1024]{1,0:T(8,128)(2,1)S(1)}, u32[]{:S(2)}, u32[]{:S(2)}) collective-permute-start(bf16[128,1024]{1,0:T(8,128)(2,1)S(1)} %shard_map.79), channel_id=1, source_target_pairs={{0,1},{1,0},{2,3},{3,2},{4,5},{5,4},{6,7},{7,6},{8,9},{9,8},{10,11... | collective-permute-start | bytes 786440 | tf_op jit(solution)/shard_map/ppermute | solution.py:417

commit v4 on v0

--- a/solution.py
+++ b/solution.py
@@ -1,9 +1,13 @@
+import functools
 import math
 
 import jax
 import jax.numpy as jnp
 from jax import lax
+from jax.experimental import pallas as pl
+from jax.experimental.pallas import tpu as pltpu
 from jax.sharding import PartitionSpec as P
+
 
 HEADS = 16
 HDIM = 128
@@ -92,7 +96,7 @@
     return jnp.transpose(parted, (2, 0, 1, 3)).reshape(device_count, piece, HDIM)
 
 
-def local(query_src, key_src, value_src, up_query, query_gain, key_gain, up_gain):
+def head_exchange(query_src, key_src, value_src, up_query, query_gain, key_gain, up_gain):
     device_count = lax.axis_size("seq")
     device_index = lax.axis_index("seq")
     block_count = device_count // HEADS
@@ -157,6 +161,263 @@
     return jnp.transpose(output_heads, (1, 0, 2)).reshape(token_count, HEADS * HDIM)
 
 
+EDGE_ROWS = 16
+PEER = 1
+
+
+def rms_rows(values):
+    return values * lax.rsqrt(jnp.mean(values * values, axis=-1, keepdims=True) + epsilon)
+
+
+def on_chip(value):
+    return pltpu.with_memory_space_constraint(value, pltpu.VMEM)
+
+
+def select_matrix(tokens, rows, slot):
+    row = lax.broadcasted_iota(jnp.int32, (rows + EDGE_ROWS, tokens), 0)
+    col = lax.broadcasted_iota(jnp.int32, (rows + EDGE_ROWS, tokens), 1)
+    pooled = (row < rows) & (col <= SHORT * row) & (col >= SHORT * row - SHIFT)
+    weight = jnp.where(row == 0, 1.0, 1.0 / SHORT)
+    edge = (row >= rows + slot * SHIFT) & (row < rows + (slot + 1) * SHIFT)
+    edge = edge & (col == tokens - SHIFT + row - rows - slot * SHIFT)
+    return jnp.where(pooled, weight, jnp.where(edge, 1.0, 0.0)).astype(jnp.bfloat16)
+
+
+def pool_kernel(*refs):
+    sources, out_hbm = refs[:5], refs[5]
+    buffers, out_ref, in_sems, out_sems = refs[6:11], refs[11], refs[12], refs[13]
+    tokens, columns = sources[0].shape
+    rows = tokens // SHORT
+    copies = [
+        pltpu.make_async_copy(source, buffer, in_sems.at[index])
+        for index, (source, buffer) in enumerate(zip(sources, buffers))
+    ]
+    for index in (0, 3, 1, 4, 2):
+        copies[index].start()
+    picks = [select_matrix(tokens, rows, slot) for slot in range(3)]
+    first = lax.broadcasted_iota(jnp.int32, (rows, HDIM), 0) == 0
+    edges, returns = [], []
+    for slot in range(3):
+        copies[slot].wait()
+        if slot < 2:
+            copies[3 + slot].wait()
+        picked = jnp.dot(picks[slot], buffers[slot][...], preferred_element_type=jnp.float32)
+        edges.append(picked[rows:])
+        span = rows if slot < 2 else rows + EDGE_ROWS
+        for head in range(columns // HDIM):
+            inside = slice(head * HDIM, (head + 1) * HDIM)
+            part = picked[:rows, inside]
+            if slot < 2:
+                gain = buffers[3 + slot][head : head + 1, :]
+                part = jnp.where(first, part, rms_rows(part) * gain)
+            else:
+                edge = sum(values[:, inside] for values in edges)
+                out_ref[head, 3 * rows :, :] = edge.astype(jnp.bfloat16)
+            out_ref[head, slot * rows : (slot + 1) * rows, :] = part.astype(jnp.bfloat16)
+        target = pl.ds(slot * rows, span)
+        copy = pltpu.make_async_copy(
+            out_ref.at[:, target], out_hbm.at[:, target], out_sems.at[slot]
+        )
+        copy.start()
+        returns.append(copy)
+    for copy in returns:
+        copy.wait()
+
+
+def pool_inputs(query_src, key_src, value_src, query_gain, key_gain):
+    tokens, columns = query_src.shape
+    heads = columns // HDIM
+    depth = 3 * (tokens // SHORT) + EDGE_ROWS
+    return pl.pallas_call(
+        pool_kernel,
+        in_specs=[pl.BlockSpec(memory_space=pl.ANY)] * 5,
+        out_specs=pl.BlockSpec(memory_space=pl.ANY),
+        out_shape=jax.ShapeDtypeStruct((heads, depth, HDIM), jnp.bfloat16),
+        scratch_shapes=[pltpu.VMEM((tokens, columns), jnp.bfloat16)] * 3
+        + [pltpu.VMEM((heads, HDIM), jnp.float32)] * 2
+        + [pltpu.VMEM((heads, depth, HDIM), jnp.bfloat16)]
+        + [pltpu.SemaphoreType.DMA((5,)), pltpu.SemaphoreType.DMA((3,))],
+    )(query_src, key_src, value_src, query_gain.reshape(heads, HDIM), key_gain.reshape(heads, HDIM))
+
+
+def scaled_exp(scores):
+    return jnp.exp2(scores * (math.log2(math.e) / math.sqrt(HDIM)))
+
+
+def across(left, right):
+    return lax.dot_general(
+        left, right, (((1,), (1,)), ((), ())), preferred_element_type=jnp.float32
+    )
+
+
+def short_kernel(block, arrived_ref, query_gain_ref, key_gain_ref, memory_ref):
+    count, depth, _ = arrived_ref.shape
+    rows = (depth - EDGE_ROWS) // 3
+    total = count * rows
+    head = lax.axis_index("seq")
+    edges = arrived_ref[:, 3 * rows :, :].astype(jnp.float32)
+    edge_row = lax.broadcasted_iota(jnp.int32, edges.shape, 1)
+    first = lax.broadcasted_iota(jnp.int32, (count, rows, HDIM), 1) == 0
+    tensors = []
+    for slot, gain_ref in enumerate((query_gain_ref, key_gain_ref, None)):
+        part = arrived_ref[:, slot * rows : (slot + 1) * rows, :].astype(jnp.float32)
+        own = (edge_row >= slot * SHIFT) & (edge_row < (slot + 1) * SHIFT)
+        tail = jnp.sum(jnp.where(own, edges, 0.0), axis=1, keepdims=True)
+        before = jnp.concatenate([jnp.zeros_like(tail[:1]), tail[:-1]], axis=0)
+        mean = (before + part[:, :1, :]) * (1.0 / SHORT)
+        if gain_ref is not None:
+            mean = rms_rows(mean) * gain_ref[pl.ds(head, 1), :][None]
+        part = jnp.where(first, mean, part).astype(jnp.bfloat16)
+        tensors.append(part.reshape(total, HDIM))
+    query, key, value = tensors
+    diagonal = lax.broadcasted_iota(jnp.int32, (block, block), 1) <= lax.broadcasted_iota(
+        jnp.int32, (block, block), 0
+    )
+    starts = range(0, total, block)
+    sums = [0.0] * len(starts)
+    numerators = [0.0] * len(starts)
+    for index, start in enumerate(starts):
+        exponent = scaled_exp(across(query[start:], key[start : start + block]))
+        for later in range(index, len(starts)):
+            offset = (later - index) * block
+            part = exponent[offset : offset + block]
+            if later == index:
+                part = jnp.where(diagonal, part, 0.0)
+            sums[later] += part
+            numerators[later] += jnp.dot(
+                part.astype(jnp.bfloat16),
+                value[start : start + block],
+                preferred_element_type=jnp.float32,
+            )
+    for index, start in enumerate(starts):
+        denominator = jnp.sum(sums[index], axis=1, keepdims=True)
+        memory_ref[start : start + block, :] = rms_rows(numerators[index] / denominator).astype(
+            jnp.bfloat16
+        )
+
+
+def short_attention(arrived, query_gain, key_gain):
+    count, depth, _ = arrived.shape
+    row_total = count * (depth - EDGE_ROWS) // 3
+    return pl.pallas_call(
+        functools.partial(short_kernel, math.gcd(128, row_total)),
+        out_shape=pltpu.VMEM((row_total, HDIM), jnp.bfloat16),
+    )(on_chip(arrived), query_gain.reshape(-1, HDIM), key_gain.reshape(-1, HDIM))
+
+
+def norm_kernel(shifts, nears, up_ref, gain_ref, *out_refs):
+    device = lax.axis_index("seq")
+    for near, out_ref in zip(nears, out_refs):
+        for index, shift in enumerate(shifts):
+            head = device ^ (near + shift)
+            columns = pl.ds(pl.multiple_of(head * HDIM, HDIM), HDIM)
+            query = rms_rows(up_ref[:, columns].astype(jnp.float32)) * gain_ref[pl.ds(head, 1), :]
+            out_ref[index] = query.astype(jnp.bfloat16)
+
+
+def norm_up(up_query, up_gain, shifts, nears):
+    tokens = up_query.shape[0]
+    shape = pltpu.VMEM((len(shifts), tokens, HDIM), jnp.bfloat16)
+    return pl.pallas_call(
+        functools.partial(norm_kernel, shifts, nears), out_shape=[shape] * len(nears)
+    )(up_query, up_gain.reshape(-1, HDIM))
+
+
+def attend_kernel(nears, first, held, *refs):
+    count = len(nears)
+    memory_refs, refs = refs[: len(held)], refs[len(held) :]
+    query_refs, out_refs = refs[:count], refs[-count:]
+    done_refs = refs[count:-count]
+    tokens = query_refs[0].shape[1]
+    row_total = memory_refs[0].shape[0]
+    device = lax.axis_index("seq")
+    token = lax.broadcasted_iota(jnp.int32, (tokens, row_total), 0)
+    column = SHORT * lax.broadcasted_iota(jnp.int32, (tokens, row_total), 1)
+    for order in range(count):
+        if first:
+            out_refs[order][:first] = done_refs[order][...]
+        visible = column - token <= (device ^ nears[order]) * tokens
+        for index, (memory_ref, slot) in enumerate(zip(memory_refs, held)):
+            memory = memory_ref[...]
+            exponent = scaled_exp(across(query_refs[order][slot], memory))
+            exponent = jnp.where(visible, exponent, 0.0)
+            denominator = jnp.sum(exponent, axis=1, keepdims=True)
+            numerator = jnp.dot(
+                exponent.astype(jnp.bfloat16), memory, preferred_element_type=jnp.float32
+            )
+            out_refs[order][first + index] = (numerator / denominator).astype(jnp.bfloat16)
+
+
+def attend(nears, memories, held, queries, done):
+    tokens = queries[nears[0]].shape[1]
+    first = done[nears[0]].shape[0] if done else 0
+    operands = [*memories, *[queries[near] for near in nears]]
+    operands += [done[near] for near in nears] if done else []
+    shape = pltpu.VMEM((first + len(held), tokens, HDIM), jnp.bfloat16)
+    results = pl.pallas_call(
+        functools.partial(attend_kernel, nears, first, held), out_shape=[shape] * len(nears)
+    )(*[on_chip(value) for value in operands])
+    return dict(zip(nears, results))
+
+
+def place_kernel(offsets, *refs):
+    piece_refs, out_hbm, sems = refs[:-2], refs[-2], refs[-1]
+    device = lax.axis_index("seq")
+    copies = []
+    for number, (offset, piece_ref) in enumerate(zip(offsets, piece_refs)):
+        for flip in (0, PEER):
+            head = device ^ (offset + flip)
+            columns = pl.ds(pl.multiple_of(head * HDIM, HDIM), HDIM)
+            copy = pltpu.make_async_copy(
+                piece_ref.at[flip], out_hbm.at[:, columns], sems.at[2 * number + flip]
+            )
+            copy.start()
+            copies.append(copy)
+    for copy in copies:
+        copy.wait()
+
+
+def place(offsets, pieces):
+    return pl.pallas_call(
+        functools.partial(place_kernel, offsets),
+        out_specs=pl.BlockSpec(memory_space=pl.ANY),
+        out_shape=jax.ShapeDtypeStruct((pieces[0].shape[1], HEADS * HDIM), jnp.bfloat16),
+        scratch_shapes=[pltpu.SemaphoreType.DMA((2 * len(pieces),))],
+    )(*[on_chip(piece) for piece in pieces])
+
+
+def swapped(value, offset):
+    count = lax.axis_size("seq")
+    return lax.ppermute(value, "seq", [(source, source ^ offset) for source in range(count)])
+
+
+def half_exchange(query_src, key_src, value_src, up_query, query_gain, key_gain, up_gain):
+    far = HEADS // 2
+    nears = tuple(range(0, far, 2))
+    outgoing = pool_inputs(query_src, key_src, value_src, query_gain, key_gain)
+    arrived = lax.all_to_all(outgoing, "seq", split_axis=0, concat_axis=0, tiled=True)
+    queries = norm_up(up_query, up_gain, (0, PEER, far, far + PEER), nears)
+    queries = dict(zip(nears, queries))
+    for near in nears[1:]:
+        queries[near] = swapped(queries[near], near)
+    memory = short_attention(arrived, query_gain, key_gain)
+    far_memory = swapped(memory, far)
+    offsets, pieces = [], []
+    for kind, held in enumerate((memory, far_memory)):
+        peer_memory = swapped(held, PEER)
+        done = attend(nears, [held], (2 * kind,), queries, None)
+        done = attend(nears, [peer_memory], (2 * kind + 1,), queries, done)
+        for near in nears:
+            pieces.append(swapped(done[near], near) if near else done[near])
+            offsets.append(near + kind * far)
+    return place(tuple(offsets), pieces)
+
+
+def local(*arrays):
+    whole = lax.axis_size("seq") == HEADS and HEADS & (HEADS - 1) == 0
+    return half_exchange(*arrays) if whole else head_exchange(*arrays)
+
+
 def solution(mesh):
     in_specs = (
         P(("groups", "seq"), None),

time: 73.7 us -> 54 us (0.73)
  waiting for transfers between devices: 23.6 us -> 10 us
  Pallas kernels: 0 us -> 10.2 us
  other arithmetic: 6.43 us -> 0 us
  local copies, waits for them, and re-layouts: 5.64 us -> 0 us
  starting transfers between devices: 15.5 us -> 12.8 us
  matrix products: 2.67 us -> 0 us
  blocking collectives: 18.2 us -> 20.6 us
  between operations: 1.04 us -> 0.08 us
    all_to_all x2 -> x0, waiting for transfers between devices: 22.7 us -> none  [the longest x1 13.5 us: local(): lax.all_to_all(up_out, 'seq', split_axis=0, concat_axis=0, tiled=True)]
    all_to_all x2 -> x0, starting transfers between devices: 13.1 us -> none  [the longest x1 9.53 us: local(): lax.all_to_all(qkv_out, 'seq', split_axis=0, concat_axis=0, tiled=True)]
    ppermute x1 -> x12, starting transfers between devices: 2.4 us -> 12.8 us  [swapped(): lax.ppermute(value, 'seq', [(source, source ^ offset) for source in range...]
    pallas_call x0 -> x8, Pallas kernels: none -> 10.2 us  [the longest x4 3.56 us: attend(): pl.pallas_call(functools.partial(attend_kernel, nears, first, held), out_...]
    ppermute x1 -> x12, waiting for transfers between devices: 0.86 us -> 10 us  [swapped(): lax.ppermute(value, 'seq', [(source, source ^ offset) for source in range...]
    convert_element_type x8 -> x0, other arithmetic: 3.21 us -> none  [the longest x3 1.45 us: pooled_rows(): jnp.concatenate([edge_rows, source[:source.shape[0] - SHIFT]], axis=0)]
    another operation x4 -> x0, local copies, waits for them, and re-layouts: 2.69 us -> none  [the longest x2 1.57 us: local(): jnp.stack([query_src[token_count - SHIFT:], key_src[token_count - SHIFT:]...]
    dot_general x4 -> x0, matrix products: 2.67 us -> none  [the longest x2 1.49 us: compute(): jnp.einsum('hqd,hkd->hqk', queries, key_block, preferred_element_type=jnp...]
  transfers between devices with their start and end apart: 3 -> 12, of which waited for: 3 -> 6; matrix products, arithmetic and copies ran while one was open for 4% -> 0% of each run, Pallas kernels for 0% -> 9%
where the time goes in v4:
time: 54 us; the launch traced here: 53.7 us
  blocking collectives  20.6 us (38%)
  starting transfers between devices  12.8 us (24%)
  Pallas kernels  10.2 us (19%)
  waiting for transfers between devices  10 us (19%)
    all_to_all x1, blocking collectives, half_exchange(): lax.all_to_all(outgoing, 'seq', split_axis=0, concat_axis=0, tiled=True)  20.6 us
    ppermute x12, starting transfers between devices, swapped(): lax.ppermute(value, 'seq', [(source, source ^ offset) for source in range...  12.8 us
    ppermute x12, waiting for transfers between devices, swapped(): lax.ppermute(value, 'seq', [(source, source ^ offset) for source in range...  10 us
    pallas_call x4, Pallas kernels, attend(): pl.pallas_call(functools.partial(attend_kernel, nears, first, held), out_...  3.56 us
    pallas_call x1, Pallas kernels, pool_inputs(): pl.pallas_call(pool_kernel, in_specs=[pl.BlockSpec(memory_space=pl.ANY)]...  2.62 us
    pallas_call x1, Pallas kernels, short_attention(): pl.pallas_call(functools.partial(short_kernel, math.gcd(128, row_total)),...  1.71 us
    pallas_call x1, Pallas kernels, norm_up(): pl.pallas_call(functools.partial(norm_kernel, shifts, nears), out_shape=[...  1.4 us
  transfers between devices with their start and end apart: 12, of which 6 were waited for; matrix products, arithmetic and copies ran while one was open for 0% of the time, Pallas kernels for 9%

profile of v4, /device:TPU:0, one launch (start us, length us, event | category | flops | bytes accessed | tf_op | source)
XLA Modules:
  0.0 53.7 jit_solution(13417508676866327504)
XLA Ops:
  0.0 2.6 %shard_map.73 = bf16[16,112,128]{2,1,0:T(8,128)(2,1)} custom-call(bf16[128,2048]{1,0:T(8,128)(2,1)} %refs_0_.1, bf16[128,2048]{1,0:T(8,128)(2,1)} %refs_1_.1, bf16[128,2048]{1,0:T(8,128)(2,1)} %refs_2_.1, f32[16,128]{1,0:T(8,128)} %bitcast.3, f32[16,128]{1,0:T(8,128)} %bitcast.5), custom_call_target="tpu_custom_call" | custom-call | tf_op jit(solution)/shard_map/pallas_call | solution.py:231
  2.6 20.6 %all_to_all.5.arrived_ref = bf16[16,112,128]{2,1,0:T(8,128)(2,1)S(1)} all-to-all(bf16[16,112,128]{2,1,0:T(8,128)(2,1)} %shard_map.73), channel_id=1, replica_groups=mesh['groups'=2,'seq'=16] {'seq'}, dimensions={0} | all-to-all | bytes 917504 | tf_op jit(solution)/shard_map/all_to_all | solution.py:398
  23.2 1.7 %shard_map.74.refs_0_ = bf16[512,128]{1,0:T(8,128)(2,1)S(1)} custom-call(bf16[16,112,128]{2,1,0:T(8,128)(2,1)S(1)} %all_to_all.5.arrived_ref, f32[16,128]{1,0:T(8,128)} %bitcast.4, f32[16,128]{1,0:T(8,128)} %bitcast.6), custom_call_target="tpu_custom_call" | custom-call | tf_op jit(solution)/shard_map/pallas_call | solution.py:302
  25.0 2.1 %collective-permute-start.7 = (bf16[512,128]{1,0:T(8,128)(2,1)S(1)}, bf16[512,128]{1,0:T(8,128)(2,1)S(1)}, u32[]{:S(2)}, u32[]{:S(2)}) collective-permute-start(bf16[512,128]{1,0:T(8,128)(2,1)S(1)} %shard_map.74.refs_0_), channel_id=1, source_target_pairs={{0,8},{1,9},{2,10},{3,11},{4,12},{5,13},{6,14},{7,15},{8,0},{9,1},... | collective-permute-start | bytes 393224 | tf_op jit(solution)/shard_map/ppermute | solution.py:391
  27.1 1.4 %shard_map.75 = (bf16[4,128,128]{2,1,0:T(8,128)(2,1)S(1)}, bf16[4,128,128]{2,1,0:T(8,128)(2,1)S(1)}, bf16[4,128,128]{2,1,0:T(8,128)(2,1)S(1)}, bf16[4,128,128]{2,1,0:T(8,128)(2,1)S(1)}) custom-call(bf16[128,2048]{1,0:T(8,128)(2,1)} %up_ref.1, f32[16,128]{1,0:T(8,128)} %bitcast.7), custom_call_target="tpu_custom_call" | custom-call | tf_op jit(solution)/shard_map/pallas_call | solution.py:321
  28.5 0.1 collective-permute-start.1
  28.6 1.5 %collective-permute-start.2 = (bf16[4,128,128]{2,1,0:T(8,128)(2,1)S(1)}, bf16[4,128,128]{2,1,0:T(8,128)(2,1)S(1)}, u32[]{:S(2)}, u32[]{:S(2)}) collective-permute-start(bf16[4,128,128]{2,1,0:T(8,128)(2,1)S(1)} %get-tuple-element.27), channel_id=1, source_target_pairs={{0,4},{1,5},{2,6},{3,7},{4,0},{5,1},{6,2},{7,3},{8,12},{9,13},{10,... | collective-permute-start | bytes 393224 | tf_op jit(solution)/shard_map/ppermute | solution.py:391
  30.0 2.0 %collective-permute-start.3 = (bf16[4,128,128]{2,1,0:T(8,128)(2,1)S(1)}, bf16[4,128,128]{2,1,0:T(8,128)(2,1)S(1)}, u32[]{:S(2)}, u32[]{:S(2)}) collective-permute-start(bf16[4,128,128]{2,1,0:T(8,128)(2,1)S(1)} %get-tuple-element.28), channel_id=1, source_target_pairs={{0,6},{1,7},{2,4},{3,5},{4,2},{5,3},{6,0},{7,1},{8,14},{9,15},{10,... | collective-permute-start | bytes 393224 | tf_op jit(solution)/shard_map/ppermute | solution.py:391
  32.1 0.0 collective-permute-start
  32.1 2.3 %collective-permute-done.7.refs_0_ = bf16[512,128]{1,0:T(8,128)(2,1)S(1)} collective-permute-done((bf16[512,128]{1,0:T(8,128)(2,1)S(1)}, bf16[512,128]{1,0:T(8,128)(2,1)S(1)}, u32[]{:S(2)}, u32[]{:S(2)}) %collective-permute-start.7) | collective-permute-done | bytes 131104 | tf_op jit(solution)/shard_map/ppermute | solution.py:391
  34.4 0.0 collective-permute-start.8
  34.4 0.0 collective-permute-done.1.refs_2_
  34.4 2.4 %collective-permute-done.2.refs_3_ = bf16[4,128,128]{2,1,0:T(8,128)(2,1)S(1)} collective-permute-done((bf16[4,128,128]{2,1,0:T(8,128)(2,1)S(1)}, bf16[4,128,128]{2,1,0:T(8,128)(2,1)S(1)}, u32[]{:S(2)}, u32[]{:S(2)}) %collective-permute-start.2) | collective-permute-done | bytes 131104 | tf_op jit(solution)/shard_map/ppermute | solution.py:391
  36.8 2.4 %collective-permute-done.3.refs_4_ = bf16[4,128,128]{2,1,0:T(8,128)(2,1)S(1)} collective-permute-done((bf16[4,128,128]{2,1,0:T(8,128)(2,1)S(1)}, bf16[4,128,128]{2,1,0:T(8,128)(2,1)S(1)}, u32[]{:S(2)}, u32[]{:S(2)}) %collective-permute-start.3) | collective-permute-done | bytes 131104 | tf_op jit(solution)/shard_map/ppermute | solution.py:391
  39.1 0.9 %shard_map.76 = (bf16[1,128,128]{2,1,0:T(8,128)(2,1)S(1)}, bf16[1,128,128]{2,1,0:T(8,128)(2,1)S(1)}, bf16[1,128,128]{2,1,0:T(8,128)(2,1)S(1)}, bf16[1,128,128]{2,1,0:T(8,128)(2,1)S(1)}) custom-call(bf16[512,128]{1,0:T(8,128)(2,1)S(1)} %shard_map.74.refs_0_, bf16[4,128,128]{2,1,0:T(8,128)(2,1)S(1)} %get-tuple-element.25.refs_1_, ...), custom_call_target="tpu_custom_call" | custom-call | tf_op jit(solution)/shard_map/pallas_call | solution.py:357
  40.0 0.0 collective-permute-done.refs_0_
  40.0 0.9 %shard_map.77 = (bf16[2,128,128]{2,1,0:T(8,128)(2,1)S(1)}, bf16[2,128,128]{2,1,0:T(8,128)(2,1)S(1)}, bf16[2,128,128]{2,1,0:T(8,128)(2,1)S(1)}, bf16[2,128,128]{2,1,0:T(8,128)(2,1)S(1)}) custom-call(bf16[512,128]{1,0:T(8,128)(2,1)S(1)} %collective-permute-done.refs_0_, bf16[4,128,128]{2,1,0:T(8,128)(2,1)S(1)} %get-tuple-element.25.refs_1_, ...), custom_call_target="tpu_custom_call" | custom-call | tf_op jit(solution)/shard_map/pallas_call | solution.py:357
  41.0 0.6 %collective-permute-start.4 = (bf16[2,128,128]{2,1,0:T(8,128)(2,1)S(1)}, bf16[2,128,128]{2,1,0:T(8,128)(2,1)S(1)}, u32[]{:S(2)}, u32[]{:S(2)}) collective-permute-start(bf16[2,128,128]{2,1,0:T(8,128)(2,1)S(1)} %get-tuple-element.34), channel_id=1, source_target_pairs={{0,2},{1,3},{2,0},{3,1},{4,6},{5,7},{6,4},{7,5},{8,10},{9,11},{10,... | collective-permute-start | bytes 196616 | tf_op jit(solution)/shard_map/ppermute | solution.py:391
  41.6 0.0 collective-permute-start.5
  41.6 2.9 %collective-permute-start.6 = (bf16[2,128,128]{2,1,0:T(8,128)(2,1)S(1)}, bf16[2,128,128]{2,1,0:T(8,128)(2,1)S(1)}, u32[]{:S(2)}, u32[]{:S(2)}) collective-permute-start(bf16[2,128,128]{2,1,0:T(8,128)(2,1)S(1)} %get-tuple-element.36), channel_id=1, source_target_pairs={{0,6},{1,7},{2,4},{3,5},{4,2},{5,3},{6,0},{7,1},{8,14},{9,15},{10,... | collective-permute-start | bytes 196616 | tf_op jit(solution)/shard_map/ppermute | solution.py:391
  44.5 0.9 %shard_map.78 = (bf16[1,128,128]{2,1,0:T(8,128)(2,1)S(1)}, bf16[1,128,128]{2,1,0:T(8,128)(2,1)S(1)}, bf16[1,128,128]{2,1,0:T(8,128)(2,1)S(1)}, bf16[1,128,128]{2,1,0:T(8,128)(2,1)S(1)}) custom-call(bf16[512,128]{1,0:T(8,128)(2,1)S(1)} %collective-permute-done.7.refs_0_, bf16[4,128,128]{2,1,0:T(8,128)(2,1)S(1)} %get-tuple-element.25.refs_1_, ...), custom_call_target="tpu_custom_call" | custom-call | tf_op jit(solution)/shard_map/pallas_call | solution.py:357
  45.4 0.0 collective-permute-done.8.refs_0_
  45.4 0.9 %shard_map.79 = (bf16[2,128,128]{2,1,0:T(8,128)(2,1)S(1)}, bf16[2,128,128]{2,1,0:T(8,128)(2,1)S(1)}, bf16[2,128,128]{2,1,0:T(8,128)(2,1)S(1)}, bf16[2,128,128]{2,1,0:T(8,128)(2,1)S(1)}) custom-call(bf16[512,128]{1,0:T(8,128)(2,1)S(1)} %collective-permute-done.8.refs_0_, bf16[4,128,128]{2,1,0:T(8,128)(2,1)S(1)} %get-tuple-element.25.refs_1_, ...), custom_call_target="tpu_custom_call" | custom-call | tf_op jit(solution)/shard_map/pallas_call | solution.py:357
  46.3 0.6 %collective-permute-start.9 = (bf16[2,128,128]{2,1,0:T(8,128)(2,1)S(1)}, bf16[2,128,128]{2,1,0:T(8,128)(2,1)S(1)}, u32[]{:S(2)}, u32[]{:S(2)}) collective-permute-start(bf16[2,128,128]{2,1,0:T(8,128)(2,1)S(1)} %get-tuple-element.42), channel_id=1, source_target_pairs={{0,2},{1,3},{2,0},{3,1},{4,6},{5,7},{6,4},{7,5},{8,10},{9,11},{10,... | collective-permute-start | bytes 196616 | tf_op jit(solution)/shard_map/ppermute | solution.py:391
  46.9 0.0 collective-permute-start.10
  46.9 0.0 collective-permute-done.4.refs_1_
  46.9 2.9 %collective-permute-start.11 = (bf16[2,128,128]{2,1,0:T(8,128)(2,1)S(1)}, bf16[2,128,128]{2,1,0:T(8,128)(2,1)S(1)}, u32[]{:S(2)}, u32[]{:S(2)}) collective-permute-start(bf16[2,128,128]{2,1,0:T(8,128)(2,1)S(1)} %get-tuple-element.44), channel_id=1, source_target_pairs={{0,6},{1,7},{2,4},{3,5},{4,2},{5,3},{6,0},{7,1},{8,14},{9,15},{10,... | collective-permute-start | bytes 196616 | tf_op jit(solution)/shard_map/ppermute | solution.py:391
  49.9 0.0 collective-permute-done.5.refs_2_
  49.9 0.0 collective-permute-done.6.refs_3_
  49.9 0.8 %collective-permute-done.9.refs_5_ = bf16[2,128,128]{2,1,0:T(8,128)(2,1)S(1)} collective-permute-done((bf16[2,128,128]{2,1,0:T(8,128)(2,1)S(1)}, bf16[2,128,128]{2,1,0:T(8,128)(2,1)S(1)}, u32[]{:S(2)}, u32[]{:S(2)}) %collective-permute-start.9) | collective-permute-done | bytes 65568 | tf_op jit(solution)/shard_map/ppermute | solution.py:391
  50.6 0.5 %collective-permute-done.10.refs_6_ = bf16[2,128,128]{2,1,0:T(8,128)(2,1)S(1)} collective-permute-done((bf16[2,128,128]{2,1,0:T(8,128)(2,1)S(1)}, bf16[2,128,128]{2,1,0:T(8,128)(2,1)S(1)}, u32[]{:S(2)}, u32[]{:S(2)}) %collective-permute-start.10) | collective-permute-done | bytes 65568 | tf_op jit(solution)/shard_map/ppermute | solution.py:391
  51.2 1.6 %collective-permute-done.11.refs_7_ = bf16[2,128,128]{2,1,0:T(8,128)(2,1)S(1)} collective-permute-done((bf16[2,128,128]{2,1,0:T(8,128)(2,1)S(1)}, bf16[2,128,128]{2,1,0:T(8,128)(2,1)S(1)}, u32[]{:S(2)}, u32[]{:S(2)}) %collective-permute-start.11) | collective-permute-done | bytes 65568 | tf_op jit(solution)/shard_map/ppermute | solution.py:391
  52.8 0.9 %shard_map.80 = bf16[128,2048]{1,0:T(8,128)(2,1)} custom-call(bf16[2,128,128]{2,1,0:T(8,128)(2,1)S(1)} %get-tuple-element.33.refs_0_, bf16[2,128,128]{2,1,0:T(8,128)(2,1)S(1)} %collective-permute-done.4.refs_1_, bf16[2,128,128]{2,1,0:T(8,128)(2,1)S(1)} %collective-permute-done.5.refs_2_, bf16[2,128,128]{2,1,0:T(8,128)(2,1)S(1)} %collective-permute-done.6.refs_3_, ...), custom_call_target="tpu_custom_call" | custom-call | tf_op jit(solution)/shard_map/pallas_call | solution.py:381
Async XLA Ops:
  25.0 9.4 %collective-permute-start.7 = (bf16[512,128]{1,0:T(8,128)(2,1)S(1)}, bf16[512,128]{1,0:T(8,128)(2,1)S(1)}, u32[]{:S(2)}, u32[]{:S(2)}) collective-permute-start(bf16[512,128]{1,0:T(8,128)(2,1)S(1)} %shard_map.74.refs_0_), channel_id=1, source_target_pairs={{0,8},{1,9},{2,10},{3,11},{4,12},{5,13},{6,14},{7,15},{8,0},{9,1},... | collective-permute-start | bytes 393224 | tf_op jit(solution)/shard_map/ppermute | solution.py:391
  28.5 5.9 %collective-permute-start.1 = (bf16[4,128,128]{2,1,0:T(8,128)(2,1)S(1)}, bf16[4,128,128]{2,1,0:T(8,128)(2,1)S(1)}, u32[]{:S(2)}, u32[]{:S(2)}) collective-permute-start(bf16[4,128,128]{2,1,0:T(8,128)(2,1)S(1)} %get-tuple-element.26), channel_id=1, source_target_pairs={{0,2},{1,3},{2,0},{3,1},{4,6},{5,7},{6,4},{7,5},{8,10},{9,11},{10,... | collective-permute-start | bytes 393224 | tf_op jit(solution)/shard_map/ppermute | solution.py:391
  28.6 8.2 %collective-permute-start.2 = (bf16[4,128,128]{2,1,0:T(8,128)(2,1)S(1)}, bf16[4,128,128]{2,1,0:T(8,128)(2,1)S(1)}, u32[]{:S(2)}, u32[]{:S(2)}) collective-permute-start(bf16[4,128,128]{2,1,0:T(8,128)(2,1)S(1)} %get-tuple-element.27), channel_id=1, source_target_pairs={{0,4},{1,5},{2,6},{3,7},{4,0},{5,1},{6,2},{7,3},{8,12},{9,13},{10,... | collective-permute-start | bytes 393224 | tf_op jit(solution)/shard_map/ppermute | solution.py:391
  30.0 9.1 %collective-permute-start.3 = (bf16[4,128,128]{2,1,0:T(8,128)(2,1)S(1)}, bf16[4,128,128]{2,1,0:T(8,128)(2,1)S(1)}, u32[]{:S(2)}, u32[]{:S(2)}) collective-permute-start(bf16[4,128,128]{2,1,0:T(8,128)(2,1)S(1)} %get-tuple-element.28), channel_id=1, source_target_pairs={{0,6},{1,7},{2,4},{3,5},{4,2},{5,3},{6,0},{7,1},{8,14},{9,15},{10,... | collective-permute-start | bytes 393224 | tf_op jit(solution)/shard_map/ppermute | solution.py:391
  32.1 8.0 %collective-permute-start = (bf16[512,128]{1,0:T(8,128)(2,1)S(1)}, bf16[512,128]{1,0:T(8,128)(2,1)S(1)}, u32[]{:S(2)}, u32[]{:S(2)}) collective-permute-start(bf16[512,128]{1,0:T(8,128)(2,1)S(1)} %shard_map.74.refs_0_), channel_id=1, source_target_pairs={{0,1},{1,0},{2,3},{3,2},{4,5},{5,4},{6,7},{7,6},{8,9},{9,8},{10,11... | collective-permute-start | bytes 393224 | tf_op jit(solution)/shard_map/ppermute | solution.py:391
  34.4 11.0 %collective-permute-start.8 = (bf16[512,128]{1,0:T(8,128)(2,1)S(1)}, bf16[512,128]{1,0:T(8,128)(2,1)S(1)}, u32[]{:S(2)}, u32[]{:S(2)}) collective-permute-start(bf16[512,128]{1,0:T(8,128)(2,1)S(1)} %collective-permute-done.7.refs_0_), channel_id=1, source_target_pairs={{0,1},{1,0},{2,3},{3,2},{4,5},{5,4},{6,7},{7,6},{8,9},{9,8},{10,11... | collective-permute-start | bytes 393224 | tf_op jit(solution)/shard_map/ppermute | solution.py:391
  41.0 6.0 %collective-permute-start.4 = (bf16[2,128,128]{2,1,0:T(8,128)(2,1)S(1)}, bf16[2,128,128]{2,1,0:T(8,128)(2,1)S(1)}, u32[]{:S(2)}, u32[]{:S(2)}) collective-permute-start(bf16[2,128,128]{2,1,0:T(8,128)(2,1)S(1)} %get-tuple-element.34), channel_id=1, source_target_pairs={{0,2},{1,3},{2,0},{3,1},{4,6},{5,7},{6,4},{7,5},{8,10},{9,11},{10,... | collective-permute-start | bytes 196616 | tf_op jit(solution)/shard_map/ppermute | solution.py:391
  41.6 8.3 %collective-permute-start.5 = (bf16[2,128,128]{2,1,0:T(8,128)(2,1)S(1)}, bf16[2,128,128]{2,1,0:T(8,128)(2,1)S(1)}, u32[]{:S(2)}, u32[]{:S(2)}) collective-permute-start(bf16[2,128,128]{2,1,0:T(8,128)(2,1)S(1)} %get-tuple-element.35), channel_id=1, source_target_pairs={{0,4},{1,5},{2,6},{3,7},{4,0},{5,1},{6,2},{7,3},{8,12},{9,13},{10,... | collective-permute-start | bytes 196616 | tf_op jit(solution)/shard_map/ppermute | solution.py:391
  41.6 8.3 %collective-permute-start.6 = (bf16[2,128,128]{2,1,0:T(8,128)(2,1)S(1)}, bf16[2,128,128]{2,1,0:T(8,128)(2,1)S(1)}, u32[]{:S(2)}, u32[]{:S(2)}) collective-permute-start(bf16[2,128,128]{2,1,0:T(8,128)(2,1)S(1)} %get-tuple-element.36), channel_id=1, source_target_pairs={{0,6},{1,7},{2,4},{3,5},{4,2},{5,3},{6,0},{7,1},{8,14},{9,15},{10,... | collective-permute-start | bytes 196616 | tf_op jit(solution)/shard_map/ppermute | solution.py:391
  46.3 4.3 %collective-permute-start.9 = (bf16[2,128,128]{2,1,0:T(8,128)(2,1)S(1)}, bf16[2,128,128]{2,1,0:T(8,128)(2,1)S(1)}, u32[]{:S(2)}, u32[]{:S(2)}) collective-permute-start(bf16[2,128,128]{2,1,0:T(8,128)(2,1)S(1)} %get-tuple-element.42), channel_id=1, source_target_pairs={{0,2},{1,3},{2,0},{3,1},{4,6},{5,7},{6,4},{7,5},{8,10},{9,11},{10,... | collective-permute-start | bytes 196616 | tf_op jit(solution)/shard_map/ppermute | solution.py:391
  46.9 4.3 %collective-permute-start.10 = (bf16[2,128,128]{2,1,0:T(8,128)(2,1)S(1)}, bf16[2,128,128]{2,1,0:T(8,128)(2,1)S(1)}, u32[]{:S(2)}, u32[]{:S(2)}) collective-permute-start(bf16[2,128,128]{2,1,0:T(8,128)(2,1)S(1)} %get-tuple-element.43), channel_id=1, source_target_pairs={{0,4},{1,5},{2,6},{3,7},{4,0},{5,1},{6,2},{7,3},{8,12},{9,13},{10,... | collective-permute-start | bytes 196616 | tf_op jit(solution)/shard_map/ppermute | solution.py:391
  46.9 5.9 %collective-permute-start.11 = (bf16[2,128,128]{2,1,0:T(8,128)(2,1)S(1)}, bf16[2,128,128]{2,1,0:T(8,128)(2,1)S(1)}, u32[]{:S(2)}, u32[]{:S(2)}) collective-permute-start(bf16[2,128,128]{2,1,0:T(8,128)(2,1)S(1)} %get-tuple-element.44), channel_id=1, source_target_pairs={{0,6},{1,7},{2,4},{3,5},{4,2},{5,3},{6,0},{7,1},{8,14},{9,15},{10,... | collective-permute-start | bytes 196616 | tf_op jit(solution)/shard_map/ppermute | solution.py:391

commit v5 on v4

--- a/solution.py
+++ b/solution.py
@@ -161,7 +161,7 @@
     return jnp.transpose(output_heads, (1, 0, 2)).reshape(token_count, HEADS * HDIM)
 
 
-EDGE_ROWS = 16
+EDGE_ROWS = 3 * SHIFT - 1
 PEER = 1
 
 
@@ -179,8 +179,10 @@
     pooled = (row < rows) & (col <= SHORT * row) & (col >= SHORT * row - SHIFT)
     weight = jnp.where(row == 0, 1.0, 1.0 / SHORT)
     edge = (row >= rows + slot * SHIFT) & (row < rows + (slot + 1) * SHIFT)
-    edge = edge & (col == tokens - SHIFT + row - rows - slot * SHIFT)
-    return jnp.where(pooled, weight, jnp.where(edge, 1.0, 0.0)).astype(jnp.bfloat16)
+    last = col >= tokens - SHIFT
+    if slot < 2:
+        last = col == tokens - SHIFT + row - rows - slot * SHIFT
+    return jnp.where(pooled, weight, jnp.where(edge & last, 1.0, 0.0)).astype(jnp.bfloat16)
 
 
 def pool_kernel(*refs):
@@ -196,6 +198,7 @@
         copies[index].start()
     picks = [select_matrix(tokens, rows, slot) for slot in range(3)]
     first = lax.broadcasted_iota(jnp.int32, (rows, HDIM), 0) == 0
+    rest = lax.broadcasted_iota(jnp.int32, (EDGE_ROWS, HDIM), 0) == EDGE_ROWS - 1
     edges, returns = [], []
     for slot in range(3):
         copies[slot].wait()
@@ -212,7 +215,9 @@
                 part = jnp.where(first, part, rms_rows(part) * gain)
             else:
                 edge = sum(values[:, inside] for values in edges)
-                out_ref[head, 3 * rows :, :] = edge.astype(jnp.bfloat16)
+                high = edge.astype(jnp.bfloat16)
+                low = (edge - high.astype(jnp.float32)).astype(jnp.bfloat16)
+                out_ref[head, 3 * rows :, :] = jnp.where(rest, low, high)
             out_ref[head, slot * rows : (slot + 1) * rows, :] = part.astype(jnp.bfloat16)
         target = pl.ds(slot * rows, span)
         copy = pltpu.make_async_copy(
@@ -302,7 +307,7 @@
     return pl.pallas_call(
         functools.partial(short_kernel, math.gcd(128, row_total)),
         out_shape=pltpu.VMEM((row_total, HDIM), jnp.bfloat16),
-    )(on_chip(arrived), query_gain.reshape(-1, HDIM), key_gain.reshape(-1, HDIM))
+    )(on_chip(arrived), *[on_chip(gain.reshape(-1, HDIM)) for gain in (query_gain, key_gain)])
 
 
 def norm_kernel(shifts, nears, up_ref, gain_ref, *out_refs):
@@ -333,19 +338,31 @@
     device = lax.axis_index("seq")
     token = lax.broadcasted_iota(jnp.int32, (tokens, row_total), 0)
     column = SHORT * lax.broadcasted_iota(jnp.int32, (tokens, row_total), 1)
-    for order in range(count):
-        if first:
-            out_refs[order][:first] = done_refs[order][...]
-        visible = column - token <= (device ^ nears[order]) * tokens
-        for index, (memory_ref, slot) in enumerate(zip(memory_refs, held)):
-            memory = memory_ref[...]
-            exponent = scaled_exp(across(query_refs[order][slot], memory))
-            exponent = jnp.where(visible, exponent, 0.0)
-            denominator = jnp.sum(exponent, axis=1, keepdims=True)
-            numerator = jnp.dot(
-                exponent.astype(jnp.bfloat16), memory, preferred_element_type=jnp.float32
-            )
-            out_refs[order][first + index] = (numerator / denominator).astype(jnp.bfloat16)
+    behind = column - token
+    for index, (memory_ref, slot) in enumerate(zip(memory_refs, held)):
+        memory = memory_ref[...]
+        query = jnp.concatenate([query_ref[slot] for query_ref in query_refs], axis=0)
+        exponent = scaled_exp(across(query, memory))
+        exponent = jnp.concatenate(
+            [
+                jnp.where(
+                    behind <= (device ^ near) * tokens,
+                    exponent[order * tokens : (order + 1) * tokens],
+                    0.0,
+                )
+                for order, near in enumerate(nears)
+            ],
+            axis=0,
+        )
+        denominator = jnp.sum(exponent, axis=1, keepdims=True)
+        numerator = jnp.dot(
+            exponent.astype(jnp.bfloat16), memory, preferred_element_type=jnp.float32
+        )
+        result = (numerator / denominator).astype(jnp.bfloat16)
+        for order, out_ref in enumerate(out_refs):
+            out_ref[first + index] = result[order * tokens : (order + 1) * tokens]
+    for done_ref, out_ref in zip(done_refs, out_refs):
+        out_ref[:first] = done_ref[...]
 
 
 def attend(nears, memories, held, queries, done):

time: 54 us -> 51.3 us (0.950)
  Pallas kernels: 10.2 us -> 8.12 us
    pallas_call x4, Pallas kernels: 3.56 us -> 2.19 us  [attend(): pl.pallas_call(functools.partial(attend_kernel, nears, first, held), out_...]
    pallas_call x1, Pallas kernels: 1.71 us -> 1 us  [short_attention(): pl.pallas_call(functools.partial(short_kernel, math.gcd(128, row_total)),...]
  transfers between devices with their start and end apart: 12 -> 12, of which waited for: 6 -> 6; matrix products, arithmetic and copies ran while one was open for 0% -> 0% of each run, Pallas kernels for 9% -> 7%
where the time goes in v5:
time: 51.3 us; the launch traced here: 51.1 us
  blocking collectives  20.1 us (39%)
  starting transfers between devices  12.6 us (25%)
  waiting for transfers between devices  10.1 us (20%)
  Pallas kernels  8.12 us (16%)
    all_to_all x1, blocking collectives, half_exchange(): lax.all_to_all(outgoing, 'seq', split_axis=0, concat_axis=0, tiled=True)  20.1 us
    ppermute x12, starting transfers between devices, swapped(): lax.ppermute(value, 'seq', [(source, source ^ offset) for source in range...  12.6 us
    ppermute x12, waiting for transfers between devices, swapped(): lax.ppermute(value, 'seq', [(source, source ^ offset) for source in range...  10.1 us
    pallas_call x1, Pallas kernels, pool_inputs(): pl.pallas_call(pool_kernel, in_specs=[pl.BlockSpec(memory_space=pl.ANY)]...  2.61 us
    pallas_call x4, Pallas kernels, attend(): pl.pallas_call(functools.partial(attend_kernel, nears, first, held), out_...  2.19 us
    pallas_call x1, Pallas kernels, norm_up(): pl.pallas_call(functools.partial(norm_kernel, shifts, nears), out_shape=[...  1.4 us
  transfers between devices with their start and end apart: 12, of which 6 were waited for; matrix products, arithmetic and copies ran while one was open for 0% of the time, Pallas kernels for 7%

profile of v5, /device:TPU:0, one launch (start us, length us, event | category | flops | bytes accessed | tf_op | source)
XLA Modules:
  0.0 51.1 jit_solution(13231087600650172726)
XLA Ops:
  0.0 2.6 %shard_map.73 = bf16[16,104,128]{2,1,0:T(8,128)(2,1)} custom-call(bf16[128,2048]{1,0:T(8,128)(2,1)} %refs_0_.1, bf16[128,2048]{1,0:T(8,128)(2,1)} %refs_1_.1, bf16[128,2048]{1,0:T(8,128)(2,1)} %refs_2_.1, f32[16,128]{1,0:T(8,128)} %bitcast.3, f32[16,128]{1,0:T(8,128)} %bitcast.5), custom_call_target="tpu_custom_call" | custom-call | tf_op jit(solution)/shard_map/pallas_call | solution.py:236
  2.6 0.0 copy-start
  2.6 0.0 copy-start.1
  2.6 20.1 %all_to_all.5.arrived_ref = bf16[16,104,128]{2,1,0:T(8,128)(2,1)S(1)} all-to-all(bf16[16,104,128]{2,1,0:T(8,128)(2,1)} %shard_map.73), channel_id=1, replica_groups=mesh['groups'=2,'seq'=16] {'seq'}, dimensions={0} | all-to-all | bytes 851968 | tf_op jit(solution)/shard_map/all_to_all | solution.py:415
  22.7 0.0 copy-done
  22.7 0.0 copy-done.1
  22.7 1.0 %shard_map.74.refs_0_ = bf16[512,128]{1,0:T(8,128)(2,1)S(1)} custom-call(bf16[16,104,128]{2,1,0:T(8,128)(2,1)S(1)} %all_to_all.5.arrived_ref, f32[16,128]{1,0:T(8,128)S(1)} %bitcast.4, f32[16,128]{1,0:T(8,128)S(1)} %bitcast.6), custom_call_target="tpu_custom_call" | custom-call | tf_op jit(solution)/shard_map/pallas_call | solution.py:307
  23.7 2.0 %collective-permute-start.7 = (bf16[512,128]{1,0:T(8,128)(2,1)S(1)}, bf16[512,128]{1,0:T(8,128)(2,1)S(1)}, u32[]{:S(2)}, u32[]{:S(2)}) collective-permute-start(bf16[512,128]{1,0:T(8,128)(2,1)S(1)} %shard_map.74.refs_0_), channel_id=1, source_target_pairs={{0,8},{1,9},{2,10},{3,11},{4,12},{5,13},{6,14},{7,15},{8,0},{9,1},... | collective-permute-start | bytes 393224 | tf_op jit(solution)/shard_map/ppermute | solution.py:408
  25.7 1.4 %shard_map.75 = (bf16[4,128,128]{2,1,0:T(8,128)(2,1)S(1)}, bf16[4,128,128]{2,1,0:T(8,128)(2,1)S(1)}, bf16[4,128,128]{2,1,0:T(8,128)(2,1)S(1)}, bf16[4,128,128]{2,1,0:T(8,128)(2,1)S(1)}) custom-call(bf16[128,2048]{1,0:T(8,128)(2,1)} %up_ref.1, f32[16,128]{1,0:T(8,128)} %bitcast.7), custom_call_target="tpu_custom_call" | custom-call | tf_op jit(solution)/shard_map/pallas_call | solution.py:326
  27.1 0.1 collective-permute-start.1
  27.2 1.4 %collective-permute-start.2 = (bf16[4,128,128]{2,1,0:T(8,128)(2,1)S(1)}, bf16[4,128,128]{2,1,0:T(8,128)(2,1)S(1)}, u32[]{:S(2)}, u32[]{:S(2)}) collective-permute-start(bf16[4,128,128]{2,1,0:T(8,128)(2,1)S(1)} %get-tuple-element.27), channel_id=1, source_target_pairs={{0,4},{1,5},{2,6},{3,7},{4,0},{5,1},{6,2},{7,3},{8,12},{9,13},{10,... | collective-permute-start | bytes 393224 | tf_op jit(solution)/shard_map/ppermute | solution.py:408
  28.6 2.0 %collective-permute-start.3 = (bf16[4,128,128]{2,1,0:T(8,128)(2,1)S(1)}, bf16[4,128,128]{2,1,0:T(8,128)(2,1)S(1)}, u32[]{:S(2)}, u32[]{:S(2)}) collective-permute-start(bf16[4,128,128]{2,1,0:T(8,128)(2,1)S(1)} %get-tuple-element.28), channel_id=1, source_target_pairs={{0,6},{1,7},{2,4},{3,5},{4,2},{5,3},{6,0},{7,1},{8,14},{9,15},{10,... | collective-permute-start | bytes 393224 | tf_op jit(solution)/shard_map/ppermute | solution.py:408
  30.7 0.0 collective-permute-start
  30.7 2.5 %collective-permute-done.7.refs_0_ = bf16[512,128]{1,0:T(8,128)(2,1)S(1)} collective-permute-done((bf16[512,128]{1,0:T(8,128)(2,1)S(1)}, bf16[512,128]{1,0:T(8,128)(2,1)S(1)}, u32[]{:S(2)}, u32[]{:S(2)}) %collective-permute-start.7) | collective-permute-done | bytes 131104 | tf_op jit(solution)/shard_map/ppermute | solution.py:408
  33.1 0.0 collective-permute-start.8
  33.1 0.0 collective-permute-done.1.refs_2_
  33.1 2.3 %collective-permute-done.2.refs_3_ = bf16[4,128,128]{2,1,0:T(8,128)(2,1)S(1)} collective-permute-done((bf16[4,128,128]{2,1,0:T(8,128)(2,1)S(1)}, bf16[4,128,128]{2,1,0:T(8,128)(2,1)S(1)}, u32[]{:S(2)}, u32[]{:S(2)}) %collective-permute-start.2) | collective-permute-done | bytes 131104 | tf_op jit(solution)/shard_map/ppermute | solution.py:408
  35.5 2.4 %collective-permute-done.3.refs_4_ = bf16[4,128,128]{2,1,0:T(8,128)(2,1)S(1)} collective-permute-done((bf16[4,128,128]{2,1,0:T(8,128)(2,1)S(1)}, bf16[4,128,128]{2,1,0:T(8,128)(2,1)S(1)}, u32[]{:S(2)}, u32[]{:S(2)}) %collective-permute-start.3) | collective-permute-done | bytes 131104 | tf_op jit(solution)/shard_map/ppermute | solution.py:408
  37.9 0.5 %shard_map.76 = (bf16[1,128,128]{2,1,0:T(8,128)(2,1)S(1)}, bf16[1,128,128]{2,1,0:T(8,128)(2,1)S(1)}, bf16[1,128,128]{2,1,0:T(8,128)(2,1)S(1)}, bf16[1,128,128]{2,1,0:T(8,128)(2,1)S(1)}) custom-call(bf16[512,128]{1,0:T(8,128)(2,1)S(1)} %shard_map.74.refs_0_, bf16[4,128,128]{2,1,0:T(8,128)(2,1)S(1)} %get-tuple-element.25.refs_1_, ...), custom_call_target="tpu_custom_call" | custom-call | tf_op jit(solution)/shard_map/pallas_call | solution.py:374
  38.4 0.0 collective-permute-done.refs_0_
  38.4 0.5 %shard_map.77 = (bf16[2,128,128]{2,1,0:T(8,128)(2,1)S(1)}, bf16[2,128,128]{2,1,0:T(8,128)(2,1)S(1)}, bf16[2,128,128]{2,1,0:T(8,128)(2,1)S(1)}, bf16[2,128,128]{2,1,0:T(8,128)(2,1)S(1)}) custom-call(bf16[512,128]{1,0:T(8,128)(2,1)S(1)} %collective-permute-done.refs_0_, bf16[4,128,128]{2,1,0:T(8,128)(2,1)S(1)} %get-tuple-element.25.refs_1_, ...), custom_call_target="tpu_custom_call" | custom-call | tf_op jit(solution)/shard_map/pallas_call | solution.py:374
  39.0 0.6 %collective-permute-start.4 = (bf16[2,128,128]{2,1,0:T(8,128)(2,1)S(1)}, bf16[2,128,128]{2,1,0:T(8,128)(2,1)S(1)}, u32[]{:S(2)}, u32[]{:S(2)}) collective-permute-start(bf16[2,128,128]{2,1,0:T(8,128)(2,1)S(1)} %get-tuple-element.34), channel_id=1, source_target_pairs={{0,2},{1,3},{2,0},{3,1},{4,6},{5,7},{6,4},{7,5},{8,10},{9,11},{10,... | collective-permute-start | bytes 196616 | tf_op jit(solution)/shard_map/ppermute | solution.py:408
  39.6 0.0 collective-permute-start.5
  39.6 2.9 %collective-permute-start.6 = (bf16[2,128,128]{2,1,0:T(8,128)(2,1)S(1)}, bf16[2,128,128]{2,1,0:T(8,128)(2,1)S(1)}, u32[]{:S(2)}, u32[]{:S(2)}) collective-permute-start(bf16[2,128,128]{2,1,0:T(8,128)(2,1)S(1)} %get-tuple-element.36), channel_id=1, source_target_pairs={{0,6},{1,7},{2,4},{3,5},{4,2},{5,3},{6,0},{7,1},{8,14},{9,15},{10,... | collective-permute-start | bytes 196616 | tf_op jit(solution)/shard_map/ppermute | solution.py:408
  42.5 0.5 %shard_map.78 = (bf16[1,128,128]{2,1,0:T(8,128)(2,1)S(1)}, bf16[1,128,128]{2,1,0:T(8,128)(2,1)S(1)}, bf16[1,128,128]{2,1,0:T(8,128)(2,1)S(1)}, bf16[1,128,128]{2,1,0:T(8,128)(2,1)S(1)}) custom-call(bf16[512,128]{1,0:T(8,128)(2,1)S(1)} %collective-permute-done.7.refs_0_, bf16[4,128,128]{2,1,0:T(8,128)(2,1)S(1)} %get-tuple-element.25.refs_1_, ...), custom_call_target="tpu_custom_call" | custom-call | tf_op jit(solution)/shard_map/pallas_call | solution.py:374
  43.1 0.0 collective-permute-done.8.refs_0_
  43.1 0.5 %shard_map.79 = (bf16[2,128,128]{2,1,0:T(8,128)(2,1)S(1)}, bf16[2,128,128]{2,1,0:T(8,128)(2,1)S(1)}, bf16[2,128,128]{2,1,0:T(8,128)(2,1)S(1)}, bf16[2,128,128]{2,1,0:T(8,128)(2,1)S(1)}) custom-call(bf16[512,128]{1,0:T(8,128)(2,1)S(1)} %collective-permute-done.8.refs_0_, bf16[4,128,128]{2,1,0:T(8,128)(2,1)S(1)} %get-tuple-element.25.refs_1_, ...), custom_call_target="tpu_custom_call" | custom-call | tf_op jit(solution)/shard_map/pallas_call | solution.py:374
  43.6 0.7 %collective-permute-start.9 = (bf16[2,128,128]{2,1,0:T(8,128)(2,1)S(1)}, bf16[2,128,128]{2,1,0:T(8,128)(2,1)S(1)}, u32[]{:S(2)}, u32[]{:S(2)}) collective-permute-start(bf16[2,128,128]{2,1,0:T(8,128)(2,1)S(1)} %get-tuple-element.42), channel_id=1, source_target_pairs={{0,2},{1,3},{2,0},{3,1},{4,6},{5,7},{6,4},{7,5},{8,10},{9,11},{10,... | collective-permute-start | bytes 196616 | tf_op jit(solution)/shard_map/ppermute | solution.py:408
  44.3 0.0 collective-permute-start.10
  44.3 0.0 collective-permute-done.4.refs_1_
  44.3 2.9 %collective-permute-start.11 = (bf16[2,128,128]{2,1,0:T(8,128)(2,1)S(1)}, bf16[2,128,128]{2,1,0:T(8,128)(2,1)S(1)}, u32[]{:S(2)}, u32[]{:S(2)}) collective-permute-start(bf16[2,128,128]{2,1,0:T(8,128)(2,1)S(1)} %get-tuple-element.44), channel_id=1, source_target_pairs={{0,6},{1,7},{2,4},{3,5},{4,2},{5,3},{6,0},{7,1},{8,14},{9,15},{10,... | collective-permute-start | bytes 196616 | tf_op jit(solution)/shard_map/ppermute | solution.py:408
  47.2 0.0 collective-permute-done.5.refs_2_
  47.2 0.0 collective-permute-done.6.refs_3_
  47.2 0.8 %collective-permute-done.9.refs_5_ = bf16[2,128,128]{2,1,0:T(8,128)(2,1)S(1)} collective-permute-done((bf16[2,128,128]{2,1,0:T(8,128)(2,1)S(1)}, bf16[2,128,128]{2,1,0:T(8,128)(2,1)S(1)}, u32[]{:S(2)}, u32[]{:S(2)}) %collective-permute-start.9) | collective-permute-done | bytes 65568 | tf_op jit(solution)/shard_map/ppermute | solution.py:408
  48.0 0.6 %collective-permute-done.10.refs_6_ = bf16[2,128,128]{2,1,0:T(8,128)(2,1)S(1)} collective-permute-done((bf16[2,128,128]{2,1,0:T(8,128)(2,1)S(1)}, bf16[2,128,128]{2,1,0:T(8,128)(2,1)S(1)}, u32[]{:S(2)}, u32[]{:S(2)}) %collective-permute-start.10) | collective-permute-done | bytes 65568 | tf_op jit(solution)/shard_map/ppermute | solution.py:408
  48.6 1.6 %collective-permute-done.11.refs_7_ = bf16[2,128,128]{2,1,0:T(8,128)(2,1)S(1)} collective-permute-done((bf16[2,128,128]{2,1,0:T(8,128)(2,1)S(1)}, bf16[2,128,128]{2,1,0:T(8,128)(2,1)S(1)}, u32[]{:S(2)}, u32[]{:S(2)}) %collective-permute-start.11) | collective-permute-done | bytes 65568 | tf_op jit(solution)/shard_map/ppermute | solution.py:408
  50.1 0.9 %shard_map.80 = bf16[128,2048]{1,0:T(8,128)(2,1)} custom-call(bf16[2,128,128]{2,1,0:T(8,128)(2,1)S(1)} %get-tuple-element.33.refs_0_, bf16[2,128,128]{2,1,0:T(8,128)(2,1)S(1)} %collective-permute-done.4.refs_1_, bf16[2,128,128]{2,1,0:T(8,128)(2,1)S(1)} %collective-permute-done.5.refs_2_, bf16[2,128,128]{2,1,0:T(8,128)(2,1)S(1)} %collective-permute-done.6.refs_3_, ...), custom_call_target="tpu_custom_call" | custom-call | tf_op jit(solution)/shard_map/pallas_call | solution.py:398
Async XLA Ops:
  2.6 20.1 %copy-start = (f32[2048]{0:T(1024)S(1)}, f32[2048]{0:T(1024)}, u32[]{:S(2)}) copy-start(f32[2048]{0:T(1024)} %param.11) | copy-start | bytes 24580
  2.6 20.1 %copy-start.1 = (f32[2048]{0:T(1024)S(1)}, f32[2048]{0:T(1024)}, u32[]{:S(2)}) copy-start(f32[2048]{0:T(1024)} %param.12) | copy-start | bytes 24580
  23.7 9.4 %collective-permute-start.7 = (bf16[512,128]{1,0:T(8,128)(2,1)S(1)}, bf16[512,128]{1,0:T(8,128)(2,1)S(1)}, u32[]{:S(2)}, u32[]{:S(2)}) collective-permute-start(bf16[512,128]{1,0:T(8,128)(2,1)S(1)} %shard_map.74.refs_0_), channel_id=1, source_target_pairs={{0,8},{1,9},{2,10},{3,11},{4,12},{5,13},{6,14},{7,15},{8,0},{9,1},... | collective-permute-start | bytes 393224 | tf_op jit(solution)/shard_map/ppermute | solution.py:408
  27.1 6.0 %collective-permute-start.1 = (bf16[4,128,128]{2,1,0:T(8,128)(2,1)S(1)}, bf16[4,128,128]{2,1,0:T(8,128)(2,1)S(1)}, u32[]{:S(2)}, u32[]{:S(2)}) collective-permute-start(bf16[4,128,128]{2,1,0:T(8,128)(2,1)S(1)} %get-tuple-element.26), channel_id=1, source_target_pairs={{0,2},{1,3},{2,0},{3,1},{4,6},{5,7},{6,4},{7,5},{8,10},{9,11},{10,... | collective-permute-start | bytes 393224 | tf_op jit(solution)/shard_map/ppermute | solution.py:408
  27.2 8.3 %collective-permute-start.2 = (bf16[4,128,128]{2,1,0:T(8,128)(2,1)S(1)}, bf16[4,128,128]{2,1,0:T(8,128)(2,1)S(1)}, u32[]{:S(2)}, u32[]{:S(2)}) collective-permute-start(bf16[4,128,128]{2,1,0:T(8,128)(2,1)S(1)} %get-tuple-element.27), channel_id=1, source_target_pairs={{0,4},{1,5},{2,6},{3,7},{4,0},{5,1},{6,2},{7,3},{8,12},{9,13},{10,... | collective-permute-start | bytes 393224 | tf_op jit(solution)/shard_map/ppermute | solution.py:408
  28.6 9.2 %collective-permute-start.3 = (bf16[4,128,128]{2,1,0:T(8,128)(2,1)S(1)}, bf16[4,128,128]{2,1,0:T(8,128)(2,1)S(1)}, u32[]{:S(2)}, u32[]{:S(2)}) collective-permute-start(bf16[4,128,128]{2,1,0:T(8,128)(2,1)S(1)} %get-tuple-element.28), channel_id=1, source_target_pairs={{0,6},{1,7},{2,4},{3,5},{4,2},{5,3},{6,0},{7,1},{8,14},{9,15},{10,... | collective-permute-start | bytes 393224 | tf_op jit(solution)/shard_map/ppermute | solution.py:408
  30.7 7.8 %collective-permute-start = (bf16[512,128]{1,0:T(8,128)(2,1)S(1)}, bf16[512,128]{1,0:T(8,128)(2,1)S(1)}, u32[]{:S(2)}, u32[]{:S(2)}) collective-permute-start(bf16[512,128]{1,0:T(8,128)(2,1)S(1)} %shard_map.74.refs_0_), channel_id=1, source_target_pairs={{0,1},{1,0},{2,3},{3,2},{4,5},{5,4},{6,7},{7,6},{8,9},{9,8},{10,11... | collective-permute-start | bytes 393224 | tf_op jit(solution)/shard_map/ppermute | solution.py:408
  33.1 9.9 %collective-permute-start.8 = (bf16[512,128]{1,0:T(8,128)(2,1)S(1)}, bf16[512,128]{1,0:T(8,128)(2,1)S(1)}, u32[]{:S(2)}, u32[]{:S(2)}) collective-permute-start(bf16[512,128]{1,0:T(8,128)(2,1)S(1)} %collective-permute-done.7.refs_0_), channel_id=1, source_target_pairs={{0,1},{1,0},{2,3},{3,2},{4,5},{5,4},{6,7},{7,6},{8,9},{9,8},{10,11... | collective-permute-start | bytes 393224 | tf_op jit(solution)/shard_map/ppermute | solution.py:408
  39.0 5.3 %collective-permute-start.4 = (bf16[2,128,128]{2,1,0:T(8,128)(2,1)S(1)}, bf16[2,128,128]{2,1,0:T(8,128)(2,1)S(1)}, u32[]{:S(2)}, u32[]{:S(2)}) collective-permute-start(bf16[2,128,128]{2,1,0:T(8,128)(2,1)S(1)} %get-tuple-element.34), channel_id=1, source_target_pairs={{0,2},{1,3},{2,0},{3,1},{4,6},{5,7},{6,4},{7,5},{8,10},{9,11},{10,... | collective-permute-start | bytes 196616 | tf_op jit(solution)/shard_map/ppermute | solution.py:408
  39.6 7.6 %collective-permute-start.5 = (bf16[2,128,128]{2,1,0:T(8,128)(2,1)S(1)}, bf16[2,128,128]{2,1,0:T(8,128)(2,1)S(1)}, u32[]{:S(2)}, u32[]{:S(2)}) collective-permute-start(bf16[2,128,128]{2,1,0:T(8,128)(2,1)S(1)} %get-tuple-element.35), channel_id=1, source_target_pairs={{0,4},{1,5},{2,6},{3,7},{4,0},{5,1},{6,2},{7,3},{8,12},{9,13},{10,... | collective-permute-start | bytes 196616 | tf_op jit(solution)/shard_map/ppermute | solution.py:408
  39.6 7.6 %collective-permute-start.6 = (bf16[2,128,128]{2,1,0:T(8,128)(2,1)S(1)}, bf16[2,128,128]{2,1,0:T(8,128)(2,1)S(1)}, u32[]{:S(2)}, u32[]{:S(2)}) collective-permute-start(bf16[2,128,128]{2,1,0:T(8,128)(2,1)S(1)} %get-tuple-element.36), channel_id=1, source_target_pairs={{0,6},{1,7},{2,4},{3,5},{4,2},{5,3},{6,0},{7,1},{8,14},{9,15},{10,... | collective-permute-start | bytes 196616 | tf_op jit(solution)/shard_map/ppermute | solution.py:408
  43.6 4.3 %collective-permute-start.9 = (bf16[2,128,128]{2,1,0:T(8,128)(2,1)S(1)}, bf16[2,128,128]{2,1,0:T(8,128)(2,1)S(1)}, u32[]{:S(2)}, u32[]{:S(2)}) collective-permute-start(bf16[2,128,128]{2,1,0:T(8,128)(2,1)S(1)} %get-tuple-element.42), channel_id=1, source_target_pairs={{0,2},{1,3},{2,0},{3,1},{4,6},{5,7},{6,4},{7,5},{8,10},{9,11},{10,... | collective-permute-start | bytes 196616 | tf_op jit(solution)/shard_map/ppermute | solution.py:408
  44.3 4.3 %collective-permute-start.10 = (bf16[2,128,128]{2,1,0:T(8,128)(2,1)S(1)}, bf16[2,128,128]{2,1,0:T(8,128)(2,1)S(1)}, u32[]{:S(2)}, u32[]{:S(2)}) collective-permute-start(bf16[2,128,128]{2,1,0:T(8,128)(2,1)S(1)} %get-tuple-element.43), channel_id=1, source_target_pairs={{0,4},{1,5},{2,6},{3,7},{4,0},{5,1},{6,2},{7,3},{8,12},{9,13},{10,... | collective-permute-start | bytes 196616 | tf_op jit(solution)/shard_map/ppermute | solution.py:408
  44.3 5.8 %collective-permute-start.11 = (bf16[2,128,128]{2,1,0:T(8,128)(2,1)S(1)}, bf16[2,128,128]{2,1,0:T(8,128)(2,1)S(1)}, u32[]{:S(2)}, u32[]{:S(2)}) collective-permute-start(bf16[2,128,128]{2,1,0:T(8,128)(2,1)S(1)} %get-tuple-element.44), channel_id=1, source_target_pairs={{0,6},{1,7},{2,4},{3,5},{4,2},{5,3},{6,0},{7,1},{8,14},{9,15},{10,... | collective-permute-start | bytes 196616 | tf_op jit(solution)/shard_map/ppermute | solution.py:408

commit v6 on v5

--- a/solution.py
+++ b/solution.py
@@ -255,7 +255,7 @@
     )
 
 
-def short_kernel(block, arrived_ref, query_gain_ref, key_gain_ref, memory_ref):
+def short_kernel(block, arrived_ref, query_gain_ref, key_gain_ref, memory_ref, *half_refs):
     count, depth, _ = arrived_ref.shape
     rows = (depth - EDGE_ROWS) // 3
     total = count * rows
@@ -296,17 +296,21 @@
             )
     for index, start in enumerate(starts):
         denominator = jnp.sum(sums[index], axis=1, keepdims=True)
-        memory_ref[start : start + block, :] = rms_rows(numerators[index] / denominator).astype(
-            jnp.bfloat16
-        )
+        result = rms_rows(numerators[index] / denominator).astype(jnp.bfloat16)
+        memory_ref[start : start + block, :] = result
+        upper, inside = divmod(start, total // 2)
+        half_refs[upper][inside : inside + block, :] = result
 
 
 def short_attention(arrived, query_gain, key_gain):
     count, depth, _ = arrived.shape
     row_total = count * (depth - EDGE_ROWS) // 3
     return pl.pallas_call(
-        functools.partial(short_kernel, math.gcd(128, row_total)),
-        out_shape=pltpu.VMEM((row_total, HDIM), jnp.bfloat16),
+        functools.partial(short_kernel, math.gcd(128, row_total // 2)),
+        out_shape=[
+            pltpu.VMEM((size, HDIM), jnp.bfloat16)
+            for size in (row_total, row_total // 2, row_total // 2)
+        ],
     )(on_chip(arrived), *[on_chip(gain.reshape(-1, HDIM)) for gain in (query_gain, key_gain)])
 
 
@@ -328,51 +332,46 @@
     )(up_query, up_gain.reshape(-1, HDIM))
 
 
-def attend_kernel(nears, first, held, *refs):
+def attend_kernel(nears, slot, parts, *refs):
     count = len(nears)
-    memory_refs, refs = refs[: len(held)], refs[len(held) :]
-    query_refs, out_refs = refs[:count], refs[-count:]
-    done_refs = refs[count:-count]
+    memory_refs, query_refs, refs = refs[:parts], refs[parts : parts + count], refs[parts + count :]
+    done_refs, out_refs = refs[:-count], refs[-count:]
     tokens = query_refs[0].shape[1]
-    row_total = memory_refs[0].shape[0]
+    memory = jnp.concatenate([memory_ref[...] for memory_ref in memory_refs], axis=0)
+    row_total = memory.shape[0]
     device = lax.axis_index("seq")
     token = lax.broadcasted_iota(jnp.int32, (tokens, row_total), 0)
     column = SHORT * lax.broadcasted_iota(jnp.int32, (tokens, row_total), 1)
     behind = column - token
-    for index, (memory_ref, slot) in enumerate(zip(memory_refs, held)):
-        memory = memory_ref[...]
-        query = jnp.concatenate([query_ref[slot] for query_ref in query_refs], axis=0)
-        exponent = scaled_exp(across(query, memory))
-        exponent = jnp.concatenate(
-            [
-                jnp.where(
-                    behind <= (device ^ near) * tokens,
-                    exponent[order * tokens : (order + 1) * tokens],
-                    0.0,
-                )
-                for order, near in enumerate(nears)
-            ],
-            axis=0,
-        )
-        denominator = jnp.sum(exponent, axis=1, keepdims=True)
-        numerator = jnp.dot(
-            exponent.astype(jnp.bfloat16), memory, preferred_element_type=jnp.float32
-        )
-        result = (numerator / denominator).astype(jnp.bfloat16)
-        for order, out_ref in enumerate(out_refs):
-            out_ref[first + index] = result[order * tokens : (order + 1) * tokens]
+    query = jnp.concatenate([query_ref[slot] for query_ref in query_refs], axis=0)
+    exponent = scaled_exp(across(query, memory))
+    exponent = jnp.concatenate(
+        [
+            jnp.where(
+                behind <= (device ^ near) * tokens,
+                exponent[order * tokens : (order + 1) * tokens],
+                0.0,
+            )
+            for order, near in enumerate(nears)
+        ],
+        axis=0,
+    )
+    denominator = jnp.sum(exponent, axis=1, keepdims=True)
+    numerator = jnp.dot(exponent.astype(jnp.bfloat16), memory, preferred_element_type=jnp.float32)
+    result = (numerator / denominator).astype(jnp.bfloat16)
+    for order, out_ref in enumerate(out_refs):
+        out_ref[out_ref.shape[0] - 1] = result[order * tokens : (order + 1) * tokens]
     for done_ref, out_ref in zip(done_refs, out_refs):
-        out_ref[:first] = done_ref[...]
-
-
-def attend(nears, memories, held, queries, done):
+        out_ref[: done_ref.shape[0]] = done_ref[...]
+
+
+def attend(nears, memory, slot, queries, done):
     tokens = queries[nears[0]].shape[1]
-    first = done[nears[0]].shape[0] if done else 0
-    operands = [*memories, *[queries[near] for near in nears]]
+    operands = [*memory, *[queries[near] for near in nears]]
     operands += [done[near] for near in nears] if done else []
-    shape = pltpu.VMEM((first + len(held), tokens, HDIM), jnp.bfloat16)
+    shape = pltpu.VMEM((2 if done else 1, tokens, HDIM), jnp.bfloat16)
     results = pl.pallas_call(
-        functools.partial(attend_kernel, nears, first, held), out_shape=[shape] * len(nears)
+        functools.partial(attend_kernel, nears, slot, len(memory)), out_shape=[shape] * len(nears)
     )(*[on_chip(value) for value in operands])
     return dict(zip(nears, results))
 
@@ -417,13 +416,16 @@
     queries = dict(zip(nears, queries))
     for near in nears[1:]:
         queries[near] = swapped(queries[near], near)
-    memory = short_attention(arrived, query_gain, key_gain)
-    far_memory = swapped(memory, far)
+    memory, lower, upper = short_attention(arrived, query_gain, key_gain)
+    far_lower = swapped(lower, far)
+    far_upper = lax.ppermute(upper, "seq", [(source, source + far) for source in range(far)])
     offsets, pieces = [], []
-    for kind, held in enumerate((memory, far_memory)):
-        peer_memory = swapped(held, PEER)
-        done = attend(nears, [held], (2 * kind,), queries, None)
-        done = attend(nears, [peer_memory], (2 * kind + 1,), queries, done)
+    for kind, held in enumerate(([memory], [far_lower, far_upper])):
+        peer_memory = []
+        for value in held:
+            peer_memory.append(swapped(value, PEER))
+        done = attend(nears, held, 2 * kind, queries, None)
+        done = attend(nears, peer_memory, 2 * kind + 1, queries, done)
         for near in nears:
             pieces.append(swapped(done[near], near) if near else done[near])
             offsets.append(near + kind * far)

time: 51.3 us -> 46.2 us (0.901)
  blocking collectives: 20.1 us -> 0 us
  starting transfers between devices: 12.6 us -> 23.6 us
  waiting for transfers between devices: 10.1 us -> 14.1 us
    all_to_all x1 -> x0, blocking collectives: 20.1 us -> none  [half_exchange(): lax.all_to_all(outgoing, 'seq', split_axis=0, concat_axis=0, tiled=True)]
    all_to_all x0 -> x1, waiting for transfers between devices: none -> 8.27 us  [half_exchange(): lax.all_to_all(outgoing, 'seq', split_axis=0, concat_axis=0, tiled=True)]
    all_to_all x0 -> x1, starting transfers between devices: none -> 7.4 us  [half_exchange(): lax.all_to_all(outgoing, 'seq', split_axis=0, concat_axis=0, tiled=True)]
    ppermute x12 -> x13, waiting for transfers between devices: 10.1 us -> 5.8 us  [swapped(): lax.ppermute(value, 'seq', [(source, source ^ offset) for source in range...]
    ppermute x0 -> x1, starting transfers between devices: none -> 3.51 us  [half_exchange(): lax.ppermute(upper, 'seq', [(source, source + far) for source in range(fa...]
    ppermute x12 -> x13, starting transfers between devices: 12.6 us -> 12.7 us  [swapped(): lax.ppermute(value, 'seq', [(source, source ^ offset) for source in range...]
  transfers between devices with their start and end apart: 12 -> 15, of which waited for: 6 -> 5; matrix products, arithmetic and copies ran while one was open for 0% -> 0% of each run, Pallas kernels for 7% -> 10%
where the time goes in v6:
time: 46.2 us; the launch traced here: 45.9 us
  starting transfers between devices  23.6 us (51%)
  waiting for transfers between devices  14.1 us (31%)
  Pallas kernels  8.13 us (18%)
    ppermute x13, starting transfers between devices, swapped(): lax.ppermute(value, 'seq', [(source, source ^ offset) for source in range...  12.7 us
    all_to_all x1, waiting for transfers between devices, half_exchange(): lax.all_to_all(outgoing, 'seq', split_axis=0, concat_axis=0, tiled=True)  8.27 us
    all_to_all x1, starting transfers between devices, half_exchange(): lax.all_to_all(outgoing, 'seq', split_axis=0, concat_axis=0, tiled=True)  7.4 us
    ppermute x13, waiting for transfers between devices, swapped(): lax.ppermute(value, 'seq', [(source, source ^ offset) for source in range...  5.8 us
    ppermute x1, starting transfers between devices, half_exchange(): lax.ppermute(upper, 'seq', [(source, source + far) for source in range(fa...  3.51 us
    pallas_call x1, Pallas kernels, pool_inputs(): pl.pallas_call(pool_kernel, in_specs=[pl.BlockSpec(memory_space=pl.ANY)]...  2.61 us
    pallas_call x4, Pallas kernels, attend(): pl.pallas_call(functools.partial(attend_kernel, nears, slot, len(memory))...  2.19 us
    pallas_call x1, Pallas kernels, norm_up(): pl.pallas_call(functools.partial(norm_kernel, shifts, nears), out_shape=[...  1.41 us
  transfers between devices with their start and end apart: 15, of which 5 were waited for; matrix products, arithmetic and copies ran while one was open for 0% of the time, Pallas kernels for 10%

profile of v6, /device:TPU:0, one launch (start us, length us, event | category | flops | bytes accessed | tf_op | source)
XLA Modules:
  0.0 45.9 jit_solution(10126625981804699203)
XLA Ops:
  0.0 2.6 %shard_map.73 = bf16[16,104,128]{2,1,0:T(8,128)(2,1)} custom-call(bf16[128,2048]{1,0:T(8,128)(2,1)} %refs_0_.1, bf16[128,2048]{1,0:T(8,128)(2,1)} %refs_1_.1, bf16[128,2048]{1,0:T(8,128)(2,1)} %refs_2_.1, f32[16,128]{1,0:T(8,128)} %bitcast.3, f32[16,128]{1,0:T(8,128)} %bitcast.5), custom_call_target="tpu_custom_call" | custom-call | tf_op jit(solution)/shard_map/pallas_call | solution.py:236
  2.6 7.4 %all-to-all-start = ((bf16[16,104,128]{2,1,0:T(8,128)(2,1)}), bf16[16,104,128]{2,1,0:T(8,128)(2,1)S(1)}, u32[]{:S(2)}, u32[]{:S(2)}) async-start(bf16[16,104,128]{2,1,0:T(8,128)(2,1)} %shard_map.73), calls=%async_computation | async-start | bytes 851968 | tf_op jit(solution)/shard_map/all_to_all | solution.py:414
  10.0 0.0 copy-start
  10.0 0.0 copy-start.1
  10.0 1.4 %shard_map.75 = (bf16[4,128,128]{2,1,0:T(8,128)(2,1)S(1)}, bf16[4,128,128]{2,1,0:T(8,128)(2,1)S(1)}, bf16[4,128,128]{2,1,0:T(8,128)(2,1)S(1)}, bf16[4,128,128]{2,1,0:T(8,128)(2,1)S(1)}) custom-call(bf16[128,2048]{1,0:T(8,128)(2,1)} %up_ref.1, f32[16,128]{1,0:T(8,128)} %bitcast.7), custom_call_target="tpu_custom_call" | custom-call | tf_op jit(solution)/shard_map/pallas_call | solution.py:330
  11.5 2.0 %collective-permute-start.1 = (bf16[4,128,128]{2,1,0:T(8,128)(2,1)S(1)}, bf16[4,128,128]{2,1,0:T(8,128)(2,1)S(1)}, u32[]{:S(2)}, u32[]{:S(2)}) collective-permute-start(bf16[4,128,128]{2,1,0:T(8,128)(2,1)S(1)} %get-tuple-element.30), channel_id=1, source_target_pairs={{0,2},{1,3},{2,0},{3,1},{4,6},{5,7},{6,4},{7,5},{8,10},{9,11},{10,... | collective-permute-start | bytes 393224 | tf_op jit(solution)/shard_map/ppermute | solution.py:407
  13.5 1.5 %collective-permute-start.2 = (bf16[4,128,128]{2,1,0:T(8,128)(2,1)S(1)}, bf16[4,128,128]{2,1,0:T(8,128)(2,1)S(1)}, u32[]{:S(2)}, u32[]{:S(2)}) collective-permute-start(bf16[4,128,128]{2,1,0:T(8,128)(2,1)S(1)} %get-tuple-element.31), channel_id=1, source_target_pairs={{0,4},{1,5},{2,6},{3,7},{4,0},{5,1},{6,2},{7,3},{8,12},{9,13},{10,... | collective-permute-start | bytes 393224 | tf_op jit(solution)/shard_map/ppermute | solution.py:407
  14.9 0.1 collective-permute-start.3
  15.0 8.3 %all-to-all-done.arrived_ref = bf16[16,104,128]{2,1,0:T(8,128)(2,1)S(1)} async-done(((bf16[16,104,128]{2,1,0:T(8,128)(2,1)}), bf16[16,104,128]{2,1,0:T(8,128)(2,1)S(1)}, u32[]{:S(2)}, u32[]{:S(2)}) %all-to-all-start) | async-done | bytes 426016 | tf_op jit(solution)/shard_map/all_to_all | solution.py:414
  23.3 0.0 copy-done
  23.3 0.0 copy-done.1
  23.3 1.0 %shard_map.74 = (bf16[512,128]{1,0:T(8,128)(2,1)S(1)}, bf16[256,128]{1,0:T(8,128)(2,1)S(1)}, bf16[256,128]{1,0:T(8,128)(2,1)S(1)}) custom-call(bf16[16,104,128]{2,1,0:T(8,128)(2,1)S(1)} %all-to-all-done.arrived_ref, f32[16,128]{1,0:T(8,128)S(1)} %bitcast.4, f32[16,128]{1,0:T(8,128)S(1)} %bitcast.6), custom_call_target="tpu_custom_call" | custom-call | tf_op jit(solution)/shard_map/pallas_call | solution.py:308
  24.3 0.1 collective-permute-start
  24.4 1.4 %collective-permute-start.7 = (bf16[256,128]{1,0:T(8,128)(2,1)S(1)}, bf16[256,128]{1,0:T(8,128)(2,1)S(1)}, u32[]{:S(2)}, u32[]{:S(2)}) collective-permute-start(bf16[256,128]{1,0:T(8,128)(2,1)S(1)} %get-tuple-element.41), channel_id=1, source_target_pairs={{0,8},{1,9},{2,10},{3,11},{4,12},{5,13},{6,14},{7,15},{8,0},{9,1},... | collective-permute-start | bytes 196616 | tf_op jit(solution)/shard_map/ppermute | solution.py:407
  25.8 0.0 collective-permute-done.1.refs_2_.refs_3_
  25.8 3.5 %collective-permute-start.9 = (bf16[256,128]{1,0:T(8,128)(2,1)S(1)}, bf16[256,128]{1,0:T(8,128)(2,1)S(1)}, u32[]{:S(2)}, u32[]{:S(2)}) collective-permute-start(bf16[256,128]{1,0:T(8,128)(2,1)S(1)} %get-tuple-element.42), channel_id=1, source_target_pairs={{0,8},{1,9},{2,10},{3,11},{4,12},{5,13},{6,14},{7,15},{16,24},{17,... | collective-permute-start | bytes 196616 | tf_op jit(solution)/shard_map/ppermute | solution.py:421
  29.3 1.9 %collective-permute-done.7.refs_0_ = bf16[256,128]{1,0:T(8,128)(2,1)S(1)} collective-permute-done((bf16[256,128]{1,0:T(8,128)(2,1)S(1)}, bf16[256,128]{1,0:T(8,128)(2,1)S(1)}, u32[]{:S(2)}, u32[]{:S(2)}) %collective-permute-start.7) | collective-permute-done | bytes 65568 | tf_op jit(solution)/shard_map/ppermute | solution.py:407
  31.2 0.1 collective-permute-start.8
  31.2 0.0 collective-permute-done.9.refs_1_
  31.3 0.4 collective-permute-start.10
  31.7 0.0 collective-permute-done.2.refs_3_.refs_4_
  31.7 0.0 collective-permute-done.3.refs_4_.refs_5_
  31.7 0.5 %shard_map.76 = (bf16[1,128,128]{2,1,0:T(8,128)(2,1)S(1)}, bf16[1,128,128]{2,1,0:T(8,128)(2,1)S(1)}, bf16[1,128,128]{2,1,0:T(8,128)(2,1)S(1)}, bf16[1,128,128]{2,1,0:T(8,128)(2,1)S(1)}) custom-call(bf16[512,128]{1,0:T(8,128)(2,1)S(1)} %get-tuple-element.28.refs_0_, bf16[4,128,128]{2,1,0:T(8,128)(2,1)S(1)} %get-tuple-element.29.refs_1_.refs_2_, ...), custom_call_target="tpu_custom_call" | custom-call | tf_op jit(solution)/shard_map/pallas_call | solution.py:373
  32.3 0.0 collective-permute-done.refs_0_
  32.3 0.5 %shard_map.77 = (bf16[2,128,128]{2,1,0:T(8,128)(2,1)S(1)}, bf16[2,128,128]{2,1,0:T(8,128)(2,1)S(1)}, bf16[2,128,128]{2,1,0:T(8,128)(2,1)S(1)}, bf16[2,128,128]{2,1,0:T(8,128)(2,1)S(1)}) custom-call(bf16[512,128]{1,0:T(8,128)(2,1)S(1)} %collective-permute-done.refs_0_, bf16[4,128,128]{2,1,0:T(8,128)(2,1)S(1)} %get-tuple-element.29.refs_1_.refs_2_, ...), custom_call_target="tpu_custom_call" | custom-call | tf_op jit(solution)/shard_map/pallas_call | solution.py:373
  32.8 0.4 collective-permute-start.4
  33.2 0.5 %shard_map.78 = (bf16[1,128,128]{2,1,0:T(8,128)(2,1)S(1)}, bf16[1,128,128]{2,1,0:T(8,128)(2,1)S(1)}, bf16[1,128,128]{2,1,0:T(8,128)(2,1)S(1)}, bf16[1,128,128]{2,1,0:T(8,128)(2,1)S(1)}) custom-call(bf16[256,128]{1,0:T(8,128)(2,1)S(1)} %collective-permute-done.7.refs_0_, bf16[256,128]{1,0:T(8,128)(2,1)S(1)} %collective-permute-done.9.refs_1_, ...), custom_call_target="tpu_custom_call" | custom-call | tf_op jit(solution)/shard_map/pallas_call | solution.py:373
  33.7 2.0 %collective-permute-start.5 = (bf16[2,128,128]{2,1,0:T(8,128)(2,1)S(1)}, bf16[2,128,128]{2,1,0:T(8,128)(2,1)S(1)}, u32[]{:S(2)}, u32[]{:S(2)}) collective-permute-start(bf16[2,128,128]{2,1,0:T(8,128)(2,1)S(1)} %get-tuple-element.39), channel_id=1, source_target_pairs={{0,4},{1,5},{2,6},{3,7},{4,0},{5,1},{6,2},{7,3},{8,12},{9,13},{10,... | collective-permute-start | bytes 196616 | tf_op jit(solution)/shard_map/ppermute | solution.py:407
  35.7 1.3 %collective-permute-start.6 = (bf16[2,128,128]{2,1,0:T(8,128)(2,1)S(1)}, bf16[2,128,128]{2,1,0:T(8,128)(2,1)S(1)}, u32[]{:S(2)}, u32[]{:S(2)}) collective-permute-start(bf16[2,128,128]{2,1,0:T(8,128)(2,1)S(1)} %get-tuple-element.40), channel_id=1, source_target_pairs={{0,6},{1,7},{2,4},{3,5},{4,2},{5,3},{6,0},{7,1},{8,14},{9,15},{10,... | collective-permute-start | bytes 196616 | tf_op jit(solution)/shard_map/ppermute | solution.py:407
  37.0 0.0 collective-permute-done.8.refs_0_
  37.0 0.0 collective-permute-done.10.refs_1_
  37.0 0.5 %shard_map.79 = (bf16[2,128,128]{2,1,0:T(8,128)(2,1)S(1)}, bf16[2,128,128]{2,1,0:T(8,128)(2,1)S(1)}, bf16[2,128,128]{2,1,0:T(8,128)(2,1)S(1)}, bf16[2,128,128]{2,1,0:T(8,128)(2,1)S(1)}) custom-call(bf16[256,128]{1,0:T(8,128)(2,1)S(1)} %collective-permute-done.8.refs_0_, bf16[256,128]{1,0:T(8,128)(2,1)S(1)} %collective-permute-done.10.refs_1_, ...), custom_call_target="tpu_custom_call" | custom-call | tf_op jit(solution)/shard_map/pallas_call | solution.py:373
  37.5 0.4 collective-permute-start.11
  37.9 1.9 %collective-permute-start.12 = (bf16[2,128,128]{2,1,0:T(8,128)(2,1)S(1)}, bf16[2,128,128]{2,1,0:T(8,128)(2,1)S(1)}, u32[]{:S(2)}, u32[]{:S(2)}) collective-permute-start(bf16[2,128,128]{2,1,0:T(8,128)(2,1)S(1)} %get-tuple-element.49), channel_id=1, source_target_pairs={{0,4},{1,5},{2,6},{3,7},{4,0},{5,1},{6,2},{7,3},{8,12},{9,13},{10,... | collective-permute-start | bytes 196616 | tf_op jit(solution)/shard_map/ppermute | solution.py:407
  39.8 0.0 collective-permute-done.4.refs_1_
  39.8 1.3 %collective-permute-start.13 = (bf16[2,128,128]{2,1,0:T(8,128)(2,1)S(1)}, bf16[2,128,128]{2,1,0:T(8,128)(2,1)S(1)}, u32[]{:S(2)}, u32[]{:S(2)}) collective-permute-start(bf16[2,128,128]{2,1,0:T(8,128)(2,1)S(1)} %get-tuple-element.50), channel_id=1, source_target_pairs={{0,6},{1,7},{2,4},{3,5},{4,2},{5,3},{6,0},{7,1},{8,14},{9,15},{10,... | collective-permute-start | bytes 196616 | tf_op jit(solution)/shard_map/ppermute | solution.py:407
  41.1 0.0 collective-permute-done.5.refs_2_
  41.1 0.0 collective-permute-done.6.refs_3_
  41.1 0.9 %collective-permute-done.11.refs_5_ = bf16[2,128,128]{2,1,0:T(8,128)(2,1)S(1)} collective-permute-done((bf16[2,128,128]{2,1,0:T(8,128)(2,1)S(1)}, bf16[2,128,128]{2,1,0:T(8,128)(2,1)S(1)}, u32[]{:S(2)}, u32[]{:S(2)}) %collective-permute-start.11) | collective-permute-done | bytes 65568 | tf_op jit(solution)/shard_map/ppermute | solution.py:407
  42.0 0.1 collective-permute-done.12.refs_6_
  42.2 2.8 %collective-permute-done.13.refs_7_ = bf16[2,128,128]{2,1,0:T(8,128)(2,1)S(1)} collective-permute-done((bf16[2,128,128]{2,1,0:T(8,128)(2,1)S(1)}, bf16[2,128,128]{2,1,0:T(8,128)(2,1)S(1)}, u32[]{:S(2)}, u32[]{:S(2)}) %collective-permute-start.13) | collective-permute-done | bytes 65568 | tf_op jit(solution)/shard_map/ppermute | solution.py:407
  45.0 0.9 %shard_map.80 = bf16[128,2048]{1,0:T(8,128)(2,1)} custom-call(bf16[2,128,128]{2,1,0:T(8,128)(2,1)S(1)} %get-tuple-element.37.refs_0_, bf16[2,128,128]{2,1,0:T(8,128)(2,1)S(1)} %collective-permute-done.4.refs_1_, bf16[2,128,128]{2,1,0:T(8,128)(2,1)S(1)} %collective-permute-done.5.refs_2_, bf16[2,128,128]{2,1,0:T(8,128)(2,1)S(1)} %collective-permute-done.6.refs_3_, ...), custom_call_target="tpu_custom_call" | custom-call | tf_op jit(solution)/shard_map/pallas_call | solution.py:397
Async XLA Ops:
  2.6 20.7 %all-to-all-start = ((bf16[16,104,128]{2,1,0:T(8,128)(2,1)}), bf16[16,104,128]{2,1,0:T(8,128)(2,1)S(1)}, u32[]{:S(2)}, u32[]{:S(2)}) async-start(bf16[16,104,128]{2,1,0:T(8,128)(2,1)} %shard_map.73), calls=%async_computation | async-start | bytes 851968 | tf_op jit(solution)/shard_map/all_to_all | solution.py:414
  10.0 13.3 %copy-start = (f32[2048]{0:T(1024)S(1)}, f32[2048]{0:T(1024)}, u32[]{:S(2)}) copy-start(f32[2048]{0:T(1024)} %param.11) | copy-start | bytes 24580
  10.0 13.3 %copy-start.1 = (f32[2048]{0:T(1024)S(1)}, f32[2048]{0:T(1024)}, u32[]{:S(2)}) copy-start(f32[2048]{0:T(1024)} %param.12) | copy-start | bytes 24580
  11.5 14.3 %collective-permute-start.1 = (bf16[4,128,128]{2,1,0:T(8,128)(2,1)S(1)}, bf16[4,128,128]{2,1,0:T(8,128)(2,1)S(1)}, u32[]{:S(2)}, u32[]{:S(2)}) collective-permute-start(bf16[4,128,128]{2,1,0:T(8,128)(2,1)S(1)} %get-tuple-element.30), channel_id=1, source_target_pairs={{0,2},{1,3},{2,0},{3,1},{4,6},{5,7},{6,4},{7,5},{8,10},{9,11},{10,... | collective-permute-start | bytes 393224 | tf_op jit(solution)/shard_map/ppermute | solution.py:407
  13.5 18.2 %collective-permute-start.2 = (bf16[4,128,128]{2,1,0:T(8,128)(2,1)S(1)}, bf16[4,128,128]{2,1,0:T(8,128)(2,1)S(1)}, u32[]{:S(2)}, u32[]{:S(2)}) collective-permute-start(bf16[4,128,128]{2,1,0:T(8,128)(2,1)S(1)} %get-tuple-element.31), channel_id=1, source_target_pairs={{0,4},{1,5},{2,6},{3,7},{4,0},{5,1},{6,2},{7,3},{8,12},{9,13},{10,... | collective-permute-start | bytes 393224 | tf_op jit(solution)/shard_map/ppermute | solution.py:407
  14.9 16.8 %collective-permute-start.3 = (bf16[4,128,128]{2,1,0:T(8,128)(2,1)S(1)}, bf16[4,128,128]{2,1,0:T(8,128)(2,1)S(1)}, u32[]{:S(2)}, u32[]{:S(2)}) collective-permute-start(bf16[4,128,128]{2,1,0:T(8,128)(2,1)S(1)} %get-tuple-element.32), channel_id=1, source_target_pairs={{0,6},{1,7},{2,4},{3,5},{4,2},{5,3},{6,0},{7,1},{8,14},{9,15},{10,... | collective-permute-start | bytes 393224 | tf_op jit(solution)/shard_map/ppermute | solution.py:407
  24.3 7.9 %collective-permute-start = (bf16[512,128]{1,0:T(8,128)(2,1)S(1)}, bf16[512,128]{1,0:T(8,128)(2,1)S(1)}, u32[]{:S(2)}, u32[]{:S(2)}) collective-permute-start(bf16[512,128]{1,0:T(8,128)(2,1)S(1)} %get-tuple-element.28.refs_0_), channel_id=1, source_target_pairs={{0,1},{1,0},{2,3},{3,2},{4,5},{5,4},{6,7},{7,6},{8,9},{9,8},{10,11... | collective-permute-start | bytes 393224 | tf_op jit(solution)/shard_map/ppermute | solution.py:407
  24.4 6.8 %collective-permute-start.7 = (bf16[256,128]{1,0:T(8,128)(2,1)S(1)}, bf16[256,128]{1,0:T(8,128)(2,1)S(1)}, u32[]{:S(2)}, u32[]{:S(2)}) collective-permute-start(bf16[256,128]{1,0:T(8,128)(2,1)S(1)} %get-tuple-element.41), channel_id=1, source_target_pairs={{0,8},{1,9},{2,10},{3,11},{4,12},{5,13},{6,14},{7,15},{8,0},{9,1},... | collective-permute-start | bytes 196616 | tf_op jit(solution)/shard_map/ppermute | solution.py:407
  25.8 5.5 %collective-permute-start.9 = (bf16[256,128]{1,0:T(8,128)(2,1)S(1)}, bf16[256,128]{1,0:T(8,128)(2,1)S(1)}, u32[]{:S(2)}, u32[]{:S(2)}) collective-permute-start(bf16[256,128]{1,0:T(8,128)(2,1)S(1)} %get-tuple-element.42), channel_id=1, source_target_pairs={{0,8},{1,9},{2,10},{3,11},{4,12},{5,13},{6,14},{7,15},{16,24},{17,... | collective-permute-start | bytes 196616 | tf_op jit(solution)/shard_map/ppermute | solution.py:421
  31.2 5.8 %collective-permute-start.8 = (bf16[256,128]{1,0:T(8,128)(2,1)S(1)}, bf16[256,128]{1,0:T(8,128)(2,1)S(1)}, u32[]{:S(2)}, u32[]{:S(2)}) collective-permute-start(bf16[256,128]{1,0:T(8,128)(2,1)S(1)} %collective-permute-done.7.refs_0_), channel_id=1, source_target_pairs={{0,1},{1,0},{2,3},{3,2},{4,5},{5,4},{6,7},{7,6},{8,9},{9,8},{10,11... | collective-permute-start | bytes 196616 | tf_op jit(solution)/shard_map/ppermute | solution.py:407
  31.3 5.7 %collective-permute-start.10 = (bf16[256,128]{1,0:T(8,128)(2,1)S(1)}, bf16[256,128]{1,0:T(8,128)(2,1)S(1)}, u32[]{:S(2)}, u32[]{:S(2)}) collective-permute-start(bf16[256,128]{1,0:T(8,128)(2,1)S(1)} %collective-permute-done.9.refs_1_), channel_id=1, source_target_pairs={{0,1},{1,0},{2,3},{3,2},{4,5},{5,4},{6,7},{7,6},{8,9},{9,8},{10,11... | collective-permute-start | bytes 196616 | tf_op jit(solution)/shard_map/ppermute | solution.py:407
  32.8 7.0 %collective-permute-start.4 = (bf16[2,128,128]{2,1,0:T(8,128)(2,1)S(1)}, bf16[2,128,128]{2,1,0:T(8,128)(2,1)S(1)}, u32[]{:S(2)}, u32[]{:S(2)}) collective-permute-start(bf16[2,128,128]{2,1,0:T(8,128)(2,1)S(1)} %get-tuple-element.38), channel_id=1, source_target_pairs={{0,2},{1,3},{2,0},{3,1},{4,6},{5,7},{6,4},{7,5},{8,10},{9,11},{10,... | collective-permute-start | bytes 196616 | tf_op jit(solution)/shard_map/ppermute | solution.py:407
  33.7 7.4 %collective-permute-start.5 = (bf16[2,128,128]{2,1,0:T(8,128)(2,1)S(1)}, bf16[2,128,128]{2,1,0:T(8,128)(2,1)S(1)}, u32[]{:S(2)}, u32[]{:S(2)}) collective-permute-start(bf16[2,128,128]{2,1,0:T(8,128)(2,1)S(1)} %get-tuple-element.39), channel_id=1, source_target_pairs={{0,4},{1,5},{2,6},{3,7},{4,0},{5,1},{6,2},{7,3},{8,12},{9,13},{10,... | collective-permute-start | bytes 196616 | tf_op jit(solution)/shard_map/ppermute | solution.py:407
  35.7 5.4 %collective-permute-start.6 = (bf16[2,128,128]{2,1,0:T(8,128)(2,1)S(1)}, bf16[2,128,128]{2,1,0:T(8,128)(2,1)S(1)}, u32[]{:S(2)}, u32[]{:S(2)}) collective-permute-start(bf16[2,128,128]{2,1,0:T(8,128)(2,1)S(1)} %get-tuple-element.40), channel_id=1, source_target_pairs={{0,6},{1,7},{2,4},{3,5},{4,2},{5,3},{6,0},{7,1},{8,14},{9,15},{10,... | collective-permute-start | bytes 196616 | tf_op jit(solution)/shard_map/ppermute | solution.py:407
  37.5 4.5 %collective-permute-start.11 = (bf16[2,128,128]{2,1,0:T(8,128)(2,1)S(1)}, bf16[2,128,128]{2,1,0:T(8,128)(2,1)S(1)}, u32[]{:S(2)}, u32[]{:S(2)}) collective-permute-start(bf16[2,128,128]{2,1,0:T(8,128)(2,1)S(1)} %get-tuple-element.48), channel_id=1, source_target_pairs={{0,2},{1,3},{2,0},{3,1},{4,6},{5,7},{6,4},{7,5},{8,10},{9,11},{10,... | collective-permute-start | bytes 196616 | tf_op jit(solution)/shard_map/ppermute | solution.py:407
  37.9 4.3 %collective-permute-start.12 = (bf16[2,128,128]{2,1,0:T(8,128)(2,1)S(1)}, bf16[2,128,128]{2,1,0:T(8,128)(2,1)S(1)}, u32[]{:S(2)}, u32[]{:S(2)}) collective-permute-start(bf16[2,128,128]{2,1,0:T(8,128)(2,1)S(1)} %get-tuple-element.49), channel_id=1, source_target_pairs={{0,4},{1,5},{2,6},{3,7},{4,0},{5,1},{6,2},{7,3},{8,12},{9,13},{10,... | collective-permute-start | bytes 196616 | tf_op jit(solution)/shard_map/ppermute | solution.py:407
  39.8 5.2 %collective-permute-start.13 = (bf16[2,128,128]{2,1,0:T(8,128)(2,1)S(1)}, bf16[2,128,128]{2,1,0:T(8,128)(2,1)S(1)}, u32[]{:S(2)}, u32[]{:S(2)}) collective-permute-start(bf16[2,128,128]{2,1,0:T(8,128)(2,1)S(1)} %get-tuple-element.50), channel_id=1, source_target_pairs={{0,6},{1,7},{2,4},{3,5},{4,2},{5,3},{6,0},{7,1},{8,14},{9,15},{10,... | collective-permute-start | bytes 196616 | tf_op jit(solution)/shard_map/ppermute | solution.py:407

commit v7 on v5

--- a/solution.py
+++ b/solution.py
@@ -314,7 +314,7 @@
     device = lax.axis_index("seq")
     for near, out_ref in zip(nears, out_refs):
         for index, shift in enumerate(shifts):
-            head = device ^ (near + shift)
+            head = device ^ near ^ shift
             columns = pl.ds(pl.multiple_of(head * HDIM, HDIM), HDIM)
             query = rms_rows(up_ref[:, columns].astype(jnp.float32)) * gain_ref[pl.ds(head, 1), :]
             out_ref[index] = query.astype(jnp.bfloat16)
@@ -328,19 +328,18 @@
     )(up_query, up_gain.reshape(-1, HDIM))
 
 
-def attend_kernel(nears, first, held, *refs):
+def attend_kernel(nears, slot, *refs):
     count = len(nears)
-    memory_refs, refs = refs[: len(held)], refs[len(held) :]
-    query_refs, out_refs = refs[:count], refs[-count:]
-    done_refs = refs[count:-count]
+    memory_ref, query_refs, refs = refs[0], refs[1 : count + 1], refs[count + 1 :]
+    done_refs, out_refs = refs[:-count], refs[-count:]
     tokens = query_refs[0].shape[1]
-    row_total = memory_refs[0].shape[0]
+    row_total = memory_ref.shape[0]
     device = lax.axis_index("seq")
-    token = lax.broadcasted_iota(jnp.int32, (tokens, row_total), 0)
-    column = SHORT * lax.broadcasted_iota(jnp.int32, (tokens, row_total), 1)
-    behind = column - token
-    for index, (memory_ref, slot) in enumerate(zip(memory_refs, held)):
-        memory = memory_ref[...]
+
+    def attend_rows(rows):
+        memory = memory_ref[:rows]
+        token = lax.broadcasted_iota(jnp.int32, (tokens, rows), 0)
+        behind = SHORT * lax.broadcasted_iota(jnp.int32, (tokens, rows), 1) - token
         query = jnp.concatenate([query_ref[slot] for query_ref in query_refs], axis=0)
         exponent = scaled_exp(across(query, memory))
         exponent = jnp.concatenate(
@@ -360,19 +359,27 @@
         )
         result = (numerator / denominator).astype(jnp.bfloat16)
         for order, out_ref in enumerate(out_refs):
-            out_ref[first + index] = result[order * tokens : (order + 1) * tokens]
+            out_ref[out_ref.shape[0] - 1] = result[order * tokens : (order + 1) * tokens]
+
+    @pl.when(device < HEADS // 2)
+    def _():
+        attend_rows(row_total // 2)
+
+    @pl.when(device >= HEADS // 2)
+    def _():
+        attend_rows(row_total)
+
     for done_ref, out_ref in zip(done_refs, out_refs):
-        out_ref[:first] = done_ref[...]
-
-
-def attend(nears, memories, held, queries, done):
+        out_ref[: done_ref.shape[0]] = done_ref[...]
+
+
+def attend(nears, memory, slot, queries, done):
     tokens = queries[nears[0]].shape[1]
-    first = done[nears[0]].shape[0] if done else 0
-    operands = [*memories, *[queries[near] for near in nears]]
+    operands = [memory, *[queries[near] for near in nears]]
     operands += [done[near] for near in nears] if done else []
-    shape = pltpu.VMEM((first + len(held), tokens, HDIM), jnp.bfloat16)
+    shape = pltpu.VMEM((2 if done else 1, tokens, HDIM), jnp.bfloat16)
     results = pl.pallas_call(
-        functools.partial(attend_kernel, nears, first, held), out_shape=[shape] * len(nears)
+        functools.partial(attend_kernel, nears, slot), out_shape=[shape] * len(nears)
     )(*[on_chip(value) for value in operands])
     return dict(zip(nears, results))
 
@@ -383,7 +390,7 @@
     copies = []
     for number, (offset, piece_ref) in enumerate(zip(offsets, piece_refs)):
         for flip in (0, PEER):
-            head = device ^ (offset + flip)
+            head = device ^ offset ^ flip
             columns = pl.ds(pl.multiple_of(head * HDIM, HDIM), HDIM)
             copy = pltpu.make_async_copy(
                 piece_ref.at[flip], out_hbm.at[:, columns], sems.at[2 * number + flip]
@@ -409,11 +416,11 @@
 
 
 def half_exchange(query_src, key_src, value_src, up_query, query_gain, key_gain, up_gain):
-    far = HEADS // 2
-    nears = tuple(range(0, far, 2))
+    far = HEADS // 2 + HEADS // 4
+    nears = tuple(range(0, HEADS // 2, 2))
     outgoing = pool_inputs(query_src, key_src, value_src, query_gain, key_gain)
     arrived = lax.all_to_all(outgoing, "seq", split_axis=0, concat_axis=0, tiled=True)
-    queries = norm_up(up_query, up_gain, (0, PEER, far, far + PEER), nears)
+    queries = norm_up(up_query, up_gain, (0, PEER, far, far ^ PEER), nears)
     queries = dict(zip(nears, queries))
     for near in nears[1:]:
         queries[near] = swapped(queries[near], near)
@@ -422,11 +429,11 @@
     offsets, pieces = [], []
     for kind, held in enumerate((memory, far_memory)):
         peer_memory = swapped(held, PEER)
-        done = attend(nears, [held], (2 * kind,), queries, None)
-        done = attend(nears, [peer_memory], (2 * kind + 1,), queries, done)
+        done = attend(nears, held, 2 * kind, queries, None)
+        done = attend(nears, peer_memory, 2 * kind + 1, queries, done)
         for near in nears:
             pieces.append(swapped(done[near], near) if near else done[near])
-            offsets.append(near + kind * far)
+            offsets.append(near ^ (kind * far))
     return place(tuple(offsets), pieces)
 
 

time: 51.3 us -> 50.3 us (0.981)
  starting transfers between devices: 12.6 us -> 12 us
  Pallas kernels: 8.12 us -> 7.59 us
    ppermute x12, starting transfers between devices: 12.6 us -> 12 us  [swapped(): lax.ppermute(value, 'seq', [(source, source ^ offset) for source in range...]
    pallas_call x4, Pallas kernels: 2.19 us -> 1.66 us  [attend(): pl.pallas_call(functools.partial(attend_kernel, nears, slot), out_shape=[...]
  transfers between devices with their start and end apart: 12 -> 12, of which waited for: 6 -> 7; matrix products, arithmetic and copies ran while one was open for 0% -> 0% of each run, Pallas kernels for 7% -> 6%
where the time goes in v7:
time: 50.3 us; the launch traced here: 50 us
  blocking collectives  20.1 us (40%)
  starting transfers between devices  12 us (24%)
  waiting for transfers between devices  10.2 us (20%)
  Pallas kernels  7.59 us (15%)
    all_to_all x1, blocking collectives, half_exchange(): lax.all_to_all(outgoing, 'seq', split_axis=0, concat_axis=0, tiled=True)  20.1 us
    ppermute x12, starting transfers between devices, swapped(): lax.ppermute(value, 'seq', [(source, source ^ offset) for source in range...  12 us
    ppermute x12, waiting for transfers between devices, swapped(): lax.ppermute(value, 'seq', [(source, source ^ offset) for source in range...  10.2 us
    pallas_call x1, Pallas kernels, pool_inputs(): pl.pallas_call(pool_kernel, in_specs=[pl.BlockSpec(memory_space=pl.ANY)]...  2.61 us
    pallas_call x4, Pallas kernels, attend(): pl.pallas_call(functools.partial(attend_kernel, nears, slot), out_shape=[...  1.66 us
    pallas_call x1, Pallas kernels, norm_up(): pl.pallas_call(functools.partial(norm_kernel, shifts, nears), out_shape=[...  1.4 us
  transfers between devices with their start and end apart: 12, of which 7 were waited for; matrix products, arithmetic and copies ran while one was open for 0% of the time, Pallas kernels for 6%

profile of v7, /device:TPU:0, one launch (start us, length us, event | category | flops | bytes accessed | tf_op | source)
XLA Modules:
  0.0 50.0 jit_solution(17329445237909351027)
XLA Ops:
  0.0 2.6 %shard_map.73 = bf16[16,104,128]{2,1,0:T(8,128)(2,1)} custom-call(bf16[128,2048]{1,0:T(8,128)(2,1)} %refs_0_.1, bf16[128,2048]{1,0:T(8,128)(2,1)} %refs_1_.1, bf16[128,2048]{1,0:T(8,128)(2,1)} %refs_2_.1, f32[16,128]{1,0:T(8,128)} %bitcast.3, f32[16,128]{1,0:T(8,128)} %bitcast.5), custom_call_target="tpu_custom_call" | custom-call | tf_op jit(solution)/shard_map/pallas_call | solution.py:236
  2.6 0.0 copy-start
  2.6 0.0 copy-start.1
  2.6 20.1 %all_to_all.5.arrived_ref = bf16[16,104,128]{2,1,0:T(8,128)(2,1)S(1)} all-to-all(bf16[16,104,128]{2,1,0:T(8,128)(2,1)} %shard_map.73), channel_id=1, replica_groups=mesh['groups'=2,'seq'=16] {'seq'}, dimensions={0} | all-to-all | bytes 851968 | tf_op jit(solution)/shard_map/all_to_all | solution.py:422
  22.7 0.0 copy-done
  22.7 0.0 copy-done.1
  22.7 1.0 %shard_map.74.refs_0_ = bf16[512,128]{1,0:T(8,128)(2,1)S(1)} custom-call(bf16[16,104,128]{2,1,0:T(8,128)(2,1)S(1)} %all_to_all.5.arrived_ref, f32[16,128]{1,0:T(8,128)S(1)} %bitcast.4, f32[16,128]{1,0:T(8,128)S(1)} %bitcast.6), custom_call_target="tpu_custom_call" | custom-call | tf_op jit(solution)/shard_map/pallas_call | solution.py:307
  23.7 1.3 %collective-permute-start.7 = (bf16[512,128]{1,0:T(8,128)(2,1)S(1)}, bf16[512,128]{1,0:T(8,128)(2,1)S(1)}, u32[]{:S(2)}, u32[]{:S(2)}) collective-permute-start(bf16[512,128]{1,0:T(8,128)(2,1)S(1)} %shard_map.74.refs_0_), channel_id=1, source_target_pairs={{0,12},{1,13},{2,14},{3,15},{4,8},{5,9},{6,10},{7,11},{8,4},{9,5},... | collective-permute-start | bytes 393224 | tf_op jit(solution)/shard_map/ppermute | solution.py:415
  25.1 1.4 %shard_map.75 = (bf16[4,128,128]{2,1,0:T(8,128)(2,1)S(1)}, bf16[4,128,128]{2,1,0:T(8,128)(2,1)S(1)}, bf16[4,128,128]{2,1,0:T(8,128)(2,1)S(1)}, bf16[4,128,128]{2,1,0:T(8,128)(2,1)S(1)}) custom-call(bf16[128,2048]{1,0:T(8,128)(2,1)} %up_ref.1, f32[16,128]{1,0:T(8,128)} %bitcast.7), custom_call_target="tpu_custom_call" | custom-call | tf_op jit(solution)/shard_map/pallas_call | solution.py:326
  26.5 1.6 %collective-permute-start.1 = (bf16[4,128,128]{2,1,0:T(8,128)(2,1)S(1)}, bf16[4,128,128]{2,1,0:T(8,128)(2,1)S(1)}, u32[]{:S(2)}, u32[]{:S(2)}) collective-permute-start(bf16[4,128,128]{2,1,0:T(8,128)(2,1)S(1)} %get-tuple-element.26), channel_id=1, source_target_pairs={{0,2},{1,3},{2,0},{3,1},{4,6},{5,7},{6,4},{7,5},{8,10},{9,11},{10,... | collective-permute-start | bytes 393224 | tf_op jit(solution)/shard_map/ppermute | solution.py:415
  28.1 0.0 collective-permute-start.2
  28.1 2.0 %collective-permute-start.3 = (bf16[4,128,128]{2,1,0:T(8,128)(2,1)S(1)}, bf16[4,128,128]{2,1,0:T(8,128)(2,1)S(1)}, u32[]{:S(2)}, u32[]{:S(2)}) collective-permute-start(bf16[4,128,128]{2,1,0:T(8,128)(2,1)S(1)} %get-tuple-element.28), channel_id=1, source_target_pairs={{0,6},{1,7},{2,4},{3,5},{4,2},{5,3},{6,0},{7,1},{8,14},{9,15},{10,... | collective-permute-start | bytes 393224 | tf_op jit(solution)/shard_map/ppermute | solution.py:415
  30.0 0.0 collective-permute-start
  30.0 1.7 %collective-permute-done.7.refs_0_ = bf16[512,128]{1,0:T(8,128)(2,1)S(1)} collective-permute-done((bf16[512,128]{1,0:T(8,128)(2,1)S(1)}, bf16[512,128]{1,0:T(8,128)(2,1)S(1)}, u32[]{:S(2)}, u32[]{:S(2)}) %collective-permute-start.7) | collective-permute-done | bytes 131104 | tf_op jit(solution)/shard_map/ppermute | solution.py:415
  31.8 0.0 collective-permute-start.8
  31.8 0.5 collective-permute-done.1.refs_2_
  32.3 2.3 %collective-permute-done.2.refs_3_ = bf16[4,128,128]{2,1,0:T(8,128)(2,1)S(1)} collective-permute-done((bf16[4,128,128]{2,1,0:T(8,128)(2,1)S(1)}, bf16[4,128,128]{2,1,0:T(8,128)(2,1)S(1)}, u32[]{:S(2)}, u32[]{:S(2)}) %collective-permute-start.2) | collective-permute-done | bytes 131104 | tf_op jit(solution)/shard_map/ppermute | solution.py:415
  34.5 2.8 %collective-permute-done.3.refs_4_ = bf16[4,128,128]{2,1,0:T(8,128)(2,1)S(1)} collective-permute-done((bf16[4,128,128]{2,1,0:T(8,128)(2,1)S(1)}, bf16[4,128,128]{2,1,0:T(8,128)(2,1)S(1)}, u32[]{:S(2)}, u32[]{:S(2)}) %collective-permute-start.3) | collective-permute-done | bytes 131104 | tf_op jit(solution)/shard_map/ppermute | solution.py:415
  37.3 0.4 shard_map.76
  37.7 0.0 collective-permute-done.refs_0_
  37.7 0.4 shard_map.77
  38.2 1.1 %collective-permute-start.4 = (bf16[2,128,128]{2,1,0:T(8,128)(2,1)S(1)}, bf16[2,128,128]{2,1,0:T(8,128)(2,1)S(1)}, u32[]{:S(2)}, u32[]{:S(2)}) collective-permute-start(bf16[2,128,128]{2,1,0:T(8,128)(2,1)S(1)} %get-tuple-element.34), channel_id=1, source_target_pairs={{0,2},{1,3},{2,0},{3,1},{4,6},{5,7},{6,4},{7,5},{8,10},{9,11},{10,... | collective-permute-start | bytes 196616 | tf_op jit(solution)/shard_map/ppermute | solution.py:415
  39.2 0.0 collective-permute-start.5
  39.2 2.5 %collective-permute-start.6 = (bf16[2,128,128]{2,1,0:T(8,128)(2,1)S(1)}, bf16[2,128,128]{2,1,0:T(8,128)(2,1)S(1)}, u32[]{:S(2)}, u32[]{:S(2)}) collective-permute-start(bf16[2,128,128]{2,1,0:T(8,128)(2,1)S(1)} %get-tuple-element.36), channel_id=1, source_target_pairs={{0,6},{1,7},{2,4},{3,5},{4,2},{5,3},{6,0},{7,1},{8,14},{9,15},{10,... | collective-permute-start | bytes 196616 | tf_op jit(solution)/shard_map/ppermute | solution.py:415
  41.7 0.4 shard_map.78
  42.1 0.0 collective-permute-done.8.refs_0_
  42.1 0.4 shard_map.79
  42.6 1.1 %collective-permute-start.9 = (bf16[2,128,128]{2,1,0:T(8,128)(2,1)S(1)}, bf16[2,128,128]{2,1,0:T(8,128)(2,1)S(1)}, u32[]{:S(2)}, u32[]{:S(2)}) collective-permute-start(bf16[2,128,128]{2,1,0:T(8,128)(2,1)S(1)} %get-tuple-element.42), channel_id=1, source_target_pairs={{0,2},{1,3},{2,0},{3,1},{4,6},{5,7},{6,4},{7,5},{8,10},{9,11},{10,... | collective-permute-start | bytes 196616 | tf_op jit(solution)/shard_map/ppermute | solution.py:415
  43.6 0.0 collective-permute-start.10
  43.6 0.0 collective-permute-done.4.refs_1_
  43.6 2.5 %collective-permute-start.11 = (bf16[2,128,128]{2,1,0:T(8,128)(2,1)S(1)}, bf16[2,128,128]{2,1,0:T(8,128)(2,1)S(1)}, u32[]{:S(2)}, u32[]{:S(2)}) collective-permute-start(bf16[2,128,128]{2,1,0:T(8,128)(2,1)S(1)} %get-tuple-element.44), channel_id=1, source_target_pairs={{0,6},{1,7},{2,4},{3,5},{4,2},{5,3},{6,0},{7,1},{8,14},{9,15},{10,... | collective-permute-start | bytes 196616 | tf_op jit(solution)/shard_map/ppermute | solution.py:415
  46.1 0.0 collective-permute-done.5.refs_2_
  46.1 0.0 collective-permute-done.6.refs_3_
  46.1 1.5 %collective-permute-done.9.refs_5_ = bf16[2,128,128]{2,1,0:T(8,128)(2,1)S(1)} collective-permute-done((bf16[2,128,128]{2,1,0:T(8,128)(2,1)S(1)}, bf16[2,128,128]{2,1,0:T(8,128)(2,1)S(1)}, u32[]{:S(2)}, u32[]{:S(2)}) %collective-permute-start.9) | collective-permute-done | bytes 65568 | tf_op jit(solution)/shard_map/ppermute | solution.py:415
  47.6 0.3 collective-permute-done.10.refs_6_
  47.9 1.2 %collective-permute-done.11.refs_7_ = bf16[2,128,128]{2,1,0:T(8,128)(2,1)S(1)} collective-permute-done((bf16[2,128,128]{2,1,0:T(8,128)(2,1)S(1)}, bf16[2,128,128]{2,1,0:T(8,128)(2,1)S(1)}, u32[]{:S(2)}, u32[]{:S(2)}) %collective-permute-start.11) | collective-permute-done | bytes 65568 | tf_op jit(solution)/shard_map/ppermute | solution.py:415
  49.1 0.9 %shard_map.80 = bf16[128,2048]{1,0:T(8,128)(2,1)} custom-call(bf16[2,128,128]{2,1,0:T(8,128)(2,1)S(1)} %get-tuple-element.33.refs_0_, bf16[2,128,128]{2,1,0:T(8,128)(2,1)S(1)} %collective-permute-done.4.refs_1_, bf16[2,128,128]{2,1,0:T(8,128)(2,1)S(1)} %collective-permute-done.5.refs_2_, bf16[2,128,128]{2,1,0:T(8,128)(2,1)S(1)} %collective-permute-done.6.refs_3_, ...), custom_call_target="tpu_custom_call" | custom-call | tf_op jit(solution)/shard_map/pallas_call | solution.py:405
Async XLA Ops:
  2.6 20.1 %copy-start = (f32[2048]{0:T(1024)S(1)}, f32[2048]{0:T(1024)}, u32[]{:S(2)}) copy-start(f32[2048]{0:T(1024)} %param.11) | copy-start | bytes 24580
  2.6 20.1 %copy-start.1 = (f32[2048]{0:T(1024)S(1)}, f32[2048]{0:T(1024)}, u32[]{:S(2)}) copy-start(f32[2048]{0:T(1024)} %param.12) | copy-start | bytes 24580
  23.7 8.0 %collective-permute-start.7 = (bf16[512,128]{1,0:T(8,128)(2,1)S(1)}, bf16[512,128]{1,0:T(8,128)(2,1)S(1)}, u32[]{:S(2)}, u32[]{:S(2)}) collective-permute-start(bf16[512,128]{1,0:T(8,128)(2,1)S(1)} %shard_map.74.refs_0_), channel_id=1, source_target_pairs={{0,12},{1,13},{2,14},{3,15},{4,8},{5,9},{6,10},{7,11},{8,4},{9,5},... | collective-permute-start | bytes 393224 | tf_op jit(solution)/shard_map/ppermute | solution.py:415
  26.5 5.8 %collective-permute-start.1 = (bf16[4,128,128]{2,1,0:T(8,128)(2,1)S(1)}, bf16[4,128,128]{2,1,0:T(8,128)(2,1)S(1)}, u32[]{:S(2)}, u32[]{:S(2)}) collective-permute-start(bf16[4,128,128]{2,1,0:T(8,128)(2,1)S(1)} %get-tuple-element.26), channel_id=1, source_target_pairs={{0,2},{1,3},{2,0},{3,1},{4,6},{5,7},{6,4},{7,5},{8,10},{9,11},{10,... | collective-permute-start | bytes 393224 | tf_op jit(solution)/shard_map/ppermute | solution.py:415
  28.1 6.4 %collective-permute-start.2 = (bf16[4,128,128]{2,1,0:T(8,128)(2,1)S(1)}, bf16[4,128,128]{2,1,0:T(8,128)(2,1)S(1)}, u32[]{:S(2)}, u32[]{:S(2)}) collective-permute-start(bf16[4,128,128]{2,1,0:T(8,128)(2,1)S(1)} %get-tuple-element.27), channel_id=1, source_target_pairs={{0,4},{1,5},{2,6},{3,7},{4,0},{5,1},{6,2},{7,3},{8,12},{9,13},{10,... | collective-permute-start | bytes 393224 | tf_op jit(solution)/shard_map/ppermute | solution.py:415
  28.1 9.2 %collective-permute-start.3 = (bf16[4,128,128]{2,1,0:T(8,128)(2,1)S(1)}, bf16[4,128,128]{2,1,0:T(8,128)(2,1)S(1)}, u32[]{:S(2)}, u32[]{:S(2)}) collective-permute-start(bf16[4,128,128]{2,1,0:T(8,128)(2,1)S(1)} %get-tuple-element.28), channel_id=1, source_target_pairs={{0,6},{1,7},{2,4},{3,5},{4,2},{5,3},{6,0},{7,1},{8,14},{9,15},{10,... | collective-permute-start | bytes 393224 | tf_op jit(solution)/shard_map/ppermute | solution.py:415
  30.0 7.7 %collective-permute-start = (bf16[512,128]{1,0:T(8,128)(2,1)S(1)}, bf16[512,128]{1,0:T(8,128)(2,1)S(1)}, u32[]{:S(2)}, u32[]{:S(2)}) collective-permute-start(bf16[512,128]{1,0:T(8,128)(2,1)S(1)} %shard_map.74.refs_0_), channel_id=1, source_target_pairs={{0,1},{1,0},{2,3},{3,2},{4,5},{5,4},{6,7},{7,6},{8,9},{9,8},{10,11... | collective-permute-start | bytes 393224 | tf_op jit(solution)/shard_map/ppermute | solution.py:415
  31.8 10.3 %collective-permute-start.8 = (bf16[512,128]{1,0:T(8,128)(2,1)S(1)}, bf16[512,128]{1,0:T(8,128)(2,1)S(1)}, u32[]{:S(2)}, u32[]{:S(2)}) collective-permute-start(bf16[512,128]{1,0:T(8,128)(2,1)S(1)} %collective-permute-done.7.refs_0_), channel_id=1, source_target_pairs={{0,1},{1,0},{2,3},{3,2},{4,5},{5,4},{6,7},{7,6},{8,9},{9,8},{10,11... | collective-permute-start | bytes 393224 | tf_op jit(solution)/shard_map/ppermute | solution.py:415
  38.2 5.5 %collective-permute-start.4 = (bf16[2,128,128]{2,1,0:T(8,128)(2,1)S(1)}, bf16[2,128,128]{2,1,0:T(8,128)(2,1)S(1)}, u32[]{:S(2)}, u32[]{:S(2)}) collective-permute-start(bf16[2,128,128]{2,1,0:T(8,128)(2,1)S(1)} %get-tuple-element.34), channel_id=1, source_target_pairs={{0,2},{1,3},{2,0},{3,1},{4,6},{5,7},{6,4},{7,5},{8,10},{9,11},{10,... | collective-permute-start | bytes 196616 | tf_op jit(solution)/shard_map/ppermute | solution.py:415
  39.2 6.9 %collective-permute-start.5 = (bf16[2,128,128]{2,1,0:T(8,128)(2,1)S(1)}, bf16[2,128,128]{2,1,0:T(8,128)(2,1)S(1)}, u32[]{:S(2)}, u32[]{:S(2)}) collective-permute-start(bf16[2,128,128]{2,1,0:T(8,128)(2,1)S(1)} %get-tuple-element.35), channel_id=1, source_target_pairs={{0,4},{1,5},{2,6},{3,7},{4,0},{5,1},{6,2},{7,3},{8,12},{9,13},{10,... | collective-permute-start | bytes 196616 | tf_op jit(solution)/shard_map/ppermute | solution.py:415
  39.2 6.9 %collective-permute-start.6 = (bf16[2,128,128]{2,1,0:T(8,128)(2,1)S(1)}, bf16[2,128,128]{2,1,0:T(8,128)(2,1)S(1)}, u32[]{:S(2)}, u32[]{:S(2)}) collective-permute-start(bf16[2,128,128]{2,1,0:T(8,128)(2,1)S(1)} %get-tuple-element.36), channel_id=1, source_target_pairs={{0,6},{1,7},{2,4},{3,5},{4,2},{5,3},{6,0},{7,1},{8,14},{9,15},{10,... | collective-permute-start | bytes 196616 | tf_op jit(solution)/shard_map/ppermute | solution.py:415
  42.6 5.0 %collective-permute-start.9 = (bf16[2,128,128]{2,1,0:T(8,128)(2,1)S(1)}, bf16[2,128,128]{2,1,0:T(8,128)(2,1)S(1)}, u32[]{:S(2)}, u32[]{:S(2)}) collective-permute-start(bf16[2,128,128]{2,1,0:T(8,128)(2,1)S(1)} %get-tuple-element.42), channel_id=1, source_target_pairs={{0,2},{1,3},{2,0},{3,1},{4,6},{5,7},{6,4},{7,5},{8,10},{9,11},{10,... | collective-permute-start | bytes 196616 | tf_op jit(solution)/shard_map/ppermute | solution.py:415
  43.6 4.3 %collective-permute-start.10 = (bf16[2,128,128]{2,1,0:T(8,128)(2,1)S(1)}, bf16[2,128,128]{2,1,0:T(8,128)(2,1)S(1)}, u32[]{:S(2)}, u32[]{:S(2)}) collective-permute-start(bf16[2,128,128]{2,1,0:T(8,128)(2,1)S(1)} %get-tuple-element.43), channel_id=1, source_target_pairs={{0,4},{1,5},{2,6},{3,7},{4,0},{5,1},{6,2},{7,3},{8,12},{9,13},{10,... | collective-permute-start | bytes 196616 | tf_op jit(solution)/shard_map/ppermute | solution.py:415
  43.6 5.4 %collective-permute-start.11 = (bf16[2,128,128]{2,1,0:T(8,128)(2,1)S(1)}, bf16[2,128,128]{2,1,0:T(8,128)(2,1)S(1)}, u32[]{:S(2)}, u32[]{:S(2)}) collective-permute-start(bf16[2,128,128]{2,1,0:T(8,128)(2,1)S(1)} %get-tuple-element.44), channel_id=1, source_target_pairs={{0,6},{1,7},{2,4},{3,5},{4,2},{5,3},{6,0},{7,1},{8,14},{9,15},{10,... | collective-permute-start | bytes 196616 | tf_op jit(solution)/shard_map/ppermute | solution.py:415

commit v8 on v7

--- a/solution.py
+++ b/solution.py
@@ -163,6 +163,7 @@
 
 EDGE_ROWS = 3 * SHIFT - 1
 PEER = 1
+ORDER = tuple(index ^ (HEADS - 5) for index in range(HEADS))
 
 
 def rms_rows(values):
@@ -210,6 +211,7 @@
         for head in range(columns // HDIM):
             inside = slice(head * HDIM, (head + 1) * HDIM)
             part = picked[:rows, inside]
+            spot = ORDER.index(head)
             if slot < 2:
                 gain = buffers[3 + slot][head : head + 1, :]
                 part = jnp.where(first, part, rms_rows(part) * gain)
@@ -217,8 +219,8 @@
                 edge = sum(values[:, inside] for values in edges)
                 high = edge.astype(jnp.bfloat16)
                 low = (edge - high.astype(jnp.float32)).astype(jnp.bfloat16)
-                out_ref[head, 3 * rows :, :] = jnp.where(rest, low, high)
-            out_ref[head, slot * rows : (slot + 1) * rows, :] = part.astype(jnp.bfloat16)
+                out_ref[spot, 3 * rows :, :] = jnp.where(rest, low, high)
+            out_ref[spot, slot * rows : (slot + 1) * rows, :] = part.astype(jnp.bfloat16)
         target = pl.ds(slot * rows, span)
         copy = pltpu.make_async_copy(
             out_ref.at[:, target], out_hbm.at[:, target], out_sems.at[slot]
@@ -260,12 +262,20 @@
     rows = (depth - EDGE_ROWS) // 3
     total = count * rows
     head = lax.axis_index("seq")
-    edges = arrived_ref[:, 3 * rows :, :].astype(jnp.float32)
+
+    def arrived(first_row, size):
+        blocks = [
+            arrived_ref[pl.ds(ORDER.index(source), 1), first_row : first_row + size, :]
+            for source in range(count)
+        ]
+        return jnp.concatenate(blocks, axis=0).astype(jnp.float32)
+
+    edges = arrived(3 * rows, EDGE_ROWS)
     edge_row = lax.broadcasted_iota(jnp.int32, edges.shape, 1)
     first = lax.broadcasted_iota(jnp.int32, (count, rows, HDIM), 1) == 0
     tensors = []
     for slot, gain_ref in enumerate((query_gain_ref, key_gain_ref, None)):
-        part = arrived_ref[:, slot * rows : (slot + 1) * rows, :].astype(jnp.float32)
+        part = arrived(slot * rows, rows)
         own = (edge_row >= slot * SHIFT) & (edge_row < (slot + 1) * SHIFT)
         tail = jnp.sum(jnp.where(own, edges, 0.0), axis=1, keepdims=True)
         before = jnp.concatenate([jnp.zeros_like(tail[:1]), tail[:-1]], axis=0)
@@ -419,7 +429,14 @@
     far = HEADS // 2 + HEADS // 4
     nears = tuple(range(0, HEADS // 2, 2))
     outgoing = pool_inputs(query_src, key_src, value_src, query_gain, key_gain)
-    arrived = lax.all_to_all(outgoing, "seq", split_axis=0, concat_axis=0, tiled=True)
+    arrived = lax.all_to_all(
+        outgoing,
+        "seq",
+        split_axis=0,
+        concat_axis=0,
+        tiled=True,
+        axis_index_groups=[list(ORDER)],
+    )
     queries = norm_up(up_query, up_gain, (0, PEER, far, far ^ PEER), nears)
     queries = dict(zip(nears, queries))
     for near in nears[1:]:

time: 50.3 us -> 48.8 us (0.970)
  blocking collectives: 20.1 us -> 16.5 us
  starting transfers between devices: 12 us -> 15.2 us
  waiting for transfers between devices: 10.2 us -> 9.14 us
    all_to_all x1, blocking collectives: 20.1 us -> 16.5 us  [half_exchange(): lax.all_to_all(outgoing, 'seq', split_axis=0, concat_axis=0, tiled=True,...]
    ppermute x12, starting transfers between devices: 12 us -> 15.2 us  [swapped(): lax.ppermute(value, 'seq', [(source, source ^ offset) for source in range...]
    ppermute x12, waiting for transfers between devices: 10.2 us -> 9.14 us  [swapped(): lax.ppermute(value, 'seq', [(source, source ^ offset) for source in range...]
  transfers between devices with their start and end apart: 12 -> 12, of which waited for: 7 -> 6; matrix products, arithmetic and copies ran while one was open for 0% -> 0% of each run, Pallas kernels for 6% -> 6%
where the time goes in v8:
time: 48.8 us; the launch traced here: 48.6 us
  blocking collectives  16.5 us (34%)
  starting transfers between devices  15.2 us (31%)
  waiting for transfers between devices  9.14 us (19%)
  Pallas kernels  7.59 us (16%)
    all_to_all x1, blocking collectives, half_exchange(): lax.all_to_all(outgoing, 'seq', split_axis=0, concat_axis=0, tiled=True,...  16.5 us
    ppermute x12, starting transfers between devices, swapped(): lax.ppermute(value, 'seq', [(source, source ^ offset) for source in range...  15.2 us
    ppermute x12, waiting for transfers between devices, swapped(): lax.ppermute(value, 'seq', [(source, source ^ offset) for source in range...  9.14 us
    pallas_call x1, Pallas kernels, pool_inputs(): pl.pallas_call(pool_kernel, in_specs=[pl.BlockSpec(memory_space=pl.ANY)]...  2.61 us
    pallas_call x4, Pallas kernels, attend(): pl.pallas_call(functools.partial(attend_kernel, nears, slot), out_shape=[...  1.66 us
    pallas_call x1, Pallas kernels, norm_up(): pl.pallas_call(functools.partial(norm_kernel, shifts, nears), out_shape=[...  1.4 us
    pallas_call x1, Pallas kernels, short_attention(): pl.pallas_call(functools.partial(short_kernel, math.gcd(128, row_total)),...  1 us
  transfers between devices with their start and end apart: 12, of which 6 were waited for; matrix products, arithmetic and copies ran while one was open for 0% of the time, Pallas kernels for 6%

profile of v8, /device:TPU:0, one launch (start us, length us, event | category | flops | bytes accessed | tf_op | source)
XLA Modules:
  0.0 48.6 jit_solution(12800450689526748252)
XLA Ops:
  0.0 2.6 %shard_map.73 = bf16[16,104,128]{2,1,0:T(8,128)(2,1)} custom-call(bf16[128,2048]{1,0:T(8,128)(2,1)} %refs_0_.1, bf16[128,2048]{1,0:T(8,128)(2,1)} %refs_1_.1, bf16[128,2048]{1,0:T(8,128)(2,1)} %refs_2_.1, f32[16,128]{1,0:T(8,128)} %bitcast.3, f32[16,128]{1,0:T(8,128)} %bitcast.5), custom_call_target="tpu_custom_call" | custom-call | tf_op jit(solution)/shard_map/pallas_call | solution.py:238
  2.6 0.0 copy-start
  2.6 0.0 copy-start.1
  2.6 16.5 %all_to_all.5.arrived_ref = bf16[16,104,128]{2,1,0:T(8,128)(2,1)S(1)} all-to-all(bf16[16,104,128]{2,1,0:T(8,128)(2,1)} %shard_map.73), channel_id=1, replica_groups={{11,10,9,8,15,14,13,12,3,2,1,0,7,6,5,4},{27,26,25,24,31,30,29,28,19,18,..., dimensions={0} | all-to-all | bytes 851968 | tf_op jit(solution)/shard_map/all_to_all | solution.py:432
  19.1 0.0 copy-done
  19.1 0.0 copy-done.1
  19.1 1.0 %shard_map.74.refs_0_ = bf16[512,128]{1,0:T(8,128)(2,1)S(1)} custom-call(bf16[16,104,128]{2,1,0:T(8,128)(2,1)S(1)} %all_to_all.5.arrived_ref, f32[16,128]{1,0:T(8,128)S(1)} %bitcast.4, f32[16,128]{1,0:T(8,128)S(1)} %bitcast.6), custom_call_target="tpu_custom_call" | custom-call | tf_op jit(solution)/shard_map/pallas_call | solution.py:317
  20.2 4.0 %collective-permute-start.7 = (bf16[512,128]{1,0:T(8,128)(2,1)S(1)}, bf16[512,128]{1,0:T(8,128)(2,1)S(1)}, u32[]{:S(2)}, u32[]{:S(2)}) collective-permute-start(bf16[512,128]{1,0:T(8,128)(2,1)S(1)} %shard_map.74.refs_0_), channel_id=1, source_target_pairs={{0,12},{1,13},{2,14},{3,15},{4,8},{5,9},{6,10},{7,11},{8,4},{9,5},... | collective-permute-start | bytes 393224 | tf_op jit(solution)/shard_map/ppermute | solution.py:425
  24.2 1.4 %shard_map.75 = (bf16[4,128,128]{2,1,0:T(8,128)(2,1)S(1)}, bf16[4,128,128]{2,1,0:T(8,128)(2,1)S(1)}, bf16[4,128,128]{2,1,0:T(8,128)(2,1)S(1)}, bf16[4,128,128]{2,1,0:T(8,128)(2,1)S(1)}) custom-call(bf16[128,2048]{1,0:T(8,128)(2,1)} %up_ref.1, f32[16,128]{1,0:T(8,128)} %bitcast.7), custom_call_target="tpu_custom_call" | custom-call | tf_op jit(solution)/shard_map/pallas_call | solution.py:336
  25.6 0.1 collective-permute-start.1
  25.7 1.7 %collective-permute-start.2 = (bf16[4,128,128]{2,1,0:T(8,128)(2,1)S(1)}, bf16[4,128,128]{2,1,0:T(8,128)(2,1)S(1)}, u32[]{:S(2)}, u32[]{:S(2)}) collective-permute-start(bf16[4,128,128]{2,1,0:T(8,128)(2,1)S(1)} %get-tuple-element.27), channel_id=1, source_target_pairs={{0,4},{1,5},{2,6},{3,7},{4,0},{5,1},{6,2},{7,3},{8,12},{9,13},{10,... | collective-permute-start | bytes 393224 | tf_op jit(solution)/shard_map/ppermute | solution.py:425
  27.4 1.8 %collective-permute-start.3 = (bf16[4,128,128]{2,1,0:T(8,128)(2,1)S(1)}, bf16[4,128,128]{2,1,0:T(8,128)(2,1)S(1)}, u32[]{:S(2)}, u32[]{:S(2)}) collective-permute-start(bf16[4,128,128]{2,1,0:T(8,128)(2,1)S(1)} %get-tuple-element.28), channel_id=1, source_target_pairs={{0,6},{1,7},{2,4},{3,5},{4,2},{5,3},{6,0},{7,1},{8,14},{9,15},{10,... | collective-permute-start | bytes 393224 | tf_op jit(solution)/shard_map/ppermute | solution.py:425
  29.2 0.0 collective-permute-start
  29.2 0.0 collective-permute-done.7.refs_0_
  29.2 0.5 %collective-permute-start.8 = (bf16[512,128]{1,0:T(8,128)(2,1)S(1)}, bf16[512,128]{1,0:T(8,128)(2,1)S(1)}, u32[]{:S(2)}, u32[]{:S(2)}) collective-permute-start(bf16[512,128]{1,0:T(8,128)(2,1)S(1)} %collective-permute-done.7.refs_0_), channel_id=1, source_target_pairs={{0,1},{1,0},{2,3},{3,2},{4,5},{5,4},{6,7},{7,6},{8,9},{9,8},{10,11... | collective-permute-start | bytes 393224 | tf_op jit(solution)/shard_map/ppermute | solution.py:425
  29.7 1.5 %collective-permute-done.1.refs_2_ = bf16[4,128,128]{2,1,0:T(8,128)(2,1)S(1)} collective-permute-done((bf16[4,128,128]{2,1,0:T(8,128)(2,1)S(1)}, bf16[4,128,128]{2,1,0:T(8,128)(2,1)S(1)}, u32[]{:S(2)}, u32[]{:S(2)}) %collective-permute-start.1) | collective-permute-done | bytes 131104 | tf_op jit(solution)/shard_map/ppermute | solution.py:425
  31.2 0.9 %collective-permute-done.2.refs_3_ = bf16[4,128,128]{2,1,0:T(8,128)(2,1)S(1)} collective-permute-done((bf16[4,128,128]{2,1,0:T(8,128)(2,1)S(1)}, bf16[4,128,128]{2,1,0:T(8,128)(2,1)S(1)}, u32[]{:S(2)}, u32[]{:S(2)}) %collective-permute-start.2) | collective-permute-done | bytes 131104 | tf_op jit(solution)/shard_map/ppermute | solution.py:425
  32.1 3.3 %collective-permute-done.3.refs_4_ = bf16[4,128,128]{2,1,0:T(8,128)(2,1)S(1)} collective-permute-done((bf16[4,128,128]{2,1,0:T(8,128)(2,1)S(1)}, bf16[4,128,128]{2,1,0:T(8,128)(2,1)S(1)}, u32[]{:S(2)}, u32[]{:S(2)}) %collective-permute-start.3) | collective-permute-done | bytes 131104 | tf_op jit(solution)/shard_map/ppermute | solution.py:425
  35.4 0.4 shard_map.76
  35.8 0.0 collective-permute-done.refs_0_
  35.8 0.4 shard_map.77
  36.2 0.8 %collective-permute-start.4 = (bf16[2,128,128]{2,1,0:T(8,128)(2,1)S(1)}, bf16[2,128,128]{2,1,0:T(8,128)(2,1)S(1)}, u32[]{:S(2)}, u32[]{:S(2)}) collective-permute-start(bf16[2,128,128]{2,1,0:T(8,128)(2,1)S(1)} %get-tuple-element.34), channel_id=1, source_target_pairs={{0,2},{1,3},{2,0},{3,1},{4,6},{5,7},{6,4},{7,5},{8,10},{9,11},{10,... | collective-permute-start | bytes 196616 | tf_op jit(solution)/shard_map/ppermute | solution.py:425
  37.0 1.0 %collective-permute-start.5 = (bf16[2,128,128]{2,1,0:T(8,128)(2,1)S(1)}, bf16[2,128,128]{2,1,0:T(8,128)(2,1)S(1)}, u32[]{:S(2)}, u32[]{:S(2)}) collective-permute-start(bf16[2,128,128]{2,1,0:T(8,128)(2,1)S(1)} %get-tuple-element.35), channel_id=1, source_target_pairs={{0,4},{1,5},{2,6},{3,7},{4,0},{5,1},{6,2},{7,3},{8,12},{9,13},{10,... | collective-permute-start | bytes 196616 | tf_op jit(solution)/shard_map/ppermute | solution.py:425
  38.1 1.7 %collective-permute-start.6 = (bf16[2,128,128]{2,1,0:T(8,128)(2,1)S(1)}, bf16[2,128,128]{2,1,0:T(8,128)(2,1)S(1)}, u32[]{:S(2)}, u32[]{:S(2)}) collective-permute-start(bf16[2,128,128]{2,1,0:T(8,128)(2,1)S(1)} %get-tuple-element.36), channel_id=1, source_target_pairs={{0,6},{1,7},{2,4},{3,5},{4,2},{5,3},{6,0},{7,1},{8,14},{9,15},{10,... | collective-permute-start | bytes 196616 | tf_op jit(solution)/shard_map/ppermute | solution.py:425
  39.8 0.4 shard_map.78
  40.2 0.0 collective-permute-done.8.refs_0_
  40.2 0.4 shard_map.79
  40.7 0.8 %collective-permute-start.9 = (bf16[2,128,128]{2,1,0:T(8,128)(2,1)S(1)}, bf16[2,128,128]{2,1,0:T(8,128)(2,1)S(1)}, u32[]{:S(2)}, u32[]{:S(2)}) collective-permute-start(bf16[2,128,128]{2,1,0:T(8,128)(2,1)S(1)} %get-tuple-element.42), channel_id=1, source_target_pairs={{0,2},{1,3},{2,0},{3,1},{4,6},{5,7},{6,4},{7,5},{8,10},{9,11},{10,... | collective-permute-start | bytes 196616 | tf_op jit(solution)/shard_map/ppermute | solution.py:425
  41.4 1.0 %collective-permute-start.10 = (bf16[2,128,128]{2,1,0:T(8,128)(2,1)S(1)}, bf16[2,128,128]{2,1,0:T(8,128)(2,1)S(1)}, u32[]{:S(2)}, u32[]{:S(2)}) collective-permute-start(bf16[2,128,128]{2,1,0:T(8,128)(2,1)S(1)} %get-tuple-element.43), channel_id=1, source_target_pairs={{0,4},{1,5},{2,6},{3,7},{4,0},{5,1},{6,2},{7,3},{8,12},{9,13},{10,... | collective-permute-start | bytes 196616 | tf_op jit(solution)/shard_map/ppermute | solution.py:425
  42.5 0.0 collective-permute-done.4.refs_1_
  42.5 1.7 %collective-permute-start.11 = (bf16[2,128,128]{2,1,0:T(8,128)(2,1)S(1)}, bf16[2,128,128]{2,1,0:T(8,128)(2,1)S(1)}, u32[]{:S(2)}, u32[]{:S(2)}) collective-permute-start(bf16[2,128,128]{2,1,0:T(8,128)(2,1)S(1)} %get-tuple-element.44), channel_id=1, source_target_pairs={{0,6},{1,7},{2,4},{3,5},{4,2},{5,3},{6,0},{7,1},{8,14},{9,15},{10,... | collective-permute-start | bytes 196616 | tf_op jit(solution)/shard_map/ppermute | solution.py:425
  44.2 0.0 collective-permute-done.5.refs_2_
  44.2 0.0 collective-permute-done.6.refs_3_
  44.2 1.1 %collective-permute-done.9.refs_5_ = bf16[2,128,128]{2,1,0:T(8,128)(2,1)S(1)} collective-permute-done((bf16[2,128,128]{2,1,0:T(8,128)(2,1)S(1)}, bf16[2,128,128]{2,1,0:T(8,128)(2,1)S(1)}, u32[]{:S(2)}, u32[]{:S(2)}) %collective-permute-start.9) | collective-permute-done | bytes 65568 | tf_op jit(solution)/shard_map/ppermute | solution.py:425
  45.3 0.4 collective-permute-done.10.refs_6_
  45.7 1.9 %collective-permute-done.11.refs_7_ = bf16[2,128,128]{2,1,0:T(8,128)(2,1)S(1)} collective-permute-done((bf16[2,128,128]{2,1,0:T(8,128)(2,1)S(1)}, bf16[2,128,128]{2,1,0:T(8,128)(2,1)S(1)}, u32[]{:S(2)}, u32[]{:S(2)}) %collective-permute-start.11) | collective-permute-done | bytes 65568 | tf_op jit(solution)/shard_map/ppermute | solution.py:425
  47.6 0.9 %shard_map.80 = bf16[128,2048]{1,0:T(8,128)(2,1)} custom-call(bf16[2,128,128]{2,1,0:T(8,128)(2,1)S(1)} %get-tuple-element.33.refs_0_, bf16[2,128,128]{2,1,0:T(8,128)(2,1)S(1)} %collective-permute-done.4.refs_1_, bf16[2,128,128]{2,1,0:T(8,128)(2,1)S(1)} %collective-permute-done.5.refs_2_, bf16[2,128,128]{2,1,0:T(8,128)(2,1)S(1)} %collective-permute-done.6.refs_3_, ...), custom_call_target="tpu_custom_call" | custom-call | tf_op jit(solution)/shard_map/pallas_call | solution.py:415
Async XLA Ops:
  2.6 16.5 %copy-start = (f32[2048]{0:T(1024)S(1)}, f32[2048]{0:T(1024)}, u32[]{:S(2)}) copy-start(f32[2048]{0:T(1024)} %param.11) | copy-start | bytes 24580
  2.6 16.5 %copy-start.1 = (f32[2048]{0:T(1024)S(1)}, f32[2048]{0:T(1024)}, u32[]{:S(2)}) copy-start(f32[2048]{0:T(1024)} %param.12) | copy-start | bytes 24580
  20.2 9.0 %collective-permute-start.7 = (bf16[512,128]{1,0:T(8,128)(2,1)S(1)}, bf16[512,128]{1,0:T(8,128)(2,1)S(1)}, u32[]{:S(2)}, u32[]{:S(2)}) collective-permute-start(bf16[512,128]{1,0:T(8,128)(2,1)S(1)} %shard_map.74.refs_0_), channel_id=1, source_target_pairs={{0,12},{1,13},{2,14},{3,15},{4,8},{5,9},{6,10},{7,11},{8,4},{9,5},... | collective-permute-start | bytes 393224 | tf_op jit(solution)/shard_map/ppermute | solution.py:425
  25.6 5.6 %collective-permute-start.1 = (bf16[4,128,128]{2,1,0:T(8,128)(2,1)S(1)}, bf16[4,128,128]{2,1,0:T(8,128)(2,1)S(1)}, u32[]{:S(2)}, u32[]{:S(2)}) collective-permute-start(bf16[4,128,128]{2,1,0:T(8,128)(2,1)S(1)} %get-tuple-element.26), channel_id=1, source_target_pairs={{0,2},{1,3},{2,0},{3,1},{4,6},{5,7},{6,4},{7,5},{8,10},{9,11},{10,... | collective-permute-start | bytes 393224 | tf_op jit(solution)/shard_map/ppermute | solution.py:425
  25.7 6.4 %collective-permute-start.2 = (bf16[4,128,128]{2,1,0:T(8,128)(2,1)S(1)}, bf16[4,128,128]{2,1,0:T(8,128)(2,1)S(1)}, u32[]{:S(2)}, u32[]{:S(2)}) collective-permute-start(bf16[4,128,128]{2,1,0:T(8,128)(2,1)S(1)} %get-tuple-element.27), channel_id=1, source_target_pairs={{0,4},{1,5},{2,6},{3,7},{4,0},{5,1},{6,2},{7,3},{8,12},{9,13},{10,... | collective-permute-start | bytes 393224 | tf_op jit(solution)/shard_map/ppermute | solution.py:425
  27.4 8.0 %collective-permute-start.3 = (bf16[4,128,128]{2,1,0:T(8,128)(2,1)S(1)}, bf16[4,128,128]{2,1,0:T(8,128)(2,1)S(1)}, u32[]{:S(2)}, u32[]{:S(2)}) collective-permute-start(bf16[4,128,128]{2,1,0:T(8,128)(2,1)S(1)} %get-tuple-element.28), channel_id=1, source_target_pairs={{0,6},{1,7},{2,4},{3,5},{4,2},{5,3},{6,0},{7,1},{8,14},{9,15},{10,... | collective-permute-start | bytes 393224 | tf_op jit(solution)/shard_map/ppermute | solution.py:425
  29.2 6.6 %collective-permute-start = (bf16[512,128]{1,0:T(8,128)(2,1)S(1)}, bf16[512,128]{1,0:T(8,128)(2,1)S(1)}, u32[]{:S(2)}, u32[]{:S(2)}) collective-permute-start(bf16[512,128]{1,0:T(8,128)(2,1)S(1)} %shard_map.74.refs_0_), channel_id=1, source_target_pairs={{0,1},{1,0},{2,3},{3,2},{4,5},{5,4},{6,7},{7,6},{8,9},{9,8},{10,11... | collective-permute-start | bytes 393224 | tf_op jit(solution)/shard_map/ppermute | solution.py:425
  29.2 11.0 %collective-permute-start.8 = (bf16[512,128]{1,0:T(8,128)(2,1)S(1)}, bf16[512,128]{1,0:T(8,128)(2,1)S(1)}, u32[]{:S(2)}, u32[]{:S(2)}) collective-permute-start(bf16[512,128]{1,0:T(8,128)(2,1)S(1)} %collective-permute-done.7.refs_0_), channel_id=1, source_target_pairs={{0,1},{1,0},{2,3},{3,2},{4,5},{5,4},{6,7},{7,6},{8,9},{9,8},{10,11... | collective-permute-start | bytes 393224 | tf_op jit(solution)/shard_map/ppermute | solution.py:425
  36.2 6.2 %collective-permute-start.4 = (bf16[2,128,128]{2,1,0:T(8,128)(2,1)S(1)}, bf16[2,128,128]{2,1,0:T(8,128)(2,1)S(1)}, u32[]{:S(2)}, u32[]{:S(2)}) collective-permute-start(bf16[2,128,128]{2,1,0:T(8,128)(2,1)S(1)} %get-tuple-element.34), channel_id=1, source_target_pairs={{0,2},{1,3},{2,0},{3,1},{4,6},{5,7},{6,4},{7,5},{8,10},{9,11},{10,... | collective-permute-start | bytes 196616 | tf_op jit(solution)/shard_map/ppermute | solution.py:425
  37.0 7.2 %collective-permute-start.5 = (bf16[2,128,128]{2,1,0:T(8,128)(2,1)S(1)}, bf16[2,128,128]{2,1,0:T(8,128)(2,1)S(1)}, u32[]{:S(2)}, u32[]{:S(2)}) collective-permute-start(bf16[2,128,128]{2,1,0:T(8,128)(2,1)S(1)} %get-tuple-element.35), channel_id=1, source_target_pairs={{0,4},{1,5},{2,6},{3,7},{4,0},{5,1},{6,2},{7,3},{8,12},{9,13},{10,... | collective-permute-start | bytes 196616 | tf_op jit(solution)/shard_map/ppermute | solution.py:425
  38.1 6.2 %collective-permute-start.6 = (bf16[2,128,128]{2,1,0:T(8,128)(2,1)S(1)}, bf16[2,128,128]{2,1,0:T(8,128)(2,1)S(1)}, u32[]{:S(2)}, u32[]{:S(2)}) collective-permute-start(bf16[2,128,128]{2,1,0:T(8,128)(2,1)S(1)} %get-tuple-element.36), channel_id=1, source_target_pairs={{0,6},{1,7},{2,4},{3,5},{4,2},{5,3},{6,0},{7,1},{8,14},{9,15},{10,... | collective-permute-start | bytes 196616 | tf_op jit(solution)/shard_map/ppermute | solution.py:425
  40.7 4.7 %collective-permute-start.9 = (bf16[2,128,128]{2,1,0:T(8,128)(2,1)S(1)}, bf16[2,128,128]{2,1,0:T(8,128)(2,1)S(1)}, u32[]{:S(2)}, u32[]{:S(2)}) collective-permute-start(bf16[2,128,128]{2,1,0:T(8,128)(2,1)S(1)} %get-tuple-element.42), channel_id=1, source_target_pairs={{0,2},{1,3},{2,0},{3,1},{4,6},{5,7},{6,4},{7,5},{8,10},{9,11},{10,... | collective-permute-start | bytes 196616 | tf_op jit(solution)/shard_map/ppermute | solution.py:425
  41.4 4.3 %collective-permute-start.10 = (bf16[2,128,128]{2,1,0:T(8,128)(2,1)S(1)}, bf16[2,128,128]{2,1,0:T(8,128)(2,1)S(1)}, u32[]{:S(2)}, u32[]{:S(2)}) collective-permute-start(bf16[2,128,128]{2,1,0:T(8,128)(2,1)S(1)} %get-tuple-element.43), channel_id=1, source_target_pairs={{0,4},{1,5},{2,6},{3,7},{4,0},{5,1},{6,2},{7,3},{8,12},{9,13},{10,... | collective-permute-start | bytes 196616 | tf_op jit(solution)/shard_map/ppermute | solution.py:425
  42.5 5.2 %collective-permute-start.11 = (bf16[2,128,128]{2,1,0:T(8,128)(2,1)S(1)}, bf16[2,128,128]{2,1,0:T(8,128)(2,1)S(1)}, u32[]{:S(2)}, u32[]{:S(2)}) collective-permute-start(bf16[2,128,128]{2,1,0:T(8,128)(2,1)S(1)} %get-tuple-element.44), channel_id=1, source_target_pairs={{0,6},{1,7},{2,4},{3,5},{4,2},{5,3},{6,0},{7,1},{8,14},{9,15},{10,... | collective-permute-start | bytes 196616 | tf_op jit(solution)/shard_map/ppermute | solution.py:425

commit v9 on v8

--- a/solution.py
+++ b/solution.py
@@ -315,7 +315,7 @@
     count, depth, _ = arrived.shape
     row_total = count * (depth - EDGE_ROWS) // 3
     return pl.pallas_call(
-        functools.partial(short_kernel, math.gcd(128, row_total)),
+        functools.partial(short_kernel, math.gcd(256, row_total)),
         out_shape=pltpu.VMEM((row_total, HDIM), jnp.bfloat16),
     )(on_chip(arrived), *[on_chip(gain.reshape(-1, HDIM)) for gain in (query_gain, key_gain)])
 
@@ -395,7 +395,7 @@
 
 
 def place_kernel(offsets, *refs):
-    piece_refs, out_hbm, sems = refs[:-2], refs[-2], refs[-1]
+    piece_refs, out_hbm, sems = refs[: len(offsets)], refs[-2], refs[-1]
     device = lax.axis_index("seq")
     copies = []
     for number, (offset, piece_ref) in enumerate(zip(offsets, piece_refs)):
@@ -411,13 +411,21 @@
         copy.wait()
 
 
-def place(offsets, pieces):
+def place(offsets, pieces, base=None):
+    count = len(pieces)
+    operands = [on_chip(piece) for piece in pieces]
+    specs = [pl.BlockSpec(memory_space=pltpu.VMEM)] * count
+    if base is not None:
+        operands.append(base)
+        specs.append(pl.BlockSpec(memory_space=pl.ANY))
     return pl.pallas_call(
         functools.partial(place_kernel, offsets),
+        in_specs=specs,
         out_specs=pl.BlockSpec(memory_space=pl.ANY),
         out_shape=jax.ShapeDtypeStruct((pieces[0].shape[1], HEADS * HDIM), jnp.bfloat16),
-        scratch_shapes=[pltpu.SemaphoreType.DMA((2 * len(pieces),))],
-    )(*[on_chip(piece) for piece in pieces])
+        input_output_aliases={} if base is None else {count: 0},
+        scratch_shapes=[pltpu.SemaphoreType.DMA((2 * count,))],
+    )(*operands)
 
 
 def swapped(value, offset):
@@ -443,15 +451,16 @@
         queries[near] = swapped(queries[near], near)
     memory = short_attention(arrived, query_gain, key_gain)
     far_memory = swapped(memory, far)
-    offsets, pieces = [], []
+    result = None
     for kind, held in enumerate((memory, far_memory)):
         peer_memory = swapped(held, PEER)
         done = attend(nears, held, 2 * kind, queries, None)
         done = attend(nears, peer_memory, 2 * kind + 1, queries, done)
+        pieces = []
         for near in nears:
             pieces.append(swapped(done[near], near) if near else done[near])
-            offsets.append(near ^ (kind * far))
-    return place(tuple(offsets), pieces)
+        result = place(tuple(near ^ (kind * far) for near in nears), pieces, result)
+    return result
 
 
 def local(*arrays):

time: 48.8 us -> 48.4 us (level)
  waiting for transfers between devices: 9.14 us -> 8.37 us
    ppermute x12, waiting for transfers between devices: 9.14 us -> 8.37 us  [swapped(): lax.ppermute(value, 'seq', [(source, source ^ offset) for source in range...]
    pallas_call x2 -> x3, Pallas kernels: 1.92 us -> 2.27 us  [the longest x2 1.52 us: place(): pl.pallas_call(functools.partial(place_kernel, offsets), in_specs=specs,...]
  transfers between devices with their start and end apart: 12 -> 12, of which waited for: 6 -> 6; matrix products, arithmetic and copies ran while one was open for 0% -> 0% of each run, Pallas kernels for 6% -> 8%
where the time goes in v9:
time: 48.4 us; the launch traced here: 48.1 us
  blocking collectives  16.5 us (34%)
  starting transfers between devices  15.2 us (31%)
  waiting for transfers between devices  8.37 us (17%)
  Pallas kernels  7.95 us (16%)
    all_to_all x1, blocking collectives, half_exchange(): lax.all_to_all(outgoing, 'seq', split_axis=0, concat_axis=0, tiled=True,...  16.5 us
    ppermute x12, starting transfers between devices, swapped(): lax.ppermute(value, 'seq', [(source, source ^ offset) for source in range...  15.2 us
    ppermute x12, waiting for transfers between devices, swapped(): lax.ppermute(value, 'seq', [(source, source ^ offset) for source in range...  8.37 us
    pallas_call x1, Pallas kernels, pool_inputs(): pl.pallas_call(pool_kernel, in_specs=[pl.BlockSpec(memory_space=pl.ANY)]...  2.61 us
    pallas_call x4, Pallas kernels, attend(): pl.pallas_call(functools.partial(attend_kernel, nears, slot), out_shape=[...  1.66 us
    pallas_call x2, Pallas kernels, place(): pl.pallas_call(functools.partial(place_kernel, offsets), in_specs=specs,...  1.52 us
    pallas_call x1, Pallas kernels, norm_up(): pl.pallas_call(functools.partial(norm_kernel, shifts, nears), out_shape=[...  1.4 us
  transfers between devices with their start and end apart: 12, of which 6 were waited for; matrix products, arithmetic and copies ran while one was open for 0% of the time, Pallas kernels for 8%

profile of v9, /device:TPU:0, one launch (start us, length us, event | category | flops | bytes accessed | tf_op | source)
XLA Modules:
  0.0 48.1 jit_solution(4562328568914250972)
XLA Ops:
  0.0 2.6 %shard_map.73 = bf16[16,104,128]{2,1,0:T(8,128)(2,1)} custom-call(bf16[128,2048]{1,0:T(8,128)(2,1)} %refs_0_.1, bf16[128,2048]{1,0:T(8,128)(2,1)} %refs_1_.1, bf16[128,2048]{1,0:T(8,128)(2,1)} %refs_2_.1, f32[16,128]{1,0:T(8,128)} %bitcast.3, f32[16,128]{1,0:T(8,128)} %bitcast.5), custom_call_target="tpu_custom_call" | custom-call | tf_op jit(solution)/shard_map/pallas_call | solution.py:238
  2.6 0.0 copy-start
  2.6 0.0 copy-start.1
  2.6 16.5 %all_to_all.5.arrived_ref = bf16[16,104,128]{2,1,0:T(8,128)(2,1)S(1)} all-to-all(bf16[16,104,128]{2,1,0:T(8,128)(2,1)} %shard_map.73), channel_id=1, replica_groups={{11,10,9,8,15,14,13,12,3,2,1,0,7,6,5,4},{27,26,25,24,31,30,29,28,19,18,..., dimensions={0} | all-to-all | bytes 851968 | tf_op jit(solution)/shard_map/all_to_all | solution.py:440
  19.1 0.0 copy-done
  19.1 0.0 copy-done.1
  19.1 0.8 %shard_map.74.refs_0_ = bf16[512,128]{1,0:T(8,128)(2,1)S(1)} custom-call(bf16[16,104,128]{2,1,0:T(8,128)(2,1)S(1)} %all_to_all.5.arrived_ref, f32[16,128]{1,0:T(8,128)S(1)} %bitcast.4, f32[16,128]{1,0:T(8,128)S(1)} %bitcast.6), custom_call_target="tpu_custom_call" | custom-call | tf_op jit(solution)/shard_map/pallas_call | solution.py:317
  19.9 4.0 %collective-permute-start = (bf16[512,128]{1,0:T(8,128)(2,1)S(1)}, bf16[512,128]{1,0:T(8,128)(2,1)S(1)}, u32[]{:S(2)}, u32[]{:S(2)}) collective-permute-start(bf16[512,128]{1,0:T(8,128)(2,1)S(1)} %shard_map.74.refs_0_), channel_id=1, source_target_pairs={{0,12},{1,13},{2,14},{3,15},{4,8},{5,9},{6,10},{7,11},{8,4},{9,5},... | collective-permute-start | bytes 393224 | tf_op jit(solution)/shard_map/ppermute | solution.py:433
  23.9 1.4 %shard_map.75 = (bf16[4,128,128]{2,1,0:T(8,128)(2,1)S(1)}, bf16[4,128,128]{2,1,0:T(8,128)(2,1)S(1)}, bf16[4,128,128]{2,1,0:T(8,128)(2,1)S(1)}, bf16[4,128,128]{2,1,0:T(8,128)(2,1)S(1)}) custom-call(bf16[128,2048]{1,0:T(8,128)(2,1)} %up_ref.1, f32[16,128]{1,0:T(8,128)} %bitcast.7), custom_call_target="tpu_custom_call" | custom-call | tf_op jit(solution)/shard_map/pallas_call | solution.py:336
  25.4 0.1 collective-permute-start.2
  25.4 1.7 %collective-permute-start.3 = (bf16[4,128,128]{2,1,0:T(8,128)(2,1)S(1)}, bf16[4,128,128]{2,1,0:T(8,128)(2,1)S(1)}, u32[]{:S(2)}, u32[]{:S(2)}) collective-permute-start(bf16[4,128,128]{2,1,0:T(8,128)(2,1)S(1)} %get-tuple-element.27), channel_id=1, source_target_pairs={{0,4},{1,5},{2,6},{3,7},{4,0},{5,1},{6,2},{7,3},{8,12},{9,13},{10,... | collective-permute-start | bytes 393224 | tf_op jit(solution)/shard_map/ppermute | solution.py:433
  27.2 1.8 %collective-permute-start.4 = (bf16[4,128,128]{2,1,0:T(8,128)(2,1)S(1)}, bf16[4,128,128]{2,1,0:T(8,128)(2,1)S(1)}, u32[]{:S(2)}, u32[]{:S(2)}) collective-permute-start(bf16[4,128,128]{2,1,0:T(8,128)(2,1)S(1)} %get-tuple-element.28), channel_id=1, source_target_pairs={{0,6},{1,7},{2,4},{3,5},{4,2},{5,3},{6,0},{7,1},{8,14},{9,15},{10,... | collective-permute-start | bytes 393224 | tf_op jit(solution)/shard_map/ppermute | solution.py:433
  28.9 0.0 collective-permute-start.8
  28.9 0.0 collective-permute-done.refs_0_
  28.9 0.5 %collective-permute-start.1 = (bf16[512,128]{1,0:T(8,128)(2,1)S(1)}, bf16[512,128]{1,0:T(8,128)(2,1)S(1)}, u32[]{:S(2)}, u32[]{:S(2)}) collective-permute-start(bf16[512,128]{1,0:T(8,128)(2,1)S(1)} %collective-permute-done.refs_0_), channel_id=1, source_target_pairs={{0,1},{1,0},{2,3},{3,2},{4,5},{5,4},{6,7},{7,6},{8,9},{9,8},{10,11... | collective-permute-start | bytes 393224 | tf_op jit(solution)/shard_map/ppermute | solution.py:433
  29.4 1.5 %collective-permute-done.2.refs_2_ = bf16[4,128,128]{2,1,0:T(8,128)(2,1)S(1)} collective-permute-done((bf16[4,128,128]{2,1,0:T(8,128)(2,1)S(1)}, bf16[4,128,128]{2,1,0:T(8,128)(2,1)S(1)}, u32[]{:S(2)}, u32[]{:S(2)}) %collective-permute-start.2) | collective-permute-done | bytes 131104 | tf_op jit(solution)/shard_map/ppermute | solution.py:433
  31.0 0.9 %collective-permute-done.3.refs_3_ = bf16[4,128,128]{2,1,0:T(8,128)(2,1)S(1)} collective-permute-done((bf16[4,128,128]{2,1,0:T(8,128)(2,1)S(1)}, bf16[4,128,128]{2,1,0:T(8,128)(2,1)S(1)}, u32[]{:S(2)}, u32[]{:S(2)}) %collective-permute-start.3) | collective-permute-done | bytes 131104 | tf_op jit(solution)/shard_map/ppermute | solution.py:433
  31.9 3.3 %collective-permute-done.4.refs_4_ = bf16[4,128,128]{2,1,0:T(8,128)(2,1)S(1)} collective-permute-done((bf16[4,128,128]{2,1,0:T(8,128)(2,1)S(1)}, bf16[4,128,128]{2,1,0:T(8,128)(2,1)S(1)}, u32[]{:S(2)}, u32[]{:S(2)}) %collective-permute-start.4) | collective-permute-done | bytes 131104 | tf_op jit(solution)/shard_map/ppermute | solution.py:433
  35.1 0.4 shard_map.78
  35.5 0.0 collective-permute-done.8.refs_0_
  35.6 0.4 shard_map.79
  36.0 0.8 %collective-permute-start.9 = (bf16[2,128,128]{2,1,0:T(8,128)(2,1)S(1)}, bf16[2,128,128]{2,1,0:T(8,128)(2,1)S(1)}, u32[]{:S(2)}, u32[]{:S(2)}) collective-permute-start(bf16[2,128,128]{2,1,0:T(8,128)(2,1)S(1)} %get-tuple-element.42), channel_id=1, source_target_pairs={{0,2},{1,3},{2,0},{3,1},{4,6},{5,7},{6,4},{7,5},{8,10},{9,11},{10,... | collective-permute-start | bytes 196616 | tf_op jit(solution)/shard_map/ppermute | solution.py:433
  36.8 1.0 %collective-permute-start.10 = (bf16[2,128,128]{2,1,0:T(8,128)(2,1)S(1)}, bf16[2,128,128]{2,1,0:T(8,128)(2,1)S(1)}, u32[]{:S(2)}, u32[]{:S(2)}) collective-permute-start(bf16[2,128,128]{2,1,0:T(8,128)(2,1)S(1)} %get-tuple-element.43), channel_id=1, source_target_pairs={{0,4},{1,5},{2,6},{3,7},{4,0},{5,1},{6,2},{7,3},{8,12},{9,13},{10,... | collective-permute-start | bytes 196616 | tf_op jit(solution)/shard_map/ppermute | solution.py:433
  37.8 1.7 %collective-permute-start.11 = (bf16[2,128,128]{2,1,0:T(8,128)(2,1)S(1)}, bf16[2,128,128]{2,1,0:T(8,128)(2,1)S(1)}, u32[]{:S(2)}, u32[]{:S(2)}) collective-permute-start(bf16[2,128,128]{2,1,0:T(8,128)(2,1)S(1)} %get-tuple-element.44), channel_id=1, source_target_pairs={{0,6},{1,7},{2,4},{3,5},{4,2},{5,3},{6,0},{7,1},{8,14},{9,15},{10,... | collective-permute-start | bytes 196616 | tf_op jit(solution)/shard_map/ppermute | solution.py:433
  39.5 0.4 shard_map.76
  40.0 0.0 collective-permute-done.1.refs_0_
  40.0 0.4 shard_map.77
  40.4 0.8 %collective-permute-start.5 = (bf16[2,128,128]{2,1,0:T(8,128)(2,1)S(1)}, bf16[2,128,128]{2,1,0:T(8,128)(2,1)S(1)}, u32[]{:S(2)}, u32[]{:S(2)}) collective-permute-start(bf16[2,128,128]{2,1,0:T(8,128)(2,1)S(1)} %get-tuple-element.34), channel_id=1, source_target_pairs={{0,2},{1,3},{2,0},{3,1},{4,6},{5,7},{6,4},{7,5},{8,10},{9,11},{10,... | collective-permute-start | bytes 196616 | tf_op jit(solution)/shard_map/ppermute | solution.py:433
  41.2 1.0 %collective-permute-start.6 = (bf16[2,128,128]{2,1,0:T(8,128)(2,1)S(1)}, bf16[2,128,128]{2,1,0:T(8,128)(2,1)S(1)}, u32[]{:S(2)}, u32[]{:S(2)}) collective-permute-start(bf16[2,128,128]{2,1,0:T(8,128)(2,1)S(1)} %get-tuple-element.35), channel_id=1, source_target_pairs={{0,4},{1,5},{2,6},{3,7},{4,0},{5,1},{6,2},{7,3},{8,12},{9,13},{10,... | collective-permute-start | bytes 196616 | tf_op jit(solution)/shard_map/ppermute | solution.py:433
  42.2 0.0 collective-permute-done.9.refs_1_
  42.2 1.7 %collective-permute-start.7 = (bf16[2,128,128]{2,1,0:T(8,128)(2,1)S(1)}, bf16[2,128,128]{2,1,0:T(8,128)(2,1)S(1)}, u32[]{:S(2)}, u32[]{:S(2)}) collective-permute-start(bf16[2,128,128]{2,1,0:T(8,128)(2,1)S(1)} %get-tuple-element.36), channel_id=1, source_target_pairs={{0,6},{1,7},{2,4},{3,5},{4,2},{5,3},{6,0},{7,1},{8,14},{9,15},{10,... | collective-permute-start | bytes 196616 | tf_op jit(solution)/shard_map/ppermute | solution.py:433
  44.0 0.0 collective-permute-done.10.refs_2_
  44.0 0.0 collective-permute-done.11.refs_3_
  44.0 0.8 %shard_map.80.refs_4_ = bf16[128,2048]{1,0:T(8,128)(2,1)} custom-call(bf16[2,128,128]{2,1,0:T(8,128)(2,1)S(1)} %get-tuple-element.41.refs_0_, bf16[2,128,128]{2,1,0:T(8,128)(2,1)S(1)} %collective-permute-done.9.refs_1_, bf16[2,128,128]{2,1,0:T(8,128)(2,1)S(1)} %collective-permute-done.10.refs_2_, bf16[2,128,128]{2,1,0:T(8,128)(2,1)S(1)} %collective-permute-done.11.refs_3_), custom_call_target="tpu_custom_call" | custom-call | tf_op jit(solution)/shard_map/pallas_call | solution.py:421
  44.7 0.3 collective-permute-done.5.refs_1_
  45.1 0.4 collective-permute-done.6.refs_2_
  45.5 1.9 %collective-permute-done.7.refs_3_ = bf16[2,128,128]{2,1,0:T(8,128)(2,1)S(1)} collective-permute-done((bf16[2,128,128]{2,1,0:T(8,128)(2,1)S(1)}, bf16[2,128,128]{2,1,0:T(8,128)(2,1)S(1)}, u32[]{:S(2)}, u32[]{:S(2)}) %collective-permute-start.7) | collective-permute-done | bytes 65568 | tf_op jit(solution)/shard_map/ppermute | solution.py:433
  47.4 0.8 %shard_map.81 = bf16[128,2048]{1,0:T(8,128)(2,1)} custom-call(bf16[2,128,128]{2,1,0:T(8,128)(2,1)S(1)} %get-tuple-element.33.refs_0_, bf16[2,128,128]{2,1,0:T(8,128)(2,1)S(1)} %collective-permute-done.5.refs_1_, bf16[2,128,128]{2,1,0:T(8,128)(2,1)S(1)} %collective-permute-done.6.refs_2_, ...), custom_call_target="tpu_custom_call", output_to_operand_aliasing={{}: (4, {})} | custom-call | tf_op jit(solution)/shard_map/pallas_call | solution.py:421
Async XLA Ops:
  2.6 16.5 %copy-start = (f32[2048]{0:T(1024)S(1)}, f32[2048]{0:T(1024)}, u32[]{:S(2)}) copy-start(f32[2048]{0:T(1024)} %param.11) | copy-start | bytes 24580
  2.6 16.5 %copy-start.1 = (f32[2048]{0:T(1024)S(1)}, f32[2048]{0:T(1024)}, u32[]{:S(2)}) copy-start(f32[2048]{0:T(1024)} %param.12) | copy-start | bytes 24580
  19.9 9.0 %collective-permute-start = (bf16[512,128]{1,0:T(8,128)(2,1)S(1)}, bf16[512,128]{1,0:T(8,128)(2,1)S(1)}, u32[]{:S(2)}, u32[]{:S(2)}) collective-permute-start(bf16[512,128]{1,0:T(8,128)(2,1)S(1)} %shard_map.74.refs_0_), channel_id=1, source_target_pairs={{0,12},{1,13},{2,14},{3,15},{4,8},{5,9},{6,10},{7,11},{8,4},{9,5},... | collective-permute-start | bytes 393224 | tf_op jit(solution)/shard_map/ppermute | solution.py:433
  25.4 5.6 %collective-permute-start.2 = (bf16[4,128,128]{2,1,0:T(8,128)(2,1)S(1)}, bf16[4,128,128]{2,1,0:T(8,128)(2,1)S(1)}, u32[]{:S(2)}, u32[]{:S(2)}) collective-permute-start(bf16[4,128,128]{2,1,0:T(8,128)(2,1)S(1)} %get-tuple-element.26), channel_id=1, source_target_pairs={{0,2},{1,3},{2,0},{3,1},{4,6},{5,7},{6,4},{7,5},{8,10},{9,11},{10,... | collective-permute-start | bytes 393224 | tf_op jit(solution)/shard_map/ppermute | solution.py:433
  25.4 6.4 %collective-permute-start.3 = (bf16[4,128,128]{2,1,0:T(8,128)(2,1)S(1)}, bf16[4,128,128]{2,1,0:T(8,128)(2,1)S(1)}, u32[]{:S(2)}, u32[]{:S(2)}) collective-permute-start(bf16[4,128,128]{2,1,0:T(8,128)(2,1)S(1)} %get-tuple-element.27), channel_id=1, source_target_pairs={{0,4},{1,5},{2,6},{3,7},{4,0},{5,1},{6,2},{7,3},{8,12},{9,13},{10,... | collective-permute-start | bytes 393224 | tf_op jit(solution)/shard_map/ppermute | solution.py:433
  27.2 8.0 %collective-permute-start.4 = (bf16[4,128,128]{2,1,0:T(8,128)(2,1)S(1)}, bf16[4,128,128]{2,1,0:T(8,128)(2,1)S(1)}, u32[]{:S(2)}, u32[]{:S(2)}) collective-permute-start(bf16[4,128,128]{2,1,0:T(8,128)(2,1)S(1)} %get-tuple-element.28), channel_id=1, source_target_pairs={{0,6},{1,7},{2,4},{3,5},{4,2},{5,3},{6,0},{7,1},{8,14},{9,15},{10,... | collective-permute-start | bytes 393224 | tf_op jit(solution)/shard_map/ppermute | solution.py:433
  28.9 6.6 %collective-permute-start.8 = (bf16[512,128]{1,0:T(8,128)(2,1)S(1)}, bf16[512,128]{1,0:T(8,128)(2,1)S(1)}, u32[]{:S(2)}, u32[]{:S(2)}) collective-permute-start(bf16[512,128]{1,0:T(8,128)(2,1)S(1)} %shard_map.74.refs_0_), channel_id=1, source_target_pairs={{0,1},{1,0},{2,3},{3,2},{4,5},{5,4},{6,7},{7,6},{8,9},{9,8},{10,11... | collective-permute-start | bytes 393224 | tf_op jit(solution)/shard_map/ppermute | solution.py:433
  28.9 11.0 %collective-permute-start.1 = (bf16[512,128]{1,0:T(8,128)(2,1)S(1)}, bf16[512,128]{1,0:T(8,128)(2,1)S(1)}, u32[]{:S(2)}, u32[]{:S(2)}) collective-permute-start(bf16[512,128]{1,0:T(8,128)(2,1)S(1)} %collective-permute-done.refs_0_), channel_id=1, source_target_pairs={{0,1},{1,0},{2,3},{3,2},{4,5},{5,4},{6,7},{7,6},{8,9},{9,8},{10,11... | collective-permute-start | bytes 393224 | tf_op jit(solution)/shard_map/ppermute | solution.py:433
  36.0 6.2 %collective-permute-start.9 = (bf16[2,128,128]{2,1,0:T(8,128)(2,1)S(1)}, bf16[2,128,128]{2,1,0:T(8,128)(2,1)S(1)}, u32[]{:S(2)}, u32[]{:S(2)}) collective-permute-start(bf16[2,128,128]{2,1,0:T(8,128)(2,1)S(1)} %get-tuple-element.42), channel_id=1, source_target_pairs={{0,2},{1,3},{2,0},{3,1},{4,6},{5,7},{6,4},{7,5},{8,10},{9,11},{10,... | collective-permute-start | bytes 196616 | tf_op jit(solution)/shard_map/ppermute | solution.py:433
  36.8 7.2 %collective-permute-start.10 = (bf16[2,128,128]{2,1,0:T(8,128)(2,1)S(1)}, bf16[2,128,128]{2,1,0:T(8,128)(2,1)S(1)}, u32[]{:S(2)}, u32[]{:S(2)}) collective-permute-start(bf16[2,128,128]{2,1,0:T(8,128)(2,1)S(1)} %get-tuple-element.43), channel_id=1, source_target_pairs={{0,4},{1,5},{2,6},{3,7},{4,0},{5,1},{6,2},{7,3},{8,12},{9,13},{10,... | collective-permute-start | bytes 196616 | tf_op jit(solution)/shard_map/ppermute | solution.py:433
  37.8 6.2 %collective-permute-start.11 = (bf16[2,128,128]{2,1,0:T(8,128)(2,1)S(1)}, bf16[2,128,128]{2,1,0:T(8,128)(2,1)S(1)}, u32[]{:S(2)}, u32[]{:S(2)}) collective-permute-start(bf16[2,128,128]{2,1,0:T(8,128)(2,1)S(1)} %get-tuple-element.44), channel_id=1, source_target_pairs={{0,6},{1,7},{2,4},{3,5},{4,2},{5,3},{6,0},{7,1},{8,14},{9,15},{10,... | collective-permute-start | bytes 196616 | tf_op jit(solution)/shard_map/ppermute | solution.py:433
  40.4 4.7 %collective-permute-start.5 = (bf16[2,128,128]{2,1,0:T(8,128)(2,1)S(1)}, bf16[2,128,128]{2,1,0:T(8,128)(2,1)S(1)}, u32[]{:S(2)}, u32[]{:S(2)}) collective-permute-start(bf16[2,128,128]{2,1,0:T(8,128)(2,1)S(1)} %get-tuple-element.34), channel_id=1, source_target_pairs={{0,2},{1,3},{2,0},{3,1},{4,6},{5,7},{6,4},{7,5},{8,10},{9,11},{10,... | collective-permute-start | bytes 196616 | tf_op jit(solution)/shard_map/ppermute | solution.py:433
  41.2 4.3 %collective-permute-start.6 = (bf16[2,128,128]{2,1,0:T(8,128)(2,1)S(1)}, bf16[2,128,128]{2,1,0:T(8,128)(2,1)S(1)}, u32[]{:S(2)}, u32[]{:S(2)}) collective-permute-start(bf16[2,128,128]{2,1,0:T(8,128)(2,1)S(1)} %get-tuple-element.35), channel_id=1, source_target_pairs={{0,4},{1,5},{2,6},{3,7},{4,0},{5,1},{6,2},{7,3},{8,12},{9,13},{10,... | collective-permute-start | bytes 196616 | tf_op jit(solution)/shard_map/ppermute | solution.py:433
  42.2 5.2 %collective-permute-start.7 = (bf16[2,128,128]{2,1,0:T(8,128)(2,1)S(1)}, bf16[2,128,128]{2,1,0:T(8,128)(2,1)S(1)}, u32[]{:S(2)}, u32[]{:S(2)}) collective-permute-start(bf16[2,128,128]{2,1,0:T(8,128)(2,1)S(1)} %get-tuple-element.36), channel_id=1, source_target_pairs={{0,6},{1,7},{2,4},{3,5},{4,2},{5,3},{6,0},{7,1},{8,14},{9,15},{10,... | collective-permute-start | bytes 196616 | tf_op jit(solution)/shard_map/ppermute | solution.py:433
